TPU v7x, 512 devices: a whole 4x4x16 slice. The times are simulated.
512 devices in a mesh: img: 4 (over x), gs: 128 (over z, y, core).
Axes of the slice: x: 4, y: 4, z: 16, core: 2. Of those that a mesh axis runs over, the one named last changes fastest.
Arguments:
- gaussians: float32 [12288, 10, 128], P('gs'), may hold values from -7.5 to 20, as said below
- target: bfloat16 [4, 128, 4096], P(None, 'img', 'gs'), may hold values from 0 to 1
- request: int32 [4, 128, 8, 3], P('img', 'gs'), may hold values from 0 to 95
- near_counts: int32 [4, 128, 8], P('img', 'gs'), may hold values from 1 to 3, 16 in all within a row
- render_tile: int32 [4, 128, 4], P('img', 'gs'), may hold values from 0 to 511, as said below
- tile_lists: int32 [4, 128, 16], P('img', 'gs'), may hold values from 0 to 15, each once within a row
- tile_counts: int32 [4, 128, 4], P('img', 'gs'), may hold values from 1 to 6, 16 in all within a row
Outputs:
- rendered: bfloat16 [4, 128, 4096], P(None, 'img', 'gs')
- pixel_grad: bfloat16 [4, 128, 4096], P(None, 'img', 'gs')
- gauss_grad: float32 [12288, 10, 128], P('gs')
Inputs may be any that keep to these rules, and one draw needn't show every extreme that they name: `gaussians`: value 3 lies in -0.8 to 0.8, values 2 and 4 in 0.02 to 0.8, value 5 in -7.5 to -4.5, values 6 and up in 0 to 1; values 0 and 1 in -4 to 20. `near_counts`: each renderer's row sums to 16. `render_tile`: in each strip every tile number 0 to 511 appears once; render slot j of renderer r draws a tile whose home (number div (4)) is (r + j (128 div (4))) mod 128. `tile_lists`: each renderer's row is a permutation of 0 to 15. `tile_counts`: each renderer's row sums to 16.
All inputs are finite; a program needn't handle non-finite values.
Results may differ from a plain program's by a relative error of at most 0.0024.
Values may be sent and summed in bfloat16 or wider, within the bound.
No kernel may reach another device: no remote copies, remote signals or barrier semaphores. Data moves between devices by JAX's collectives and lax.ppermute only.
A program may use at most 64 MiB of HBM per device.

v0:
```python
import jax
import jax.numpy as jnp
from jax import lax
from jax.sharding import PartitionSpec as P

TILE = 16
BLOCK = 128
CH = 4
TR = 2
TC = 2
SLOTS = 16
NEAR = 8
CAP = 3
RADIUS = 5


lam_weight = 0.2
loss_weight = 16.0
sigma_window = 1.5
batch_pairs = 8
highest = lax.Precision.HIGHEST


def shifted(block, axis, distance):
    devices = range(lax.axis_size(axis))
    route = [((i - distance) % len(devices), i) for i in devices]
    return lax.ppermute(block, axis, route)


def extended(block, sides, width):
    for axis, dim in sides:
        count = lax.axis_size(axis)
        forward = [(i, i + 1) for i in range(count - 1)]
        backward = [(target, source) for source, target in forward]
        low = lax.ppermute(
            lax.slice_in_dim(block, block.shape[dim] - width, None, axis=dim), axis, forward
        )
        high = lax.ppermute(lax.slice_in_dim(block, 0, width, axis=dim), axis, backward)
        block = jnp.concatenate([low, block, high], axis=dim)
    return block


def total_of_pieces(shard, axis):
    return lax.all_gather(shard, axis).sum(0)


def window_weights(radius):
    offsets = jnp.arange(-radius, radius + 1).astype(jnp.float32)
    weights = jnp.exp(-offsets * offsets / (2.0 * sigma_window * sigma_window))
    return weights / jnp.sum(weights)


def blur_valid(source, radius):
    weights = window_weights(radius)
    col_count = source.shape[2] - 2 * radius
    across = weights[0] * source[:, :, 0:col_count]
    for offset in range(1, 2 * radius + 1):
        across = across + weights[offset] * source[:, :, offset : offset + col_count]
    row_count = source.shape[1] - 2 * radius
    result = weights[0] * across[:, 0:row_count, :]
    for offset in range(1, 2 * radius + 1):
        result = result + weights[offset] * across[:, offset : offset + row_count, :]
    return result


def triangle(count, inclusive):
    position = jnp.arange(count)
    if inclusive:
        return (position[None, :] <= position[:, None]).astype(jnp.float32)
    return (position[None, :] < position[:, None]).astype(jnp.float32)


def group_masks(tile_ids, tiles_dev):
    onehot = (tile_ids[:, None] == jnp.arange(tiles_dev)[None, :]).astype(jnp.float32)
    position = jnp.arange(tile_ids.shape[0])
    same_tile = tile_ids[:, None] == tile_ids[None, :]
    earlier = (same_tile & (position[None, :] < position[:, None])).astype(jnp.float32)
    return (onehot, earlier)


def footprint(blocks, grid_x, grid_y):
    delta_x = grid_x[None, None, :] - blocks[:, 0, :, None]
    delta_y = grid_y[None, None, :] - blocks[:, 1, :, None]
    conic_a = blocks[:, 2, :, None]
    conic_c = blocks[:, 4, :, None]
    cross_term = blocks[:, 3, :, None] * jnp.sqrt(conic_a * conic_c)
    quadric = (
        conic_a * delta_x * delta_x
        + 2.0 * cross_term * delta_x * delta_y
        + conic_c * delta_y * delta_y
    )
    opaque = jax.nn.sigmoid(blocks[:, 5, :, None])
    return opaque * jnp.exp(-0.5 * quadric)


def composite(blocks, onehot, earlier, log_sum, grid_x, grid_y, lower_strict):
    alphas = footprint(blocks, grid_x, grid_y)
    log_keep = jnp.log1p(-alphas)
    inside = jnp.einsum("ij,mjp->mip", lower_strict, log_keep, precision=highest)
    block_sums = jnp.sum(log_keep, axis=1)
    before = jnp.dot(earlier, block_sums, precision=highest) + jnp.dot(
        onehot, log_sum, precision=highest
    )
    transmit = jnp.exp(inside + before[:, None, :])
    return (alphas, block_sums, transmit)


def on_device(gaussians, target, request, near_counts, render_tile, tile_lists, tile_counts):
    devices_gs = lax.axis_size("gs")
    tiles_dev = TR * TC
    stride = devices_gs // tiles_dev
    half_near = NEAR // 2
    block_vals = gaussians.shape[1]
    pixels = TILE * TILE
    wanted = request[0, 0].reshape(NEAR * CAP)
    outgoing = gaussians[wanted].reshape(NEAR, CAP, block_vals, BLOCK)
    arrived_blocks = []
    for group in range(NEAR):
        arrived_blocks.append(shifted(outgoing[group], "gs", half_near - group))
    padded = jnp.stack(arrived_blocks).reshape(NEAR * CAP, block_vals, BLOCK)
    counts_here = near_counts[0, 0]
    near_ends = jnp.cumsum(counts_here)
    near_starts = near_ends - counts_here
    slot_pos = jnp.arange(SLOTS)
    group_of = jnp.sum((slot_pos[:, None] >= near_ends[None, :]).astype(jnp.int32), axis=1)
    padded_index = group_of * CAP + slot_pos - near_starts[group_of]
    received = padded[padded_index]
    order_list = tile_lists[0, 0]
    tile_ends = jnp.cumsum(tile_counts[0, 0])
    pair_tile = jnp.sum(
        (jnp.arange(SLOTS)[:, None] >= tile_ends[None, :]).astype(jnp.int32), axis=1
    )
    steps_count = SLOTS // batch_pairs
    stacked = (
        received[order_list].reshape(steps_count, batch_pairs, block_vals, BLOCK),
        pair_tile.reshape(steps_count, batch_pairs),
    )
    pixel_idx = jnp.arange(pixels)
    grid_x = (pixel_idx % TILE).astype(jnp.float32) + 0.5
    grid_y = (pixel_idx // TILE).astype(jnp.float32) + 0.5
    lower_strict = triangle(BLOCK, False)
    lower_full = triangle(BLOCK, True)

    def forward_step(carried, packed):
        log_sum, colour = carried
        blocks, tile_ids = packed
        onehot, earlier = group_masks(tile_ids, tiles_dev)
        alphas, block_sums, transmit = composite(
            blocks, onehot, earlier, log_sum, grid_x, grid_y, lower_strict
        )
        weight = transmit * alphas
        contrib = jnp.einsum("mcg,mgp->mcp", blocks[:, 6:, :], weight, precision=highest)
        colour = colour + jnp.einsum("mt,mcp->tcp", onehot, contrib, precision=highest)
        log_sum = log_sum + jnp.dot(onehot.T, block_sums, precision=highest)
        return ((log_sum, colour), None)

    start_log = jnp.zeros((tiles_dev, pixels), jnp.float32)
    start_colour = jnp.zeros((tiles_dev, CH, pixels), jnp.float32)
    (log_end, colour), unused = lax.scan(forward_step, (start_log, start_colour), stacked)
    rendered_tiles = colour.astype(jnp.bfloat16)
    render_here = render_tile[0, 0]
    local_of = render_here % tiles_dev
    arrived_tiles = []
    arrived_tags = []
    for slot in range(tiles_dev):
        piece, piece_tag = shifted(
            (rendered_tiles[slot], local_of[slot : slot + 1]), "gs", slot * stride
        )
        arrived_tiles.append(piece)
        arrived_tags.append(piece_tag)
    arrived = jnp.stack(arrived_tiles)
    tags_all = jnp.concatenate(arrived_tags)
    place_mask = (tags_all[None, :] == jnp.arange(tiles_dev)[:, None]).astype(jnp.bfloat16)
    home_tiles = jnp.einsum(
        "ks,scp->kcp", place_mask, arrived, preferred_element_type=jnp.float32
    ).astype(jnp.bfloat16)
    home_image = (
        home_tiles.reshape(TR, TC, CH, TILE, TILE)
        .transpose(2, 0, 3, 1, 4)
        .reshape(CH, TR * TILE, TC * TILE)
    )
    error_map = home_image.astype(jnp.float32) - target.astype(jnp.float32)
    error_ext = extended(error_map, (("img", 1), ("gs", 2)), 2 * RADIUS)
    smooth_wide = blur_valid(error_ext, RADIUS)
    row_global = lax.axis_index("img") * (TR * TILE) - RADIUS + jnp.arange(TR * TILE + 2 * RADIUS)
    col_global = lax.axis_index("gs") * (TC * TILE) - RADIUS + jnp.arange(TC * TILE + 2 * RADIUS)
    row_inside = (row_global >= 0) & (row_global < TR * TILE * lax.axis_size("img"))
    col_inside = (col_global >= 0) & (col_global < TC * TILE * devices_gs)
    inside_mask = (row_inside[:, None] & col_inside[None, :]).astype(jnp.float32)
    back_blur = blur_valid(smooth_wide * inside_mask[None, :, :], RADIUS)
    pixel_grad = (loss_weight * ((1.0 - lam_weight) * error_map + lam_weight * back_blur)).astype(
        jnp.bfloat16
    )
    grad_home = (
        pixel_grad.reshape(CH, TR, TILE, TC, TILE)
        .transpose(1, 3, 0, 2, 4)
        .reshape(tiles_dev, CH, pixels)
    )
    send_back = jnp.einsum(
        "ks,kcp->scp", place_mask, grad_home, preferred_element_type=jnp.float32
    ).astype(jnp.bfloat16)
    got_list = []
    for slot in range(tiles_dev):
        got_list.append(shifted(send_back[slot], "gs", -slot * stride))
    my_grads = jnp.stack(got_list).astype(jnp.float32)
    grad_dot = jnp.sum(my_grads * colour, axis=1)
    moments = jnp.stack(
        [jnp.ones_like(grid_x), grid_x, grid_y, grid_x * grid_x, grid_x * grid_y, grid_y * grid_y],
        axis=1,
    )

    def backward_step(carried, packed):
        log_sum, prod_sum = carried
        blocks, tile_ids = packed
        onehot, earlier = group_masks(tile_ids, tiles_dev)
        alphas, block_sums, transmit = composite(
            blocks, onehot, earlier, log_sum, grid_x, grid_y, lower_strict
        )
        weight = transmit * alphas
        pair_grad = jnp.einsum("mt,tcp->mcp", onehot, my_grads, precision=highest)
        shades = blocks[:, 6:, :]
        shade_dot = jnp.einsum("mcg,mcp->mgp", shades, pair_grad, precision=highest)
        product = weight * shade_dot
        prod_sums = jnp.sum(product, axis=1)
        carried_prod = jnp.dot(earlier, prod_sums, precision=highest) + jnp.dot(
            onehot, prod_sum, precision=highest
        )
        prefix = (
            jnp.einsum("ij,mjp->mip", lower_full, product, precision=highest)
            + carried_prod[:, None, :]
        )
        pair_dot = jnp.dot(onehot, grad_dot, precision=highest)
        d_alpha = transmit * shade_dot - (pair_dot[:, None, :] - prefix) / (1.0 - alphas)
        shade_grad = jnp.einsum("mgp,mcp->mcg", weight, pair_grad, precision=highest)
        opaque = jax.nn.sigmoid(blocks[:, 5, :])
        logit_grad = (1.0 - opaque) * jnp.sum(d_alpha * alphas, axis=2)
        quad_grad = -0.5 * d_alpha * alphas
        moment_sums = jnp.einsum("mgp,pk->mgk", quad_grad, moments, precision=highest)
        mean_x = blocks[:, 0, :]
        mean_y = blocks[:, 1, :]
        conic_a = blocks[:, 2, :]
        correl = blocks[:, 3, :]
        conic_c = blocks[:, 4, :]
        weight_sum = moment_sums[..., 0]
        along_x = moment_sums[..., 1] - mean_x * weight_sum
        along_y = moment_sums[..., 2] - mean_y * weight_sum
        square_x = (
            moment_sums[..., 3] - 2.0 * mean_x * moment_sums[..., 1] + mean_x * mean_x * weight_sum
        )
        square_y = (
            moment_sums[..., 5] - 2.0 * mean_y * moment_sums[..., 2] + mean_y * mean_y * weight_sum
        )
        mixed_xy = (
            moment_sums[..., 4]
            - mean_x * moment_sums[..., 2]
            - mean_y * moment_sums[..., 1]
            + mean_x * mean_y * weight_sum
        )
        root_ac = jnp.sqrt(conic_a * conic_c)
        cross_term = correl * root_ac
        grad_mx = -2.0 * (conic_a * along_x + cross_term * along_y)
        grad_my = -2.0 * (cross_term * along_x + conic_c * along_y)
        grad_ca = square_x + correl * jnp.sqrt(conic_c / conic_a) * mixed_xy
        grad_rho = 2.0 * root_ac * mixed_xy
        grad_cc = square_y + correl * jnp.sqrt(conic_a / conic_c) * mixed_xy
        shape_grads = jnp.stack([grad_mx, grad_my, grad_ca, grad_rho, grad_cc, logit_grad], axis=1)
        log_sum = log_sum + jnp.dot(onehot.T, block_sums, precision=highest)
        prod_sum = prod_sum + jnp.dot(onehot.T, prod_sums, precision=highest)
        return ((log_sum, prod_sum), jnp.concatenate([shape_grads, shade_grad], axis=1))

    unused_carry, pair_grads = lax.scan(backward_step, (start_log, start_log), stacked)
    slot_grads = (
        jnp.zeros((SLOTS, block_vals, BLOCK), jnp.float32)
        .at[order_list]
        .set(pair_grads.reshape(SLOTS, block_vals, BLOCK))
    )
    padded_grads = (
        jnp.zeros((NEAR * CAP, block_vals, BLOCK), jnp.float32)
        .at[padded_index]
        .set(slot_grads)
        .reshape(NEAR, CAP, block_vals, BLOCK)
    )
    returned_list = []
    for group in range(NEAR):
        returned_list.append(shifted(padded_grads[group], "gs", group - half_near))
    returned = jnp.stack(returned_list).reshape(NEAR * CAP, block_vals * BLOCK)
    select = (wanted[None, :] == jnp.arange(gaussians.shape[0])[:, None]).astype(jnp.float32)
    local_sum = jnp.dot(select, returned, precision=highest)
    summed = total_of_pieces(local_sum, "img").reshape(gaussians.shape)
    return (home_image, pixel_grad, summed)


def solution(mesh):
    in_specs = (
        P("gs", None, None),
        P(None, "img", "gs"),
        P("img", "gs", None, None),
        P("img", "gs", None),
        P("img", "gs", None),
        P("img", "gs", None),
        P("img", "gs", None),
    )
    out_specs = (P(None, "img", "gs"), P(None, "img", "gs"), P("gs", None, None))
    return jax.shard_map(
        on_device, mesh=mesh, in_specs=in_specs, out_specs=out_specs, check_vma=False
    )
```

profile of v0, /device:TPU:1, one launch (start us, length us, event | category | flops | bytes accessed | tf_op | source)
XLA Modules:
  0.0 263.7 jit_solution(7542475670553481739)
XLA Ops:
  9.1 5.6 %collective-permute-start.4 = (f32[3,10,128]{2,0,1:T(4,128)S(1)}, f32[3,10,128]{2,0,1:T(4,128)S(1)}, u32[]{:S(2)}, u32[]{:S(2)}) collective-permute-start(f32[3,10,128]{2,0,1:T(4,128)S(1)} %get-tuple-element.395), channel_id=1, source_target_pairs={{124,0},{125,1},{126,2},{127,3},{0,4},{1,5},{2,6},{3,7},{4,8},{5,9... | collective-permute-start | bytes 46088 | tf_op jit(solution)/shard_map/ppermute | solution.py:27
  14.7 4.2 %collective-permute-start.5 = (f32[3,10,128]{2,0,1:T(4,128)S(1)}, f32[3,10,128]{2,0,1:T(4,128)S(1)}, u32[]{:S(2)}, u32[]{:S(2)}) collective-permute-start(f32[3,10,128]{2,0,1:T(4,128)S(1)} %get-tuple-element.394), channel_id=1, source_target_pairs={{125,0},{126,1},{127,2},{0,3},{1,4},{2,5},{3,6},{4,7},{5,8},{6,9},... | collective-permute-start | bytes 46088 | tf_op jit(solution)/shard_map/ppermute | solution.py:27
  18.9 3.2 %collective-permute-start.6 = (f32[3,10,128]{2,0,1:T(4,128)S(1)}, f32[3,10,128]{2,0,1:T(4,128)S(1)}, u32[]{:S(2)}, u32[]{:S(2)}) collective-permute-start(f32[3,10,128]{2,0,1:T(4,128)S(1)} %get-tuple-element.393), channel_id=1, source_target_pairs={{126,0},{127,1},{0,2},{1,3},{2,4},{3,5},{4,6},{5,7},{6,8},{7,9},{8... | collective-permute-start | bytes 46088 | tf_op jit(solution)/shard_map/ppermute | solution.py:27
  22.1 1.9 collective-permute-start.7
  28.1 2.4 collective-permute-start.9
  30.5 7.3 %collective-permute-start.10 = (f32[3,10,128]{2,0,1:T(4,128)S(1)}, f32[3,10,128]{2,0,1:T(4,128)S(1)}, u32[]{:S(2)}, u32[]{:S(2)}) collective-permute-start(f32[3,10,128]{2,0,1:T(4,128)S(1)} %get-tuple-element.389), channel_id=1, source_target_pairs={{2,0},{3,1},{4,2},{5,3},{6,4},{7,5},{8,6},{9,7},{10,8},{11,9},{12,... | collective-permute-start | bytes 46088 | tf_op jit(solution)/shard_map/ppermute | solution.py:27
  37.9 5.5 %collective-permute-start.11 = (f32[3,10,128]{2,0,1:T(4,128)S(1)}, f32[3,10,128]{2,0,1:T(4,128)S(1)}, u32[]{:S(2)}, u32[]{:S(2)}) collective-permute-start(f32[3,10,128]{2,0,1:T(4,128)S(1)} %get-tuple-element.388), channel_id=1, source_target_pairs={{3,0},{4,1},{5,2},{6,3},{7,4},{8,5},{9,6},{10,7},{11,8},{12,9},{13... | collective-permute-start | bytes 46088 | tf_op jit(solution)/shard_map/ppermute | solution.py:27
  43.5 1.2 collective-permute-start
  44.7 4.5 %collective-permute-start.1 = (s32[1]{0:T(128)}, s32[1]{0:T(128)}, u32[]{:S(2)}, u32[]{:S(2)}) collective-permute-start(s32[1]{0:T(128)} %get-tuple-element.422), channel_id=1, source_target_pairs={{96,0},{97,1},{98,2},{99,3},{100,4},{101,5},{102,6},{103,7},{104,8... | collective-permute-start | bytes 20 | tf_op jit(solution)/shard_map/ppermute | solution.py:27
  49.3 10.6 %collective-permute-start.2 = (s32[1]{0:T(128)}, s32[1]{0:T(128)}, u32[]{:S(2)}, u32[]{:S(2)}) collective-permute-start(s32[1]{0:T(128)} %get-tuple-element.421), channel_id=1, source_target_pairs={{64,0},{65,1},{66,2},{67,3},{68,4},{69,5},{70,6},{71,7},{72,8},{73... | collective-permute-start | bytes 20 | tf_op jit(solution)/shard_map/ppermute | solution.py:27
  60.0 5.2 %collective-permute-start.3 = (s32[1]{0:T(128)}, s32[1]{0:T(128)}, u32[]{:S(2)}, u32[]{:S(2)}) collective-permute-start(s32[1]{0:T(128)} %get-tuple-element.420), channel_id=1, source_target_pairs={{32,0},{33,1},{34,2},{35,3},{36,4},{37,5},{38,6},{39,7},{40,8},{41... | collective-permute-start | bytes 20 | tf_op jit(solution)/shard_map/ppermute | solution.py:27
  66.5 10.1 %while.28 = (s32[]{:T(128)}, f32[4,256]{1,0:T(4,128)S(1)}, f32[4,4,256]{2,0,1:T(4,128)S(1)}, s32[2,8]{1,0:T(2,128)S(1)}, f32[2,8,10,128]{3,1,2,0:T(8,128)S(1)}, /*index=5*/s32[]{:T(128)}, s32[]{:T(128)}) while((s32[]{:T(128)}, f32[4,256]{1,0:T(4,128)S(1)}, f32[4,4,256]{2,0,1:T(4,128)S(1)}, s32[2,8]{1,0:T(2,128)S(1)}, ...), condition=%wide.region_6.7_spmd.clone, body=%wide.region_4.6_spmd.clone.sunk | while | flops 426824992 | bytes 2509089 | solution.py:159
  66.5 1.0 fusion.285
  68.0 2.3 fusion.287
  70.3 1.0 fusion.288
  71.6 1.0 fusion.285
  73.0 2.3 fusion.287
  75.3 1.0 fusion.288
  76.7 4.0 %collective-permute-start.13 = (bf16[4,256]{1,0:T(4,128)(2,1)S(1)}, bf16[4,256]{1,0:T(4,128)(2,1)S(1)}, u32[]{:S(2)}, u32[]{:S(2)}) collective-permute-start(bf16[4,256]{1,0:T(4,128)(2,1)S(1)} %bitcast.367), channel_id=1, source_target_pairs={{96,0},{97,1},{98,2},{99,3},{100,4},{101,5},{102,6},{103,7},{104,8... | collective-permute-start | bytes 6152 | tf_op jit(solution)/shard_map/ppermute | solution.py:27
  80.7 4.9 %collective-permute-start.14 = (bf16[4,256]{1,0:T(4,128)(2,1)S(1)}, bf16[4,256]{1,0:T(4,128)(2,1)S(1)}, u32[]{:S(2)}, u32[]{:S(2)}) collective-permute-start(bf16[4,256]{1,0:T(4,128)(2,1)S(1)} %bitcast.364), channel_id=1, source_target_pairs={{64,0},{65,1},{66,2},{67,3},{68,4},{69,5},{70,6},{71,7},{72,8},{73... | collective-permute-start | bytes 6152 | tf_op jit(solution)/shard_map/ppermute | solution.py:27
  85.6 4.0 %collective-permute-start.15 = (bf16[4,256]{1,0:T(4,128)(2,1)S(1)}, bf16[4,256]{1,0:T(4,128)(2,1)S(1)}, u32[]{:S(2)}, u32[]{:S(2)}) collective-permute-start(bf16[4,256]{1,0:T(4,128)(2,1)S(1)} %bitcast.363), channel_id=1, source_target_pairs={{32,0},{33,1},{34,2},{35,3},{36,4},{37,5},{38,6},{39,7},{40,8},{41... | collective-permute-start | bytes 6152 | tf_op jit(solution)/shard_map/ppermute | solution.py:27
  89.7 2.6 pad_add_fusion
  92.3 1.5 collective-permute-done.14
  94.7 3.1 %collective-permute-start.16 = (f32[4,10,32]{2,1,0:T(8,128)S(1)}, f32[4,10,32]{2,1,0:T(8,128)S(1)}, u32[]{:S(2)}, u32[]{:S(2)}) collective-permute-start(f32[4,10,32]{2,1,0:T(8,128)S(1)} %get-tuple-element.398), channel_id=1, source_target_pairs={{0,128},{128,256},{256,384},{1,129},{129,257},{257,385},{2,130},{1... | collective-permute-start | bytes 15368 | tf_op jit(solution)/shard_map/ppermute | solution.py:35
  97.9 1.3 collective-permute-start.17
  99.2 3.3 %collective-permute-done.17 = f32[4,10,32]{2,1,0:T(8,128)S(1)} collective-permute-done((f32[4,10,32]{2,1,0:T(8,128)S(1)}, f32[4,10,32]{2,1,0:T(8,128)S(1)}, u32[]{:S(2)}, u32[]{:S(2)}) %collective-permute-start.17) | collective-permute-done | bytes 5152 | tf_op jit(solution)/shard_map/ppermute | solution.py:38
  102.6 5.0 %collective-permute-start.18 = (f32[4,52,10]{2,1,0:T(8,128)S(1)}, f32[4,52,10]{2,1,0:T(8,128)S(1)}, u32[]{:S(2)}, u32[]{:S(2)}) collective-permute-start(f32[4,52,10]{2,1,0:T(8,128)S(1)} %get-tuple-element.396), channel_id=1, source_target_pairs={{0,1},{1,2},{2,3},{3,4},{4,5},{5,6},{6,7},{7,8},{8,9},{9,10},{10,1... | collective-permute-start | bytes 24968 | tf_op jit(solution)/shard_map/ppermute | solution.py:35
  107.7 1.9 collective-permute-start.19
  109.7 4.2 %collective-permute-done.19 = f32[4,52,10]{2,1,0:T(8,128)S(1)} collective-permute-done((f32[4,52,10]{2,1,0:T(8,128)S(1)}, f32[4,52,10]{2,1,0:T(8,128)S(1)}, u32[]{:S(2)}, u32[]{:S(2)}) %collective-permute-start.19) | collective-permute-done | bytes 8352 | tf_op jit(solution)/shard_map/ppermute | solution.py:38
  114.0 7.2 %fusion.134 = f32[4,52,42]{2,1,0:T(8,128)S(1)} fusion(f32[4,52,52]{2,1,0:T(8,128)S(1)} %pad_maximum_fusion.1, f32[4,10,32]{2,1,0:T(8,128)S(1)} %collective-permute-done.17, f32[4,32,32]{2,1,0:T(8,128)S(1)} %convert_subtract_fusion, f32[4,10,32]{2,1,0:T(8,128)S(1)} %collective-permute-done.16, f32[4,52,10]{2,1,0:T(8,128)S(1)} %collective-permute-done.18, ...), kind=kLoop, calls=%fused_computation.197 | loop fusion | flops 235872 | bytes 392748 | tf_op jit(solution)/shard_map/add | solution.py:58
  121.2 7.0 %fusion.154 = f32[4,42,42]{2,1,0:T(8,128)S(1)} fusion(f32[4,52,42]{2,1,0:T(8,128)S(1)} %fusion.134, f32[42,42]{1,0:T(8,128)S(1)} %and_convert_fusion, f32[]{:T(128)} %bitcast.39, f32[]{:T(128)} %bitcast.38, f32[]{:T(128)} %bitcast.37, f32[]{:T(128)} %bitcast.36, f32[]{:T(128)} %bitcast.35, f32[]{:T(128)} %bitcast.34, f32[]{:T(128)} %bitcast.33, ...), kind=kLoop, calls=%fused_computation.241 | loop fusion | flops 155232 | bytes 345788 | tf_op jit(solution)/shard_map/mul | solution.py:190
  128.1 7.1 %fusion.143 = f32[4,42,32]{2,1,0:T(8,128)S(1)} fusion(f32[4,42,42]{2,1,0:T(8,128)S(1)} %fusion.154, f32[]{:T(128)} %bitcast.39, f32[]{:T(128)} %bitcast.38, f32[]{:T(128)} %bitcast.37, f32[]{:T(128)} %bitcast.36, f32[]{:T(128)} %bitcast.35, f32[]{:T(128)} %bitcast.34, f32[]{:T(128)} %bitcast.33, f32[]{:T(128)} %bitcast.32, f32[]{:T(128)} %bitcast.31, ...), kind=kLoop, calls=%fused_computation.219 | loop fusion | flops 112896 | bytes 258092 | tf_op jit(solution)/shard_map/add | solution.py:58
  135.3 6.9 %fusion.168 = bf16[4,32,32]{2,1,0:T(8,128)(2,1)S(1)} fusion(f32[4,42,32]{2,1,0:T(8,128)S(1)} %fusion.143, f32[]{:T(128)} %bitcast.39, f32[]{:T(128)} %bitcast.38, f32[]{:T(128)} %bitcast.37, f32[]{:T(128)} %bitcast.36, f32[]{:T(128)} %bitcast.35, f32[]{:T(128)} %bitcast.34, f32[]{:T(128)} %bitcast.33, f32[]{:T(128)} %bitcast.32, f32[]{:T(128)} %bitcast.31, ...), kind=kLoop, calls=%fused_computation.266 | loop fusion | flops 118784 | bytes 204844 | tf_op jit(solution)/shard_map/convert_element_type | solution.py:191
  142.7 5.4 %collective-permute-start.21 = (bf16[4,256]{1,0:T(4,128)(2,1)S(1)}, bf16[4,256]{1,0:T(4,128)(2,1)S(1)}, u32[]{:S(2)}, u32[]{:S(2)}) collective-permute-start(bf16[4,256]{1,0:T(4,128)(2,1)S(1)} %bitcast.369), channel_id=1, source_target_pairs={{32,0},{33,1},{34,2},{35,3},{36,4},{37,5},{38,6},{39,7},{40,8},{41... | collective-permute-start | bytes 6152 | tf_op jit(solution)/shard_map/ppermute | solution.py:27
  148.2 9.4 %collective-permute-start.22 = (bf16[4,256]{1,0:T(4,128)(2,1)S(1)}, bf16[4,256]{1,0:T(4,128)(2,1)S(1)}, u32[]{:S(2)}, u32[]{:S(2)}) collective-permute-start(bf16[4,256]{1,0:T(4,128)(2,1)S(1)} %bitcast.371), channel_id=1, source_target_pairs={{64,0},{65,1},{66,2},{67,3},{68,4},{69,5},{70,6},{71,7},{72,8},{73... | collective-permute-start | bytes 6152 | tf_op jit(solution)/shard_map/ppermute | solution.py:27
  157.6 4.2 %collective-permute-start.23 = (bf16[4,256]{1,0:T(4,128)(2,1)S(1)}, bf16[4,256]{1,0:T(4,128)(2,1)S(1)}, u32[]{:S(2)}, u32[]{:S(2)}) collective-permute-start(bf16[4,256]{1,0:T(4,128)(2,1)S(1)} %bitcast.373), channel_id=1, source_target_pairs={{96,0},{97,1},{98,2},{99,3},{100,4},{101,5},{102,6},{103,7},{104,8... | collective-permute-start | bytes 6152 | tf_op jit(solution)/shard_map/ppermute | solution.py:27
  161.9 3.9 %collective-permute-done.23 = bf16[4,256]{1,0:T(4,128)(2,1)S(1)} collective-permute-done((bf16[4,256]{1,0:T(4,128)(2,1)S(1)}, bf16[4,256]{1,0:T(4,128)(2,1)S(1)}, u32[]{:S(2)}, u32[]{:S(2)}) %collective-permute-start.23) | collective-permute-done | bytes 2080 | tf_op jit(solution)/shard_map/ppermute | solution.py:27
  165.9 23.6 %while.29 = (s32[]{:T(128)}, f32[4,256]{1,0:T(4,128)S(1)}, f32[4,256]{1,0:T(4,128)S(1)}, f32[2,8,10,128]{3,2,1,0:T(8,128)S(1)}, s32[2,8]{1,0:T(2,128)S(1)}, /*in...) while((s32[]{:T(128)}, f32[4,256]{1,0:T(4,128)S(1)}, ...), condition=%wide.region_13.14_spmd.clone, body=%wide.region_9.13_spmd.clone.sunk | while | flops 878024256 | bytes 9445830 | solution.py:271
  166.0 1.0 fusion.308
  167.4 1.8 fusion.311
  169.5 2.3 multiply_reduce_fusion.4
  172.4 2.2 multiply_reduce_fusion.5
  174.6 1.3 fusion.315
  176.0 1.3 fusion.317
  177.8 1.0 fusion.308
  179.2 1.8 fusion.311
  181.2 2.3 multiply_reduce_fusion.4
  184.2 2.2 multiply_reduce_fusion.5
  186.4 1.3 fusion.315
  187.8 1.3 fusion.317
  189.5 1.0 scatter_fusion
  190.6 1.0 scatter_fusion.1
  191.6 3.2 %collective-permute-start.24 = (f32[3,10,128]{2,1,0:T(8,128)S(1)}, f32[3,10,128]{2,1,0:T(8,128)S(1)}, u32[]{:S(2)}, u32[]{:S(2)}) collective-permute-start(f32[3,10,128]{2,1,0:T(8,128)S(1)} %get-tuple-element.387), channel_id=1, source_target_pairs={{4,0},{5,1},{6,2},{7,3},{8,4},{9,5},{10,6},{11,7},{12,8},{13,9},{1... | collective-permute-start | bytes 46088 | tf_op jit(solution)/shard_map/ppermute | solution.py:27
  194.9 4.7 %collective-permute-start.25 = (f32[3,10,128]{2,1,0:T(8,128)S(1)}, f32[3,10,128]{2,1,0:T(8,128)S(1)}, u32[]{:S(2)}, u32[]{:S(2)}) collective-permute-start(f32[3,10,128]{2,1,0:T(8,128)S(1)} %get-tuple-element.386), channel_id=1, source_target_pairs={{3,0},{4,1},{5,2},{6,3},{7,4},{8,5},{9,6},{10,7},{11,8},{12,9},{13... | collective-permute-start | bytes 46088 | tf_op jit(solution)/shard_map/ppermute | solution.py:27
  199.6 5.4 %collective-permute-start.26 = (f32[3,10,128]{2,1,0:T(8,128)S(1)}, f32[3,10,128]{2,1,0:T(8,128)S(1)}, u32[]{:S(2)}, u32[]{:S(2)}) collective-permute-start(f32[3,10,128]{2,1,0:T(8,128)S(1)} %get-tuple-element.385), channel_id=1, source_target_pairs={{2,0},{3,1},{4,2},{5,3},{6,4},{7,5},{8,6},{9,7},{10,8},{11,9},{12,... | collective-permute-start | bytes 46088 | tf_op jit(solution)/shard_map/ppermute | solution.py:27
  205.0 2.1 collective-permute-start.27
  207.1 3.5 %collective-permute-start.29 = (f32[3,10,128]{2,1,0:T(8,128)S(1)}, f32[3,10,128]{2,1,0:T(8,128)S(1)}, u32[]{:S(2)}, u32[]{:S(2)}) collective-permute-start(f32[3,10,128]{2,1,0:T(8,128)S(1)} %get-tuple-element.382), channel_id=1, source_target_pairs={{127,0},{0,1},{1,2},{2,3},{3,4},{4,5},{5,6},{6,7},{7,8},{8,9},{9,1... | collective-permute-start | bytes 46088 | tf_op jit(solution)/shard_map/ppermute | solution.py:27
  210.6 2.8 %collective-permute-start.30 = (f32[3,10,128]{2,1,0:T(8,128)S(1)}, f32[3,10,128]{2,1,0:T(8,128)S(1)}, u32[]{:S(2)}, u32[]{:S(2)}) collective-permute-start(f32[3,10,128]{2,1,0:T(8,128)S(1)} %get-tuple-element.381), channel_id=1, source_target_pairs={{126,0},{127,1},{0,2},{1,3},{2,4},{3,5},{4,6},{5,7},{6,8},{7,9},{8... | collective-permute-start | bytes 46088 | tf_op jit(solution)/shard_map/ppermute | solution.py:27
  213.4 4.5 %collective-permute-start.31 = (f32[3,10,128]{2,1,0:T(8,128)S(1)}, f32[3,10,128]{2,1,0:T(8,128)S(1)}, u32[]{:S(2)}, u32[]{:S(2)}) collective-permute-start(f32[3,10,128]{2,1,0:T(8,128)S(1)} %get-tuple-element.380), channel_id=1, source_target_pairs={{125,0},{126,1},{127,2},{0,3},{1,4},{2,5},{3,6},{4,7},{5,8},{6,9},... | collective-permute-start | bytes 46088 | tf_op jit(solution)/shard_map/ppermute | solution.py:27
  218.5 3.5 %collective-permute-done.31 = f32[3,10,128]{2,1,0:T(8,128)S(1)} collective-permute-done((f32[3,10,128]{2,1,0:T(8,128)S(1)}, f32[3,10,128]{2,1,0:T(8,128)S(1)}, u32[]{:S(2)}, u32[]{:S(2)}) %collective-permute-start.31) | collective-permute-done | bytes 15392 | tf_op jit(solution)/shard_map/ppermute | solution.py:27
  222.1 1.1 fusion.130
  223.2 30.7 %all-gather.3.cloned.1.call-done = f32[384,1280]{1,0:T(8,128)} async-done(((f32[96,1280]{1,0:T(8,128)}), f32[384,1280]{1,0:T(8,128)}) %all-gather.3.cloned.1.call-update) | async-done | bytes 1966096 | tf_op jit(solution)/shard_map/all_gather | solution.py:44
  253.9 1.7 reduce_sum.94
  255.8 1.0 copy.291
  (198 shorter events, 14.7 us)
Async XLA Ops:
  7.2 1.1 copy-start
  7.2 17.5 %copy-start.4 = (s32[1,1,8]{2,1,0:T(1,128)S(1)}, s32[1,1,8]{2,1,0:T(1,128)}, u32[]{:S(2)}) copy-start(s32[1,1,8]{2,1,0:T(1,128)} %param.14) | copy-start | bytes 100
  7.2 18.4 %copy-start.5 = (s32[1,1,16]{2,1,0:T(1,128)S(1)}, s32[1,1,16]{2,1,0:T(1,128)}, u32[]{:S(2)}) copy-start(s32[1,1,16]{2,1,0:T(1,128)} %param.16) | copy-start | bytes 196
  7.2 18.4 %copy-start.6 = (s32[1,1,4]{2,1,0:T(1,128)S(1)}, s32[1,1,4]{2,1,0:T(1,128)}, u32[]{:S(2)}) copy-start(s32[1,1,4]{2,1,0:T(1,128)} %param.17) | copy-start | bytes 52
  7.2 18.7 %copy-start.7 = (s32[1,1,4]{2,1,0:T(1,128)S(1)}, s32[1,1,4]{2,1,0:T(1,128)}, u32[]{:S(2)}) copy-start(s32[1,1,4]{2,1,0:T(1,128)} %param.15) | copy-start | bytes 52
  7.2 246.7 %all-gather.3.cloned.1.call-start = ((), (), s32[]{:S(2)}) async-start(), calls=%async_computation | async-start | bytes 2457600 | tf_op jit(solution)/shard_map/all_gather | solution.py:44
  9.1 19.1 %collective-permute-start.4 = (f32[3,10,128]{2,0,1:T(4,128)S(1)}, f32[3,10,128]{2,0,1:T(4,128)S(1)}, u32[]{:S(2)}, u32[]{:S(2)}) collective-permute-start(f32[3,10,128]{2,0,1:T(4,128)S(1)} %get-tuple-element.395), channel_id=1, source_target_pairs={{124,0},{125,1},{126,2},{127,3},{0,4},{1,5},{2,6},{3,7},{4,8},{5,9... | collective-permute-start | bytes 46088 | tf_op jit(solution)/shard_map/ppermute | solution.py:27
  14.7 15.8 %collective-permute-start.5 = (f32[3,10,128]{2,0,1:T(4,128)S(1)}, f32[3,10,128]{2,0,1:T(4,128)S(1)}, u32[]{:S(2)}, u32[]{:S(2)}) collective-permute-start(f32[3,10,128]{2,0,1:T(4,128)S(1)} %get-tuple-element.394), channel_id=1, source_target_pairs={{125,0},{126,1},{127,2},{0,3},{1,4},{2,5},{3,6},{4,7},{5,8},{6,9},... | collective-permute-start | bytes 46088 | tf_op jit(solution)/shard_map/ppermute | solution.py:27
  18.9 19.0 %collective-permute-start.6 = (f32[3,10,128]{2,0,1:T(4,128)S(1)}, f32[3,10,128]{2,0,1:T(4,128)S(1)}, u32[]{:S(2)}, u32[]{:S(2)}) collective-permute-start(f32[3,10,128]{2,0,1:T(4,128)S(1)} %get-tuple-element.393), channel_id=1, source_target_pairs={{126,0},{127,1},{0,2},{1,3},{2,4},{3,5},{4,6},{5,7},{6,8},{7,9},{8... | collective-permute-start | bytes 46088 | tf_op jit(solution)/shard_map/ppermute | solution.py:27
  22.1 21.4 %collective-permute-start.7 = (f32[3,10,128]{2,0,1:T(4,128)S(1)}, f32[3,10,128]{2,0,1:T(4,128)S(1)}, u32[]{:S(2)}, u32[]{:S(2)}) collective-permute-start(f32[3,10,128]{2,0,1:T(4,128)S(1)} %get-tuple-element.392), channel_id=1, source_target_pairs={{127,0},{0,1},{1,2},{2,3},{3,4},{4,5},{5,6},{6,7},{7,8},{8,9},{9,1... | collective-permute-start | bytes 46088 | tf_op jit(solution)/shard_map/ppermute | solution.py:27
  24.0 20.7 %collective-permute-start.8 = (f32[3,10,128]{2,0,1:T(4,128)S(1)}, f32[3,10,128]{2,0,1:T(4,128)S(1)}, u32[]{:S(2)}, u32[]{:S(2)}) collective-permute-start(f32[3,10,128]{2,0,1:T(4,128)S(1)} %get-tuple-element.391), channel_id=1, source_target_pairs={{0,0},{1,1},{2,2},{3,3},{4,4},{5,5},{6,6},{7,7},{8,8},{9,9},{10,10... | collective-permute-start | bytes 46088 | tf_op jit(solution)/shard_map/ppermute | solution.py:27
  28.1 21.2 %collective-permute-start.9 = (f32[3,10,128]{2,0,1:T(4,128)S(1)}, f32[3,10,128]{2,0,1:T(4,128)S(1)}, u32[]{:S(2)}, u32[]{:S(2)}) collective-permute-start(f32[3,10,128]{2,0,1:T(4,128)S(1)} %get-tuple-element.390), channel_id=1, source_target_pairs={{1,0},{2,1},{3,2},{4,3},{5,4},{6,5},{7,6},{8,7},{9,8},{10,9},{11,1... | collective-permute-start | bytes 46088 | tf_op jit(solution)/shard_map/ppermute | solution.py:27
  30.5 29.4 %collective-permute-start.10 = (f32[3,10,128]{2,0,1:T(4,128)S(1)}, f32[3,10,128]{2,0,1:T(4,128)S(1)}, u32[]{:S(2)}, u32[]{:S(2)}) collective-permute-start(f32[3,10,128]{2,0,1:T(4,128)S(1)} %get-tuple-element.389), channel_id=1, source_target_pairs={{2,0},{3,1},{4,2},{5,3},{6,4},{7,5},{8,6},{9,7},{10,8},{11,9},{12,... | collective-permute-start | bytes 46088 | tf_op jit(solution)/shard_map/ppermute | solution.py:27
  37.9 27.3 %collective-permute-start.11 = (f32[3,10,128]{2,0,1:T(4,128)S(1)}, f32[3,10,128]{2,0,1:T(4,128)S(1)}, u32[]{:S(2)}, u32[]{:S(2)}) collective-permute-start(f32[3,10,128]{2,0,1:T(4,128)S(1)} %get-tuple-element.388), channel_id=1, source_target_pairs={{3,0},{4,1},{5,2},{6,3},{7,4},{8,5},{9,6},{10,7},{11,8},{12,9},{13... | collective-permute-start | bytes 46088 | tf_op jit(solution)/shard_map/ppermute | solution.py:27
  43.5 33.2 %collective-permute-start = (s32[1]{0:T(128)}, s32[1]{0:T(128)}, u32[]{:S(2)}, u32[]{:S(2)}) collective-permute-start(s32[1]{0:T(128)} %get-tuple-element.419), channel_id=1, source_target_pairs={{0,0},{1,1},{2,2},{3,3},{4,4},{5,5},{6,6},{7,7},{8,8},{9,9},{10,10... | collective-permute-start | bytes 20 | tf_op jit(solution)/shard_map/ppermute | solution.py:27
  44.7 36.0 %collective-permute-start.1 = (s32[1]{0:T(128)}, s32[1]{0:T(128)}, u32[]{:S(2)}, u32[]{:S(2)}) collective-permute-start(s32[1]{0:T(128)} %get-tuple-element.422), channel_id=1, source_target_pairs={{96,0},{97,1},{98,2},{99,3},{100,4},{101,5},{102,6},{103,7},{104,8... | collective-permute-start | bytes 20 | tf_op jit(solution)/shard_map/ppermute | solution.py:27
  49.3 36.3 %collective-permute-start.2 = (s32[1]{0:T(128)}, s32[1]{0:T(128)}, u32[]{:S(2)}, u32[]{:S(2)}) collective-permute-start(s32[1]{0:T(128)} %get-tuple-element.421), channel_id=1, source_target_pairs={{64,0},{65,1},{66,2},{67,3},{68,4},{69,5},{70,6},{71,7},{72,8},{73... | collective-permute-start | bytes 20 | tf_op jit(solution)/shard_map/ppermute | solution.py:27
  60.0 29.6 %collective-permute-start.3 = (s32[1]{0:T(128)}, s32[1]{0:T(128)}, u32[]{:S(2)}, u32[]{:S(2)}) collective-permute-start(s32[1]{0:T(128)} %get-tuple-element.420), channel_id=1, source_target_pairs={{32,0},{33,1},{34,2},{35,3},{36,4},{37,5},{38,6},{39,7},{40,8},{41... | collective-permute-start | bytes 20 | tf_op jit(solution)/shard_map/ppermute | solution.py:27
  66.4 28.2 %copy-start.3 = (bf16[4,32,32]{2,1,0:T(8,128)(2,1)S(1)}, bf16[4,32,32]{2,1,0:T(8,128)(2,1)}, u32[]{:S(2)}) copy-start(bf16[4,32,32]{2,1,0:T(8,128)(2,1)} %param.12) | copy-start | bytes 24580
  76.6 15.6 %collective-permute-start.12 = (bf16[4,256]{1,0:T(4,128)(2,1)S(1)}, bf16[4,256]{1,0:T(4,128)(2,1)S(1)}, u32[]{:S(2)}, u32[]{:S(2)}) collective-permute-start(bf16[4,256]{1,0:T(4,128)(2,1)S(1)} %bitcast.365), channel_id=1, source_target_pairs={{0,0},{1,1},{2,2},{3,3},{4,4},{5,5},{6,6},{7,7},{8,8},{9,9},{10,10... | collective-permute-start | bytes 6152 | tf_op jit(solution)/shard_map/ppermute | solution.py:27
  76.7 15.6 %collective-permute-start.13 = (bf16[4,256]{1,0:T(4,128)(2,1)S(1)}, bf16[4,256]{1,0:T(4,128)(2,1)S(1)}, u32[]{:S(2)}, u32[]{:S(2)}) collective-permute-start(bf16[4,256]{1,0:T(4,128)(2,1)S(1)} %bitcast.367), channel_id=1, source_target_pairs={{96,0},{97,1},{98,2},{99,3},{100,4},{101,5},{102,6},{103,7},{104,8... | collective-permute-start | bytes 6152 | tf_op jit(solution)/shard_map/ppermute | solution.py:27
  80.7 13.0 %collective-permute-start.14 = (bf16[4,256]{1,0:T(4,128)(2,1)S(1)}, bf16[4,256]{1,0:T(4,128)(2,1)S(1)}, u32[]{:S(2)}, u32[]{:S(2)}) collective-permute-start(bf16[4,256]{1,0:T(4,128)(2,1)S(1)} %bitcast.364), channel_id=1, source_target_pairs={{64,0},{65,1},{66,2},{67,3},{68,4},{69,5},{70,6},{71,7},{72,8},{73... | collective-permute-start | bytes 6152 | tf_op jit(solution)/shard_map/ppermute | solution.py:27
  85.6 8.5 %collective-permute-start.15 = (bf16[4,256]{1,0:T(4,128)(2,1)S(1)}, bf16[4,256]{1,0:T(4,128)(2,1)S(1)}, u32[]{:S(2)}, u32[]{:S(2)}) collective-permute-start(bf16[4,256]{1,0:T(4,128)(2,1)S(1)} %bitcast.363), channel_id=1, source_target_pairs={{32,0},{33,1},{34,2},{35,3},{36,4},{37,5},{38,6},{39,7},{40,8},{41... | collective-permute-start | bytes 6152 | tf_op jit(solution)/shard_map/ppermute | solution.py:27
  94.7 40.6 %copy-start.1 = (bf16[4,32,32]{2,1,0:T(8,128)(2,1)}, bf16[4,32,32]{2,1,0:T(8,128)(2,1)S(1)}, u32[]{:S(2)}) copy-start(bf16[4,32,32]{2,1,0:T(8,128)(2,1)S(1)} %reshape.469) | copy-start | bytes 24580
  94.7 4.4 %collective-permute-start.16 = (f32[4,10,32]{2,1,0:T(8,128)S(1)}, f32[4,10,32]{2,1,0:T(8,128)S(1)}, u32[]{:S(2)}, u32[]{:S(2)}) collective-permute-start(f32[4,10,32]{2,1,0:T(8,128)S(1)} %get-tuple-element.398), channel_id=1, source_target_pairs={{0,128},{128,256},{256,384},{1,129},{129,257},{257,385},{2,130},{1... | collective-permute-start | bytes 15368 | tf_op jit(solution)/shard_map/ppermute | solution.py:35
  97.9 4.7 %collective-permute-start.17 = (f32[4,10,32]{2,1,0:T(8,128)S(1)}, f32[4,10,32]{2,1,0:T(8,128)S(1)}, u32[]{:S(2)}, u32[]{:S(2)}) collective-permute-start(f32[4,10,32]{2,1,0:T(8,128)S(1)} %get-tuple-element.399), channel_id=1, source_target_pairs={{128,0},{256,128},{384,256},{129,1},{257,129},{385,257},{130,2},{2... | collective-permute-start | bytes 15368 | tf_op jit(solution)/shard_map/ppermute | solution.py:38
  102.6 7.0 %collective-permute-start.18 = (f32[4,52,10]{2,1,0:T(8,128)S(1)}, f32[4,52,10]{2,1,0:T(8,128)S(1)}, u32[]{:S(2)}, u32[]{:S(2)}) collective-permute-start(f32[4,52,10]{2,1,0:T(8,128)S(1)} %get-tuple-element.396), channel_id=1, source_target_pairs={{0,1},{1,2},{2,3},{3,4},{4,5},{5,6},{6,7},{7,8},{8,9},{9,10},{10,1... | collective-permute-start | bytes 24968 | tf_op jit(solution)/shard_map/ppermute | solution.py:35
  107.7 6.1 %collective-permute-start.19 = (f32[4,52,10]{2,1,0:T(8,128)S(1)}, f32[4,52,10]{2,1,0:T(8,128)S(1)}, u32[]{:S(2)}, u32[]{:S(2)}) collective-permute-start(f32[4,52,10]{2,1,0:T(8,128)S(1)} %get-tuple-element.397), channel_id=1, source_target_pairs={{1,0},{2,1},{3,2},{4,3},{5,4},{6,5},{7,6},{8,7},{9,8},{10,9},{11,1... | collective-permute-start | bytes 24968 | tf_op jit(solution)/shard_map/ppermute | solution.py:38
  142.2 23.7 %copy-start.2 = (bf16[4,32,32]{2,1,0:T(8,128)(2,1)}, bf16[4,32,32]{2,1,0:T(8,128)(2,1)S(1)}, u32[]{:S(2)}) copy-start(bf16[4,32,32]{2,1,0:T(8,128)(2,1)S(1)} %fusion.168) | copy-start | bytes 24580
  142.7 19.2 %collective-permute-start.20 = (bf16[4,256]{1,0:T(4,128)(2,1)S(1)}, bf16[4,256]{1,0:T(4,128)(2,1)S(1)}, u32[]{:S(2)}, u32[]{:S(2)}) collective-permute-start(bf16[4,256]{1,0:T(4,128)(2,1)S(1)} %bitcast.368), channel_id=1, source_target_pairs={{0,0},{1,1},{2,2},{3,3},{4,4},{5,5},{6,6},{7,7},{8,8},{9,9},{10,10... | collective-permute-start | bytes 6152 | tf_op jit(solution)/shard_map/ppermute | solution.py:27
  142.7 19.2 %collective-permute-start.21 = (bf16[4,256]{1,0:T(4,128)(2,1)S(1)}, bf16[4,256]{1,0:T(4,128)(2,1)S(1)}, u32[]{:S(2)}, u32[]{:S(2)}) collective-permute-start(bf16[4,256]{1,0:T(4,128)(2,1)S(1)} %bitcast.369), channel_id=1, source_target_pairs={{32,0},{33,1},{34,2},{35,3},{36,4},{37,5},{38,6},{39,7},{40,8},{41... | collective-permute-start | bytes 6152 | tf_op jit(solution)/shard_map/ppermute | solution.py:27
  148.2 13.7 %collective-permute-start.22 = (bf16[4,256]{1,0:T(4,128)(2,1)S(1)}, bf16[4,256]{1,0:T(4,128)(2,1)S(1)}, u32[]{:S(2)}, u32[]{:S(2)}) collective-permute-start(bf16[4,256]{1,0:T(4,128)(2,1)S(1)} %bitcast.371), channel_id=1, source_target_pairs={{64,0},{65,1},{66,2},{67,3},{68,4},{69,5},{70,6},{71,7},{72,8},{73... | collective-permute-start | bytes 6152 | tf_op jit(solution)/shard_map/ppermute | solution.py:27
  157.6 8.2 %collective-permute-start.23 = (bf16[4,256]{1,0:T(4,128)(2,1)S(1)}, bf16[4,256]{1,0:T(4,128)(2,1)S(1)}, u32[]{:S(2)}, u32[]{:S(2)}) collective-permute-start(bf16[4,256]{1,0:T(4,128)(2,1)S(1)} %bitcast.373), channel_id=1, source_target_pairs={{96,0},{97,1},{98,2},{99,3},{100,4},{101,5},{102,6},{103,7},{104,8... | collective-permute-start | bytes 6152 | tf_op jit(solution)/shard_map/ppermute | solution.py:27
  191.6 15.5 %collective-permute-start.24 = (f32[3,10,128]{2,1,0:T(8,128)S(1)}, f32[3,10,128]{2,1,0:T(8,128)S(1)}, u32[]{:S(2)}, u32[]{:S(2)}) collective-permute-start(f32[3,10,128]{2,1,0:T(8,128)S(1)} %get-tuple-element.387), channel_id=1, source_target_pairs={{4,0},{5,1},{6,2},{7,3},{8,4},{9,5},{10,6},{11,7},{12,8},{13,9},{1... | collective-permute-start | bytes 46088 | tf_op jit(solution)/shard_map/ppermute | solution.py:27
  194.9 15.7 %collective-permute-start.25 = (f32[3,10,128]{2,1,0:T(8,128)S(1)}, f32[3,10,128]{2,1,0:T(8,128)S(1)}, u32[]{:S(2)}, u32[]{:S(2)}) collective-permute-start(f32[3,10,128]{2,1,0:T(8,128)S(1)} %get-tuple-element.386), channel_id=1, source_target_pairs={{3,0},{4,1},{5,2},{6,3},{7,4},{8,5},{9,6},{10,7},{11,8},{12,9},{13... | collective-permute-start | bytes 46088 | tf_op jit(solution)/shard_map/ppermute | solution.py:27
  199.6 13.8 %collective-permute-start.26 = (f32[3,10,128]{2,1,0:T(8,128)S(1)}, f32[3,10,128]{2,1,0:T(8,128)S(1)}, u32[]{:S(2)}, u32[]{:S(2)}) collective-permute-start(f32[3,10,128]{2,1,0:T(8,128)S(1)} %get-tuple-element.385), channel_id=1, source_target_pairs={{2,0},{3,1},{4,2},{5,3},{6,4},{7,5},{8,6},{9,7},{10,8},{11,9},{12,... | collective-permute-start | bytes 46088 | tf_op jit(solution)/shard_map/ppermute | solution.py:27
  205.0 13.0 %collective-permute-start.27 = (f32[3,10,128]{2,1,0:T(8,128)S(1)}, f32[3,10,128]{2,1,0:T(8,128)S(1)}, u32[]{:S(2)}, u32[]{:S(2)}) collective-permute-start(f32[3,10,128]{2,1,0:T(8,128)S(1)} %get-tuple-element.384), channel_id=1, source_target_pairs={{1,0},{2,1},{3,2},{4,3},{5,4},{6,5},{7,6},{8,7},{9,8},{10,9},{11,1... | collective-permute-start | bytes 46088 | tf_op jit(solution)/shard_map/ppermute | solution.py:27
  207.1 10.9 %collective-permute-start.28 = (f32[3,10,128]{2,1,0:T(8,128)S(1)}, f32[3,10,128]{2,1,0:T(8,128)S(1)}, u32[]{:S(2)}, u32[]{:S(2)}) collective-permute-start(f32[3,10,128]{2,1,0:T(8,128)S(1)} %get-tuple-element.383), channel_id=1, source_target_pairs={{0,0},{1,1},{2,2},{3,3},{4,4},{5,5},{6,6},{7,7},{8,8},{9,9},{10,10... | collective-permute-start | bytes 46088 | tf_op jit(solution)/shard_map/ppermute | solution.py:27
  207.1 10.9 %collective-permute-start.29 = (f32[3,10,128]{2,1,0:T(8,128)S(1)}, f32[3,10,128]{2,1,0:T(8,128)S(1)}, u32[]{:S(2)}, u32[]{:S(2)}) collective-permute-start(f32[3,10,128]{2,1,0:T(8,128)S(1)} %get-tuple-element.382), channel_id=1, source_target_pairs={{127,0},{0,1},{1,2},{2,3},{3,4},{4,5},{5,6},{6,7},{7,8},{8,9},{9,1... | collective-permute-start | bytes 46088 | tf_op jit(solution)/shard_map/ppermute | solution.py:27
  210.6 7.9 %collective-permute-start.30 = (f32[3,10,128]{2,1,0:T(8,128)S(1)}, f32[3,10,128]{2,1,0:T(8,128)S(1)}, u32[]{:S(2)}, u32[]{:S(2)}) collective-permute-start(f32[3,10,128]{2,1,0:T(8,128)S(1)} %get-tuple-element.381), channel_id=1, source_target_pairs={{126,0},{127,1},{0,2},{1,3},{2,4},{3,5},{4,6},{5,7},{6,8},{7,9},{8... | collective-permute-start | bytes 46088 | tf_op jit(solution)/shard_map/ppermute | solution.py:27
  213.4 8.6 %collective-permute-start.31 = (f32[3,10,128]{2,1,0:T(8,128)S(1)}, f32[3,10,128]{2,1,0:T(8,128)S(1)}, u32[]{:S(2)}, u32[]{:S(2)}) collective-permute-start(f32[3,10,128]{2,1,0:T(8,128)S(1)} %get-tuple-element.380), channel_id=1, source_target_pairs={{125,0},{126,1},{127,2},{0,3},{1,4},{2,5},{3,6},{4,7},{5,8},{6,9},... | collective-permute-start | bytes 46088 | tf_op jit(solution)/shard_map/ppermute | solution.py:27
Sparse Core Ops, SparseCore 0:
  223.3 30.4 all-gather.2
where the time goes:
time: 265 us; the launch traced here: 264 us
  starting transfers between devices  121 us (46%)
  waiting for transfers between devices  48.1 us (18%)
  other arithmetic  39.1 us (15%)
  matrix products  30.1 us (11%)
  between operations  15 us (6%)
  local copies, waits for them, and re-layouts  9.78 us (4%)
    ppermute x28, starting transfers between devices, shifted(): return lax.ppermute(block, axis, route)  110 us
    all_gather x1, waiting for transfers between devices, total_of_pieces(): return lax.all_gather(shard, axis).sum(0)  30.7 us
    add x2, other arithmetic, blur_valid(): across = across + weights[offset] * source[:, :, offset:offset + col_count]  14.4 us
    ppermute x28, waiting for transfers between devices, shifted(): return lax.ppermute(block, axis, route)  9.92 us
    ppermute x2, starting transfers between devices, extended(): lax.ppermute(lax.slice_in_dim(block, block.shape[dim] - width, None, axis...  8.17 us
    dot_general x4, matrix products, composite(): jnp.einsum('ij,mjp->mip', lower_strict, log_keep, precision=highest)  8.16 us
    ppermute x2, waiting for transfers between devices, extended(): lax.ppermute(lax.slice_in_dim(block, 0, width, axis=dim), axis, backward)  7.49 us
    mul x1, other arithmetic, on_device(): back_blur = blur_valid(smooth_wide * inside_mask[None, :, :], RADIUS)  6.95 us
  transfers between devices with their start and end apart: 33, of which 8 were waited for; matrix products, arithmetic and copies ran while one was open for 7% of the time, Pallas kernels for 0%

commit v1 on v0

v1 whole, which is shorter than its diff:
```python
import functools
import math

import jax
import jax.numpy as jnp
import numpy as np
from jax import lax
from jax.experimental import pallas as pl
from jax.experimental.pallas import tpu as pltpu
from jax.sharding import Mesh
from jax.sharding import PartitionSpec as P

TILE = 16
BLOCK = 128
CH = 4
SLOTS = 16
NEAR = 8
CAP = 3
RADIUS = 5
TILES = 4
PIX = 256
N_IMG = 4
N_ZQ = 4
N_ZR = 4
N_YC = 8
BLK_DEV = 96
VALS = 10
MSG = 32
SIDE = 32

lam_weight = 0.2
loss_weight = 16.0
sigma_window = 1.5
log2e = math.log2(math.e)

f32 = jnp.float32
bf16 = jnp.bfloat16
highest = lax.Precision.HIGHEST
GS = ("zq", "zr", "yc")

REQ, CNT, REN, LST, TCN, YC, IMG, ZQ, MID = 0, 24, 32, 36, 52, 56, 57, 58, 59


def constants():
    lane = np.arange(128)
    pix = np.arange(PIX)
    x = pix % TILE - 7.5
    y = pix // TILE - 7.5
    moments = np.stack([np.ones(PIX), x, y, x * x, x * y, y * y], axis=1)
    mom = np.zeros((PIX, 32))
    for part in range(3):
        mom[:, part * 8 : part * 8 + 6] = moments
    momt = np.zeros((16, PIX))
    momt[:6] = moments.T
    before = (np.arange(128)[:, None] < np.arange(128)[None, :]).astype(float)
    ones = np.ones((128, 128))
    tri = np.tile(np.concatenate([before, ones], axis=1), (2, 1))
    trib = np.tile(np.concatenate([before.T, ones], axis=1), (2, 1))
    spread = (pix[:, None] % 16 == lane[None, :] % 16).astype(float)
    place = np.zeros((CH, SIDE, 128))
    for c in range(CH):
        for col in range(SIDE):
            place[c, col, (col // 16) * 64 + c * 16 + col % 16] = 1.0
    offsets = np.arange(-RADIUS, RADIUS + 1)
    window = np.exp(-offsets * offsets / (2.0 * sigma_window**2))
    window = window / window.sum()
    rows = N_IMG * SIDE

    def band(count):
        full = np.zeros((count, count))
        for a in range(count):
            for b in range(max(0, a - RADIUS), min(count, a + RADIUS + 1)):
                full[a, b] = window[b - a + RADIUS]
        return full

    vert = band(rows)
    vert = (vert @ vert).reshape(N_IMG, SIDE, rows)
    wide = band(96)
    inner = (wide @ wide)[16:80, 32:64]
    edge = band(64)
    edge = edge @ edge
    left = np.zeros((64, 32))
    left[16:] = edge[:48, :32]
    right = np.zeros((64, 32))
    right[:48] = edge[16:, 32:]
    horiz = np.zeros((3, 256, 128))
    for kind, table in enumerate((inner, left, right)):
        for src in range(64):
            strip = src // 16 - 1
            for c in range(CH):
                if 0 <= strip < 2:
                    row = strip * 64 + c * 16 + src % 16
                elif strip == 2:
                    row = 128 + c * 16 + src % 16
                else:
                    row = 192 + c * 16 + src % 16
                for dst in range(32):
                    horiz[kind, row, (dst // 16) * 64 + c * 16 + dst % 16] = table[src, dst]
    return dict(
        mom=jnp.asarray(mom, bf16),
        momt=jnp.asarray(momt, bf16),
        tri=jnp.asarray(tri, bf16),
        trib=jnp.asarray(trib, bf16),
        spread=jnp.asarray(spread, bf16),
        spreadt=jnp.asarray(spread.T, bf16),
        place=jnp.asarray(place, bf16),
        placet=jnp.asarray(place.transpose(0, 2, 1), bf16),
        vert=jnp.asarray(vert, f32),
        horiz=jnp.asarray(horiz, f32),
    )


def dot(a, b, dims=((1,), (0,)), precision=None):
    return lax.dot_general(a, b, (dims, ((), ())), precision=precision, preferred_element_type=f32)


def halves(value):
    high = value.astype(bf16)
    low = (value - high.astype(f32)).astype(bf16)
    return high, low


def iota(shape, dim):
    return lax.broadcasted_iota(jnp.int32, shape, dim)


def source_places(ints):
    ends = []
    total = 0
    for o in range(NEAR):
        total = total + ints[CNT + o]
        ends.append(total)
    places = []
    for e in range(SLOTS):
        s = ints[LST + e]
        group = 0
        start = 0
        for o in range(NEAR):
            past = s >= ends[o]
            group = group + jnp.where(past, 1, 0)
            start = start + jnp.where(past, ints[CNT + o], 0)
        apart = ints[YC] + group - NEAR // 2
        near = jnp.bitwise_and(apart, 7)
        chunk = jnp.where(apart == near, near, 8 + jnp.bitwise_and(near, 3))
        places.append(chunk * CAP + s - start)
    return places


def list_slots(ints):
    ends = []
    total = 0
    for t in range(TILES - 1):
        total = total + ints[TCN + t]
        ends.append(total)
    slots = []
    for e in range(SLOTS):
        slot = 0
        for t in range(TILES - 1):
            slot = slot + jnp.where(ends[t] <= e, 1, 0)
        slots.append(slot)
    return slots


def pack_kernel(ints, gauss, out):
    lane = iota((1, 128), 1) % 32
    for chunk in range(N_YC):
        group = jnp.bitwise_and(ints[YC] + NEAR // 2 - chunk, 7)
        ids = []
        for c in range(CAP):
            idx = ints[REQ + group * CAP + c]
            out[chunk, 10 * c : 10 * c + 10, :] = gauss[idx]
            ids.append(idx)
        row = jnp.where(lane < 10, ids[0], jnp.where(lane < 20, ids[1], ids[2]))
        out[chunk, 30:32, :] = jnp.broadcast_to(row.astype(f32), (2, 128))


def forward_kernel(ints, own, cross, target, mom, tri, spread, place, payload, raws, pair_w, beta_o,
                   blk, vals, coefs, cols):
    for m in range(12):
        for c in range(CAP):
            src = own[m, 10 * c : 10 * c + 10, :] if m < 8 else cross[m - 8, 10 * c : 10 * c + 10, :]
            blk[m * CAP + c, 0:10, :] = src
    places = source_places(ints)
    slots = list_slots(ints)
    for e in range(SLOTS):
        raw = blk[places[e]]
        raws[e] = raw
        for v in range(6):
            vals[v, e : e + 1, :] = raw[v : v + 1, :]
    mx = vals[0] - 8.0
    my = vals[1] - 8.0
    ca = vals[2]
    cc = vals[4]
    cb = vals[3] * jnp.sqrt(ca * cc)
    logit = vals[5]
    logsig = logit - jnp.log1p(jnp.exp(logit))
    ax = ca * mx + cb * my
    ay = cb * mx + cc * my
    table = [
        log2e * (logsig - 0.5 * (ax * mx + ay * my)),
        log2e * ax,
        log2e * ay,
        (-0.5 * log2e) * ca,
        -log2e * cb,
        (-0.5 * log2e) * cc,
    ]
    coefs[...] = jnp.zeros_like(coefs)
    for k in range(6):
        high = table[k].astype(bf16).astype(f32)
        rest = table[k] - high
        mid = rest.astype(bf16).astype(f32)
        for e in range(SLOTS):
            coefs[e, k : k + 1, :] = high[e : e + 1, :]
            coefs[e, 8 + k : 9 + k, :] = mid[e : e + 1, :]
            coefs[e, 16 + k : 17 + k, :] = (rest - mid)[e : e + 1, :]
    cols[...] = jnp.zeros_like(cols)
    carry = jnp.zeros((PIX, 128), f32)
    for e in range(SLOTS):
        power = dot(mom[...], coefs[e].astype(bf16))
        alpha = jnp.exp2(power)
        lost = alpha * (
            -log2e + alpha * (-log2e / 2 + alpha * (-log2e / 3 + alpha * (-log2e / 4 + alpha * (-log2e / 5))))
        )
        sums = dot(jnp.concatenate(halves(lost), axis=1), tri[...])
        if e:
            carry = jnp.where(slots[e] == slots[e - 1], carry, 0.0)
        weight = jnp.exp2(sums[:, :128] + carry) * alpha
        carry = carry + sums[:, 128:]
        beta_o[e] = alpha * (1.0 + alpha * (1.0 + alpha * (1.0 + alpha * (1.0 + alpha))))
        both = jnp.concatenate(halves(weight), axis=1)
        pair_w[e] = both
        shade_high, shade_low = halves(raws[e, 6:10, :])
        upper = jnp.concatenate([shade_high, shade_high], axis=1)
        lower = jnp.concatenate([shade_low, jnp.zeros_like(shade_low)], axis=1)
        cols[slots[e]] += dot(jnp.concatenate([upper.astype(f32), lower.astype(f32)], axis=0).astype(bf16), both,
                              ((1,), (1,)))
    row_of = iota((TILE, PIX), 1) // TILE == iota((TILE, PIX), 0)
    lane = iota((TILE, 128), 1)
    pieces = []
    for s in range(TILES):
        colour = cols[s]
        colour = colour[0:4, :] + colour[4:8, :]
        for c in range(CH):
            pieces.append(jnp.where(row_of, jnp.broadcast_to(colour[c : c + 1, :], (TILE, PIX)), 0.0))
    laid = dot(jnp.concatenate(pieces, axis=0).astype(bf16), spread[...])
    tiles = []
    for s in range(TILES):
        tile = jnp.zeros((TILE, 128), f32)
        for c in range(CH):
            at = s * 64 + c * 16
            tile = jnp.where((lane // 16) % 4 == c, laid[at : at + 16, :], tile)
        tiles.append(tile)
    goal = jnp.zeros((SIDE, 128), f32)
    for c in range(CH):
        goal = goal + dot(target[c], place[c])
    body = jnp.concatenate(
        [jnp.where(lane < 64, tiles[0], tiles[1]), jnp.where(lane < 64, tiles[2], tiles[3]), goal], axis=0
    ).astype(bf16)
    row = iota((8, 128), 0)
    tags = jnp.zeros((8, 128), jnp.int32)
    for s in range(TILES):
        tags = jnp.where(row == s, jnp.bitwise_and(ints[REN + s], 3), tags)
    tags = tags.astype(f32).astype(bf16)
    for q in range(N_IMG * N_ZQ):
        payload[q, 0:64, :] = body
        payload[q, 64:72, :] = tags


def error_kernel(ints, got, vert, placet, up, err_own, rendered, errs, images):
    lane = iota((TILE, 128), 1)
    half = lane // 64
    halff = half.astype(f32)
    for strip in range(N_IMG):
        for home in range(N_ZQ):
            acc = [jnp.zeros((TILE, 128), f32), jnp.zeros((TILE, 128), f32)]
            for s in range(TILES):
                src = strip * 4 + (home - s) % 4
                both = got[src, 16 * (s // 2) : 16 * (s // 2) + 16, :].astype(f32)
                turned = pltpu.roll(both, 64, 1)
                tile = jnp.where(half == s % 2, both, turned)
                tag = jnp.broadcast_to(got[src, 64:72, :].astype(f32)[s : s + 1, :], (TILE, 128)) - halff
                acc[0] = jnp.where(tag == 0.0, tile, acc[0])
                acc[1] = jnp.where(tag == 2.0, tile, acc[1])
            image = jnp.concatenate(acc, axis=0)
            images[strip * 4 + home] = image
            goal = got[strip * 4 + home, 32:64, :].astype(f32)
            errs[strip * 32 : strip * 32 + 32, home * 128 : home * 128 + 128] = image - goal
    img = ints[IMG]
    blurred = dot(vert[img], errs[...], precision=highest)
    for home in range(N_ZQ):
        up[home] = blurred[:, home * 128 : home * 128 + 128]
        err_own[home] = errs[pl.ds(pl.multiple_of(img * 32, 32), 32), home * 128 : home * 128 + 128]
    mine = images[img * 4 + ints[ZQ]].astype(bf16)
    for c in range(CH):
        rendered[c] = dot(mine, placet[c]).astype(bf16)


def backward_kernel(ints, up, got_mate, got_other, err_own, horiz, placet, spreadt, momt, trib, raws, pair_w,
                    beta_i, own, cross, grad_out, msg_own, msg_cross,
                    ext, back, grads, grow, gcol, vals, sums, blk, pack):
    parity = jnp.bitwise_and(ints[YC], 1)
    place_mid = ints[MID]
    lane32 = iota((SIDE, 128), 1)
    for home in range(N_ZQ):
        at_left = home - jnp.where(place_mid == 0, 1, 0)
        at_right = home + jnp.where(place_mid == 31, 1, 0)
        in_left = at_left >= 0
        in_right = at_right < N_ZQ
        at_left = jnp.maximum(at_left, 0)
        at_right = jnp.minimum(at_right, N_ZQ - 1)
        left = jnp.where(parity == 0, got_other[at_left], got_mate[at_left])
        right = jnp.where(parity == 0, got_mate[at_right], got_other[at_right])
        left = jnp.where(in_left, left, 0.0)
        right = jnp.where(in_right, right, 0.0)
        rows = slice(home * 32, home * 32 + 32)
        ext[rows, 0:128] = up[home]
        ext[rows, 128:256] = jnp.where(lane32 < 64, right, left)
    back[...] = dot(ext[...], horiz[0], precision=highest)

    @pl.when(place_mid == 0)
    def _():
        back[0:32, :] = dot(ext[0:32, :], horiz[1], precision=highest)

    @pl.when(place_mid == 31)
    def _():
        back[96:128, :] = dot(ext[96:128, :], horiz[2], precision=highest)

    for home in range(N_ZQ):
        total = loss_weight * (
            (1.0 - lam_weight) * err_own[home] + lam_weight * back[home * 32 : home * 32 + 32, :]
        )
        grads[home] = total.astype(bf16).astype(f32)
    mine = grads[ints[ZQ]].astype(bf16)
    for c in range(CH):
        grad_out[c] = dot(mine, placet[c]).astype(bf16)

    lane = iota((TILE, 128), 1)
    pieces = []
    for s in range(TILES):
        home = jnp.bitwise_and(ints[ZQ] + s, 3)
        local = jnp.bitwise_and(ints[REN + s], 3)
        down = local // 2
        across = jnp.bitwise_and(local, 1)
        tile = grads[home, pl.ds(pl.multiple_of(down * 16, 16), 16), :]
        for c in range(CH):
            pieces.append(jnp.where(lane // 16 == across * 4 + c, tile, 0.0))
    laid = dot(jnp.concatenate(pieces, axis=0).astype(bf16), spreadt[...])
    row_of = iota((TILE, PIX), 1) // TILE == iota((TILE, PIX), 0)
    for s in range(TILES):
        lines = []
        for c in range(CH):
            at = s * 64 + c * 16
            lines.append(jnp.sum(jnp.where(row_of, laid[at : at + 16, :], 0.0), axis=0, keepdims=True))
        four = jnp.concatenate(lines, axis=0)
        sixteen = jnp.concatenate([four, four, four, jnp.zeros_like(four)], axis=0)
        grow[s] = sixteen.astype(bf16)
        gcol[s] = jnp.transpose(sixteen).astype(bf16)

    slots = list_slots(ints)
    places = source_places(ints)
    carry = jnp.zeros((PIX, 128), f32)
    for e in reversed(range(SLOTS)):
        both = pair_w[e]
        weight = both[:, :128].astype(f32) + both[:, 128:].astype(f32)
        shade = raws[e, 6:10, :]
        high = shade.astype(bf16).astype(f32)
        rest = shade - high
        mid = rest.astype(bf16).astype(f32)
        shades = jnp.concatenate([high, mid, rest - mid, jnp.zeros_like(high)], axis=0).astype(bf16)
        shade_dot = dot(gcol[slots[e]], shades)
        product = weight * shade_dot
        after = dot(jnp.concatenate(halves(product), axis=1), trib[...])
        if e < SLOTS - 1:
            carry = jnp.where(slots[e] == slots[e + 1], carry, 0.0)
        unit = product - (after[:, :128] + carry) * beta_i[e]
        carry = carry + after[:, 128:]
        moment = dot(momt[...], jnp.concatenate(halves(unit), axis=1))
        moment = moment[:, :128] + moment[:, 128:]
        shade_grad = dot(grow[slots[e]], both)
        shade_grad = shade_grad[:, :128] + shade_grad[:, 128:]
        for k in range(6):
            vals[k, e : e + 1, :] = raws[e, k : k + 1, :]
            sums[k, e : e + 1, :] = moment[k : k + 1, :]
        for c in range(CH):
            sums[6 + c, e : e + 1, :] = shade_grad[c : c + 1, :]
    mx = vals[0] - 8.0
    my = vals[1] - 8.0
    ca = vals[2]
    rho = vals[3]
    cc = vals[4]
    opaque = jax.nn.sigmoid(vals[5])
    m0 = -0.5 * sums[0]
    m1 = -0.5 * sums[1]
    m2 = -0.5 * sums[2]
    m3 = -0.5 * sums[3]
    m4 = -0.5 * sums[4]
    m5 = -0.5 * sums[5]
    along_x = m1 - mx * m0
    along_y = m2 - my * m0
    square_x = m3 - 2.0 * mx * m1 + mx * mx * m0
    square_y = m5 - 2.0 * my * m2 + my * my * m0
    mixed = m4 - mx * m2 - my * m1 + mx * my * m0
    root = jnp.sqrt(ca * cc)
    cb = rho * root
    out = [
        -2.0 * (ca * along_x + cb * along_y),
        -2.0 * (cb * along_x + cc * along_y),
        square_x + rho * jnp.sqrt(cc / ca) * mixed,
        2.0 * root * mixed,
        square_y + rho * jnp.sqrt(ca / cc) * mixed,
        (1.0 - opaque) * sums[0],
    ] + [sums[6 + c] for c in range(CH)]
    blk[...] = jnp.zeros_like(blk)
    for e in range(SLOTS):
        for v in range(VALS):
            blk[places[e], v : v + 1, :] = out[v][e : e + 1, :]
    lane1 = iota((2, 128), 1)
    group = jnp.where(lane1 // 32 == jnp.bitwise_and(ints[YC], 3), 1.0, 0.0)
    for m in range(12):
        for c in range(CAP):
            pack[m, 10 * c : 10 * c + 10, :] = blk[m * CAP + c, 0:10, :]
        ids = own[m, 30:32, :] if m < 8 else cross[m - 8, 30:32, :]
        pack[m, 30:32, :] = ids * group
    msg_own[...] = pack[0:8].astype(bf16)
    msg_cross[...] = pack[8:12].astype(bf16)


def collect_kernel(got, out):
    lane = iota((1, 128), 1)
    line = lane % 32
    value = jnp.where(line < 10, line, jnp.where(line < 20, line - 10, line - 20))
    goals = []
    for quad in range(8):
        ids = jnp.zeros((1, 128), f32)
        for m in range(4):
            ids = ids + got[quad * 4 + m, 16:32, :].astype(f32)[14:15, :]
        goals.append(jnp.where(line < 30, ids.astype(jnp.int32) * 16 + value, -1))
    flat = got[...].reshape(32 * MSG, 128)
    rows = 384
    for part in range(BLK_DEV * 16 // rows):
        here = iota((rows, 128), 0) + part * rows
        hits = [jnp.where(here == goal, 1.0, 0.0).astype(bf16) for goal in goals]
        total = dot(jnp.concatenate(hits, axis=1), flat)
        out[part * 24 : part * 24 + 24] = total.reshape(24, 16, 128)[:, :VALS, :]


VM = pl.BlockSpec(memory_space=pltpu.VMEM)
SM = pl.BlockSpec(memory_space=pltpu.SMEM)


def call(kernel, outs, scratch, n_in, name, flops=0):
    return pl.pallas_call(
        kernel,
        out_shape=tuple(jax.ShapeDtypeStruct(shape, dtype) for shape, dtype in outs),
        in_specs=[SM] + [VM] * (n_in - 1) if name != "collect" else [VM] * n_in,
        out_specs=tuple(VM for _ in outs),
        scratch_shapes=[pltpu.VMEM(shape, dtype) for shape, dtype in scratch],
        name=name,
    )


def on_device(gaussians, target, request, near_counts, render_tile, tile_lists, tile_counts):
    table = constants()
    yc = lax.axis_index("yc")
    img = lax.axis_index("img")
    zq = lax.axis_index("zq")
    mid = lax.axis_index("zr") * N_YC + yc
    ints = jnp.concatenate(
        [
            request.reshape(24),
            near_counts.reshape(8),
            render_tile.reshape(4),
            tile_lists.reshape(16),
            tile_counts.reshape(4),
            jnp.stack([yc, img, zq, mid, yc, yc, yc, yc]).astype(jnp.int32),
        ]
    )
    n_gs = N_ZQ * N_ZR * N_YC
    up_route = []
    for r in range(n_gs):
        j = r % N_YC
        if j < 4:
            up_route.append((r, (r + N_YC) % n_gs))
        elif j > 4:
            up_route.append((r, (r - N_YC) % n_gs))
    back_route = [(b, a) for a, b in up_route]

    (sent,) = call(pack_kernel, [((N_YC, MSG, 128), f32)], [], 2, "pack")(ints, gaussians)
    own = lax.all_to_all(sent, "yc", 0, 0, tiled=True)
    crossing = jnp.where(yc < 4, own[4:8], own[0:4])
    cross = lax.ppermute(crossing, GS, up_route)

    payload, raws, pair_w, beta = call(
        forward_kernel,
        [
            ((N_IMG * N_ZQ, 72, 128), bf16),
            ((SLOTS, 16, 128), f32),
            ((SLOTS, PIX, 256), bf16),
            ((SLOTS, PIX, 128), f32),
        ],
        [((36, 16, 128), f32), ((6, 16, 128), f32), ((SLOTS, 32, 128), f32), ((TILES, 8, PIX), f32)],
        8,
        "forward",
    )(ints, own, cross, target, table["mom"], table["tri"], table["spread"], table["place"])
    got = lax.all_to_all(payload, ("img", "zq"), 0, 0, tiled=True)

    up, err_own, rendered = call(
        error_kernel,
        [((N_ZQ, SIDE, 128), f32), ((N_ZQ, SIDE, 128), f32), ((CH, SIDE, SIDE), bf16)],
        [((N_IMG * SIDE, 512), f32), ((16, SIDE, 128), f32)],
        4,
        "error",
    )(ints, got, table["vert"], table["placet"])

    other = [((2 * c - 1) % n_gs, 2 * c) for c in range(n_gs // 2)]
    other = other + [(b, a) for a, b in other]
    got_other = lax.ppermute(up, GS, other)
    got_mate = lax.ppermute(up, GS, [(r, r ^ 1) for r in range(n_gs)])

    pixel_grad, msg_own, msg_cross = call(
        backward_kernel,
        [((CH, SIDE, SIDE), bf16), ((N_YC, MSG, 128), bf16), ((4, MSG, 128), bf16)],
        [
            ((128, 256), f32),
            ((128, 128), f32),
            ((N_ZQ, SIDE, 128), f32),
            ((TILES, 16, PIX), bf16),
            ((TILES, PIX, 16), bf16),
            ((6, 16, 128), f32),
            ((10, 16, 128), f32),
            ((36, 16, 128), f32),
            ((12, MSG, 128), f32),
        ],
        15,
        "backward",
    )(
        ints, up, got_mate, got_other, err_own, table["horiz"], table["placet"], table["spreadt"], table["momt"],
        table["trib"], raws, pair_w, beta, own, cross,
    )
    returned = lax.ppermute(msg_cross, GS, back_route)
    apart = jnp.arange(N_YC) + NEAR // 2 - yc
    straight = ((apart >= 0) & (apart < NEAR))[:, None, None]
    merged = jnp.where(straight, msg_own, jnp.concatenate([returned, returned], axis=0))
    spread_out = jnp.broadcast_to(merged[None], (N_IMG, N_YC, MSG, 128)).reshape(N_IMG * N_YC, MSG, 128)
    all_msgs = lax.all_to_all(spread_out, ("img", "yc"), 0, 0, tiled=True)
    (summed,) = call(collect_kernel, [((BLK_DEV, VALS, 128), f32)], [], 1, "collect")(all_msgs)
    return (rendered, pixel_grad, summed)


def solution(mesh):
    wide = Mesh(mesh.devices.reshape(N_IMG, N_ZQ, N_ZR, N_YC), ("img", "zq", "zr", "yc"))
    in_specs = (
        P(GS, None, None),
        P(None, "img", GS),
        P("img", GS, None, None),
        P("img", GS, None),
        P("img", GS, None),
        P("img", GS, None),
        P("img", GS, None),
    )
    out_specs = (P(None, "img", GS), P(None, "img", GS), P(GS, None, None))
    return jax.shard_map(on_device, mesh=wide, in_specs=in_specs, out_specs=out_specs, check_vma=False)
```

time: 265 us -> 123 us (0.46)
  starting transfers between devices: 121 us -> 22.2 us
  blocking collectives: 0 us -> 48.1 us
  other arithmetic: 39.1 us -> 0.94 us
  waiting for transfers between devices: 48.1 us -> 16.4 us
  matrix products: 30.1 us -> 0 us
  Pallas kernels: 0 us -> 25.9 us
  between operations: 15 us -> 0.7 us
    ppermute x32 -> x4, starting transfers between devices: 121 us -> 12.1 us  [the longest x1 6.19 us: on_device(): got_other = lax.ppermute(up, GS, other)]
    all_to_all x0 -> x2, blocking collectives: none -> 48.1 us  [the longest x1 30.9 us: on_device(): got = lax.all_to_all(payload, ('img', 'zq'), 0, 0, tiled=True)]
    all_gather x1 -> x0, waiting for transfers between devices: 30.7 us -> none  [total_of_pieces(): return lax.all_gather(shard, axis).sum(0)]
    dot_general x41 -> x0, matrix products: 30.1 us -> none  [the longest x4 8.16 us: composite(): jnp.einsum('ij,mjp->mip', lower_strict, log_keep, precision=highest)]
    pallas_call x0 -> x5, Pallas kernels: none -> 25.9 us  [the longest x1 9.85 us: on_device(): call(backward_kernel, [((CH, SIDE, SIDE), bf16), ((N_YC, MSG, 128), bf16)...]
    add x11 -> x0, other arithmetic: 14.5 us -> none  [the longest x2 14.4 us: blur_valid(): across = across + weights[offset] * source[:, :, offset:offset + col_count]]
    all_to_all x0 -> x1, starting transfers between devices: none -> 10.1 us  [on_device(): own = lax.all_to_all(sent, 'yc', 0, 0, tiled=True)]
    convert_element_type x4 -> x0, other arithmetic: 7.02 us -> none  [the longest x1 6.93 us: on_device(): (loss_weight * ((1.0 - lam_weight) * error_map + lam_weight * back_blur))...]
  transfers between devices with their start and end apart: 33 -> 5, of which waited for: 8 -> 5; matrix products, arithmetic and copies ran while one was open for 7% -> 0% of each run, Pallas kernels for 0% -> 0%
where the time goes in v1:
time: 123 us; the launch traced here: 122 us
  blocking collectives  48.1 us (39%)
  Pallas kernels  25.9 us (21%)
  starting transfers between devices  22.2 us (18%)
  waiting for transfers between devices  16.4 us (13%)
  local copies, waits for them, and re-layouts  7.74 us (6%)
    all_to_all x1, blocking collectives, on_device(): got = lax.all_to_all(payload, ('img', 'zq'), 0, 0, tiled=True)  30.9 us
    all_to_all x1, blocking collectives, on_device(): all_msgs = lax.all_to_all(spread_out, ('img', 'yc'), 0, 0, tiled=True)  17.2 us
    all_to_all x1, starting transfers between devices, on_device(): own = lax.all_to_all(sent, 'yc', 0, 0, tiled=True)  10.1 us
    pallas_call x1, Pallas kernels, on_device(): call(backward_kernel, [((CH, SIDE, SIDE), bf16), ((N_YC, MSG, 128), bf16)...  9.85 us
    pallas_call x1, Pallas kernels, on_device(): call(forward_kernel, [((N_IMG * N_ZQ, 72, 128), bf16), ((SLOTS, 16, 128),...  9.32 us
    ppermute x1, waiting for transfers between devices, on_device(): cross = lax.ppermute(crossing, GS, up_route)  6.66 us
    unnamed x11, local copies, waits for them, and re-layouts  6.3 us
    ppermute x1, starting transfers between devices, on_device(): got_other = lax.ppermute(up, GS, other)  6.19 us
  transfers between devices with their start and end apart: 5, of which 5 were waited for; matrix products, arithmetic and copies ran while one was open for 0% of the time, Pallas kernels for 0%

profile of v1, /device:TPU:1, one launch (start us, length us, event | category | flops | bytes accessed | tf_op | source)
XLA Modules:
  0.0 122.0 jit_solution(9147136477396095898)
XLA Ops:
  0.6 0.8 copy.23
  1.4 0.1 reshape.33
  1.5 2.2 %copy.24.gauss = f32[96,10,128]{2,1,0:T(8,128)} copy(f32[96,10,128]{2,0,1:T(8,128)} %param.17) | data formatting | bytes 983040 | tf_op args[0]
  3.7 1.3 %concatenate.6.ints = s32[64]{0:T(128)} concatenate(s32[24]{0:T(128)S(1)} %reshape.33, s32[8]{0:T(128)} %bitcast.12, s32[4]{0:T(128)} %bitcast.13, s32[16]{0:T(128)} %bitcast.14, s32[4]{0:T(128)} %bitcast.15, s32[1]{0:T(128)} %bitcast.4, s32[1]{0:T(128)} %bitcast.5, s32[1]{0:T(128)} %bitcast.6, s32[1]{0:T(128)} %bitcast.7, s32[1]{0:T(128)} %bitcast.4, s32[1]{0:T(128)} %bitcast.4, ...), dimensions={0} | concatenate | bytes 512 | tf_op jit(solution)/shard_map/concatenate | solution.py:468
  5.0 1.8 %pack.1 = f32[8,32,128]{2,1,0:T(8,128)} custom-call(s32[64]{0:T(128)} %concatenate.6.ints, f32[96,10,128]{2,1,0:T(8,128)} %copy.24.gauss), custom_call_target="tpu_custom_call" | custom-call | tf_op jit(solution)/shard_map/pack/pallas_call | solution.py:488
  6.9 10.1 %all-to-all-start = ((f32[8,32,128]{2,1,0:T(8,128)}), f32[8,32,128]{2,1,0:T(8,128)S(1)}, u32[]{:S(2)}, u32[]{:S(2)}) async-start(f32[8,32,128]{2,1,0:T(8,128)} %pack.1), calls=%async_computation | async-start | bytes 262144 | tf_op jit(solution)/shard_map/all_to_all | solution.py:489
  17.0 5.3 %all-to-all-done.own = f32[8,32,128]{2,1,0:T(8,128)S(1)} async-done(((f32[8,32,128]{2,1,0:T(8,128)}), f32[8,32,128]{2,1,0:T(8,128)S(1)}, u32[]{:S(2)}, u32[]{:S(2)}) %all-to-all-start) | async-done | bytes 131104 | tf_op jit(solution)/shard_map/all_to_all | solution.py:489
  22.2 0.0 copy-start
  22.3 1.9 %collective-permute-start = (f32[4,32,128]{2,1,0:T(8,128)S(1)}, f32[4,32,128]{2,1,0:T(8,128)S(1)}, u32[]{:S(2)}, u32[]{:S(2)}) collective-permute-start(f32[4,32,128]{2,1,0:T(8,128)S(1)} %slice_select_fusion), channel_id=1, source_target_pairs={{0,8},{1,9},{2,10},{3,11},{5,125},{6,126},{7,127},{8,16},{9,17},{1... | collective-permute-start | bytes 196616 | tf_op jit(solution)/shard_map/ppermute | solution.py:491
  24.2 6.7 %collective-permute-done.cross = f32[4,32,128]{2,1,0:T(8,128)S(1)} collective-permute-done((f32[4,32,128]{2,1,0:T(8,128)S(1)}, f32[4,32,128]{2,1,0:T(8,128)S(1)}, u32[]{:S(2)}, u32[]{:S(2)}) %collective-permute-start) | collective-permute-done | bytes 65568 | tf_op jit(solution)/shard_map/ppermute | solution.py:491
  30.8 0.0 copy-done
  30.8 0.0 copy-start.1
  30.9 0.6 copy-done.1
  31.5 9.3 %forward.1 = (bf16[16,72,128]{2,1,0:T(8,128)(2,1)}, f32[16,16,128]{2,1,0:T(8,128)}, bf16[16,256,256]{2,1,0:T(8,128)(2,1)}, f32[16,256,128]{2,1,0:T(8,128)}) custom-call(s32[64]{0:T(128)} %concatenate.6.ints, f32[8,32,128]{2,1,0:T(8,128)} %copy-done, f32[4,32,128]{2,1,0:T(8,128)} %copy-done.1, bf16[4,32,32]{2,1,0:T(8,128)(2,1)} %target.1, ...), custom_call_target="tpu_custom_call" | custom-call | tf_op jit(solution)/shard_map/forward/pallas_call | solution.py:493
  40.8 30.9 %all_to_all.15.got = bf16[16,72,128]{2,1,0:T(8,128)(2,1)} all-to-all(bf16[16,72,128]{2,1,0:T(8,128)(2,1)} %get-tuple-element.13), channel_id=1, replica_groups=mesh['img'=4,'zq'=4,'zr'=4,'yc'=8] {'img','zq'}, dimensions={0} | all-to-all | bytes 589824 | tf_op jit(solution)/shard_map/all_to_all | solution.py:505
  71.7 2.1 %error.1 = (f32[4,32,128]{2,1,0:T(8,128)}, f32[4,32,128]{2,1,0:T(8,128)}, bf16[4,32,32]{2,1,0:T(8,128)(2,1)}) custom-call(s32[64]{0:T(128)} %concatenate.6.ints, bf16[16,72,128]{2,1,0:T(8,128)(2,1)} %all_to_all.15.got, f32[4,32,128]{2,1,0:T(8,128)} %constant.51.clone.vert, bf16[4,128,32]{2,1,0:T(8,128)(2,1)} %constant.50.clone.placet), custom_call_target="tpu_custom_call" | custom-call | tf_op jit(solution)/shard_map/error/pallas_call | solution.py:507
  73.9 6.2 %collective-permute-start.2 = (f32[4,32,128]{2,1,0:T(8,128)}, f32[4,32,128]{2,1,0:T(8,128)S(1)}, u32[]{:S(2)}, u32[]{:S(2)}) collective-permute-start(f32[4,32,128]{2,1,0:T(8,128)} %get-tuple-element.15.up), channel_id=1, source_target_pairs={{127,0},{1,2},{3,4},{5,6},{7,8},{9,10},{11,12},{13,14},{15,16},{17... | collective-permute-start | bytes 196616 | tf_op jit(solution)/shard_map/ppermute | solution.py:517
  80.1 2.1 %collective-permute-start.1 = (f32[4,32,128]{2,1,0:T(8,128)}, f32[4,32,128]{2,1,0:T(8,128)S(1)}, u32[]{:S(2)}, u32[]{:S(2)}) collective-permute-start(f32[4,32,128]{2,1,0:T(8,128)} %get-tuple-element.15.up), channel_id=1, source_target_pairs={{0,1},{1,0},{2,3},{3,2},{4,5},{5,4},{6,7},{7,6},{8,9},{9,8},{10,11... | collective-permute-start | bytes 196616 | tf_op jit(solution)/shard_map/ppermute | solution.py:518
  82.1 0.1 collective-permute-done.2.got_other
  82.2 0.0 copy-start.2
  82.2 1.2 collective-permute-done.1.got_mate
  83.4 0.0 copy-start.3
  83.4 0.0 copy-done.2
  83.4 0.6 copy-done.3
  84.0 9.8 %backward.1 = (bf16[4,32,32]{2,1,0:T(8,128)(2,1)}, bf16[8,32,128]{2,1,0:T(8,128)(2,1)}, bf16[4,32,128]{2,1,0:T(8,128)(2,1)}) custom-call(s32[64]{0:T(128)} %concatenate.6.ints, f32[4,32,128]{2,1,0:T(8,128)} %get-tuple-element.15.up, f32[4,32,128]{2,1,0:T(8,128)} %copy-done.3, f32[4,32,128]{2,1,0:T(8,128)} %copy-done.2, ...), custom_call_target="tpu_custom_call" | custom-call | tf_op jit(solution)/shard_map/backward/pallas_call | solution.py:520
  93.9 1.9 %collective-permute-start.3 = (bf16[4,32,128]{2,1,0:T(8,128)(2,1)}, bf16[4,32,128]{2,1,0:T(8,128)(2,1)S(1)}, u32[]{:S(2)}, u32[]{:S(2)}) collective-permute-start(bf16[4,32,128]{2,1,0:T(8,128)(2,1)} %get-tuple-element.22), channel_id=1, source_target_pairs={{8,0},{9,1},{10,2},{11,3},{125,5},{126,6},{127,7},{16,8},{17,9},{1... | collective-permute-start | bytes 98312 | tf_op jit(solution)/shard_map/ppermute | solution.py:540
  95.8 3.2 %collective-permute-done.3 = bf16[4,32,128]{2,1,0:T(8,128)(2,1)S(1)} collective-permute-done((bf16[4,32,128]{2,1,0:T(8,128)(2,1)}, bf16[4,32,128]{2,1,0:T(8,128)(2,1)S(1)}, u32[]{:S(2)}, u32[]{:S(2)}) %collective-permute-start.3) | collective-permute-done | bytes 32800 | tf_op jit(solution)/shard_map/ppermute | solution.py:540
  99.0 0.9 maximum_select_fusion
  100.0 17.2 %all_to_all.16.got = bf16[32,32,128]{2,1,0:T(8,128)(2,1)} all-to-all(bf16[32,32,128]{2,1,0:T(8,128)(2,1)S(1)} %bitcast.11), channel_id=1, replica_groups=mesh['img'=4,'zq'=4,'zr'=4,'yc'=8] {'img','yc'}, dimensions={0} | all-to-all | bytes 524288 | tf_op jit(solution)/shard_map/all_to_all | solution.py:545
  117.1 2.8 %collect.1 = f32[96,10,128]{2,1,0:T(8,128)} custom-call(bf16[32,32,128]{2,1,0:T(8,128)(2,1)} %all_to_all.16.got), custom_call_target="tpu_custom_call" | custom-call | tf_op jit(solution)/shard_map/collect/pallas_call | solution.py:546
  119.9 2.1 %copy.25 = f32[96,10,128]{2,0,1:T(8,128)} copy(f32[96,10,128]{2,1,0:T(8,128)} %collect.1) | data formatting | bytes 983040
  (3 shorter events, 0.1 us)
Async XLA Ops:
  6.9 15.4 %all-to-all-start = ((f32[8,32,128]{2,1,0:T(8,128)}), f32[8,32,128]{2,1,0:T(8,128)S(1)}, u32[]{:S(2)}, u32[]{:S(2)}) async-start(f32[8,32,128]{2,1,0:T(8,128)} %pack.1), calls=%async_computation | async-start | bytes 262144 | tf_op jit(solution)/shard_map/all_to_all | solution.py:489
  22.2 8.6 %copy-start = (f32[8,32,128]{2,1,0:T(8,128)}, f32[8,32,128]{2,1,0:T(8,128)S(1)}, u32[]{:S(2)}) copy-start(f32[8,32,128]{2,1,0:T(8,128)S(1)} %all-to-all-done.own) | copy-start | bytes 393220
  22.3 8.6 %collective-permute-start = (f32[4,32,128]{2,1,0:T(8,128)S(1)}, f32[4,32,128]{2,1,0:T(8,128)S(1)}, u32[]{:S(2)}, u32[]{:S(2)}) collective-permute-start(f32[4,32,128]{2,1,0:T(8,128)S(1)} %slice_select_fusion), channel_id=1, source_target_pairs={{0,8},{1,9},{2,10},{3,11},{5,125},{6,126},{7,127},{8,16},{9,17},{1... | collective-permute-start | bytes 196616 | tf_op jit(solution)/shard_map/ppermute | solution.py:491
  30.8 0.6 copy-start.1
  73.9 8.3 %collective-permute-start.2 = (f32[4,32,128]{2,1,0:T(8,128)}, f32[4,32,128]{2,1,0:T(8,128)S(1)}, u32[]{:S(2)}, u32[]{:S(2)}) collective-permute-start(f32[4,32,128]{2,1,0:T(8,128)} %get-tuple-element.15.up), channel_id=1, source_target_pairs={{127,0},{1,2},{3,4},{5,6},{7,8},{9,10},{11,12},{13,14},{15,16},{17... | collective-permute-start | bytes 196616 | tf_op jit(solution)/shard_map/ppermute | solution.py:517
  80.1 3.4 %collective-permute-start.1 = (f32[4,32,128]{2,1,0:T(8,128)}, f32[4,32,128]{2,1,0:T(8,128)S(1)}, u32[]{:S(2)}, u32[]{:S(2)}) collective-permute-start(f32[4,32,128]{2,1,0:T(8,128)} %get-tuple-element.15.up), channel_id=1, source_target_pairs={{0,1},{1,0},{2,3},{3,2},{4,5},{5,4},{6,7},{7,6},{8,9},{9,8},{10,11... | collective-permute-start | bytes 196616 | tf_op jit(solution)/shard_map/ppermute | solution.py:518
  82.2 1.2 copy-start.2
  83.4 0.6 copy-start.3
  93.9 5.1 %collective-permute-start.3 = (bf16[4,32,128]{2,1,0:T(8,128)(2,1)}, bf16[4,32,128]{2,1,0:T(8,128)(2,1)S(1)}, u32[]{:S(2)}, u32[]{:S(2)}) collective-permute-start(bf16[4,32,128]{2,1,0:T(8,128)(2,1)} %get-tuple-element.22), channel_id=1, source_target_pairs={{8,0},{9,1},{10,2},{11,3},{125,5},{126,6},{127,7},{16,8},{17,9},{1... | collective-permute-start | bytes 98312 | tf_op jit(solution)/shard_map/ppermute | solution.py:540

commit v2 on v1

--- a/solution.py
+++ b/solution.py
@@ -14,6 +14,7 @@
 BLOCK = 128
 CH = 4
 SLOTS = 16
+PAIRS = SLOTS // 2
 NEAR = 8
 CAP = 3
 RADIUS = 5
@@ -38,8 +39,6 @@
 highest = lax.Precision.HIGHEST
 GS = ("zq", "zr", "yc")
 
-REQ, CNT, REN, LST, TCN, YC, IMG, ZQ, MID = 0, 24, 32, 36, 52, 56, 57, 58, 59
-
 
 def constants():
     lane = np.arange(128)
@@ -52,10 +51,10 @@
         mom[:, part * 8 : part * 8 + 6] = moments
     momt = np.zeros((16, PIX))
     momt[:6] = moments.T
-    before = (np.arange(128)[:, None] < np.arange(128)[None, :]).astype(float)
-    ones = np.ones((128, 128))
-    tri = np.tile(np.concatenate([before, ones], axis=1), (2, 1))
-    trib = np.tile(np.concatenate([before.T, ones], axis=1), (2, 1))
+    long = (np.arange(256)[:, None] < np.arange(256)[None, :]).astype(float)
+    alone = long * (np.arange(256)[:, None] // 128 == np.arange(256)[None, :] // 128)
+    tri = np.stack([alone, long])
+    trib = np.stack([alone.T, long.T])
     spread = (pix[:, None] % 16 == lane[None, :] % 16).astype(float)
     place = np.zeros((CH, SIDE, 128))
     for c in range(CH):
@@ -124,33 +123,33 @@
     return lax.broadcasted_iota(jnp.int32, shape, dim)
 
 
-def source_places(ints):
+def source_places(counts, lists, yc):
     ends = []
     total = 0
     for o in range(NEAR):
-        total = total + ints[CNT + o]
+        total = total + counts[o]
         ends.append(total)
     places = []
     for e in range(SLOTS):
-        s = ints[LST + e]
+        s = lists[e]
         group = 0
         start = 0
         for o in range(NEAR):
             past = s >= ends[o]
             group = group + jnp.where(past, 1, 0)
-            start = start + jnp.where(past, ints[CNT + o], 0)
-        apart = ints[YC] + group - NEAR // 2
+            start = start + jnp.where(past, counts[o], 0)
+        apart = yc + group - NEAR // 2
         near = jnp.bitwise_and(apart, 7)
         chunk = jnp.where(apart == near, near, 8 + jnp.bitwise_and(near, 3))
         places.append(chunk * CAP + s - start)
     return places
 
 
-def list_slots(ints):
+def list_slots(tile_counts):
     ends = []
     total = 0
     for t in range(TILES - 1):
-        total = total + ints[TCN + t]
+        total = total + tile_counts[t]
         ends.append(total)
     slots = []
     for e in range(SLOTS):
@@ -161,32 +160,41 @@
     return slots
 
 
-def pack_kernel(ints, gauss, out):
+def pack_kernel(request, gauss, out):
+    yc = lax.axis_index("yc")
     lane = iota((1, 128), 1) % 32
     for chunk in range(N_YC):
-        group = jnp.bitwise_and(ints[YC] + NEAR // 2 - chunk, 7)
+        group = jnp.bitwise_and(yc + NEAR // 2 - chunk, 7)
         ids = []
         for c in range(CAP):
-            idx = ints[REQ + group * CAP + c]
-            out[chunk, 10 * c : 10 * c + 10, :] = gauss[idx]
+            idx = request[c, 0, group]
+            for v in range(VALS):
+                out[chunk, 10 * c + v : 10 * c + v + 1, :] = gauss[v, pl.ds(idx, 1), :]
             ids.append(idx)
         row = jnp.where(lane < 10, ids[0], jnp.where(lane < 20, ids[1], ids[2]))
         out[chunk, 30:32, :] = jnp.broadcast_to(row.astype(f32), (2, 128))
 
 
-def forward_kernel(ints, own, cross, target, mom, tri, spread, place, payload, raws, pair_w, beta_o,
-                   blk, vals, coefs, cols):
+def forward_kernel(counts, lists, tile_counts, render, own, cross, target, mom, tri, spread, place,
+                   payload, raws, pair_o, beta_o, blk, vals, coefs, shades, cols, pair_w, beta, sems):
     for m in range(12):
         for c in range(CAP):
             src = own[m, 10 * c : 10 * c + 10, :] if m < 8 else cross[m - 8, 10 * c : 10 * c + 10, :]
             blk[m * CAP + c, 0:10, :] = src
-    places = source_places(ints)
-    slots = list_slots(ints)
+    places = source_places(counts, lists, lax.axis_index("yc"))
+    slots = list_slots(tile_counts)
+    shades[...] = jnp.zeros_like(shades)
     for e in range(SLOTS):
         raw = blk[places[e]]
         raws[e] = raw
         for v in range(6):
             vals[v, e : e + 1, :] = raw[v : v + 1, :]
+        shade = raw[6:10, :]
+        high = shade.astype(bf16).astype(f32)
+        at = 4 * (e % 2)
+        lanes = slice(128 * (e % 2), 128 * (e % 2) + 128)
+        shades[e // 2, at : at + 4, lanes] = high
+        shades[e // 2, 8 + at : 12 + at, lanes] = shade - high
     mx = vals[0] - 8.0
     my = vals[1] - 8.0
     ca = vals[2]
@@ -210,30 +218,37 @@
         rest = table[k] - high
         mid = rest.astype(bf16).astype(f32)
         for e in range(SLOTS):
-            coefs[e, k : k + 1, :] = high[e : e + 1, :]
-            coefs[e, 8 + k : 9 + k, :] = mid[e : e + 1, :]
-            coefs[e, 16 + k : 17 + k, :] = (rest - mid)[e : e + 1, :]
+            lanes = slice(128 * (e % 2), 128 * (e % 2) + 128)
+            coefs[e // 2, k : k + 1, lanes] = high[e : e + 1, :]
+            coefs[e // 2, 8 + k : 9 + k, lanes] = mid[e : e + 1, :]
+            coefs[e // 2, 16 + k : 17 + k, lanes] = (rest - mid)[e : e + 1, :]
     cols[...] = jnp.zeros_like(cols)
+    upper = iota((8, PIX), 0) < 4
     carry = jnp.zeros((PIX, 128), f32)
-    for e in range(SLOTS):
-        power = dot(mom[...], coefs[e].astype(bf16))
-        alpha = jnp.exp2(power)
-        lost = alpha * (
-            -log2e + alpha * (-log2e / 2 + alpha * (-log2e / 3 + alpha * (-log2e / 4 + alpha * (-log2e / 5))))
-        )
-        sums = dot(jnp.concatenate(halves(lost), axis=1), tri[...])
-        if e:
-            carry = jnp.where(slots[e] == slots[e - 1], carry, 0.0)
-        weight = jnp.exp2(sums[:, :128] + carry) * alpha
-        carry = carry + sums[:, 128:]
-        beta_o[e] = alpha * (1.0 + alpha * (1.0 + alpha * (1.0 + alpha * (1.0 + alpha))))
-        both = jnp.concatenate(halves(weight), axis=1)
-        pair_w[e] = both
-        shade_high, shade_low = halves(raws[e, 6:10, :])
-        upper = jnp.concatenate([shade_high, shade_high], axis=1)
-        lower = jnp.concatenate([shade_low, jnp.zeros_like(shade_low)], axis=1)
-        cols[slots[e]] += dot(jnp.concatenate([upper.astype(f32), lower.astype(f32)], axis=0).astype(bf16), both,
-                              ((1,), (1,)))
+    for pair in range(PAIRS):
+        first, second = 2 * pair, 2 * pair + 1
+        same = slots[first] == slots[second]
+        alpha = jnp.exp2(dot(mom[...], coefs[pair].astype(bf16)))
+        lost = alpha * (-1.0 + alpha * (-1.0 / 2 + alpha * (-1.0 / 3 + alpha * (-1.0 / 4))))
+        beta[pair] = (alpha * jnp.exp(-lost)).astype(bf16)
+        sums = dot(lost.astype(bf16), tri[jnp.where(same, 1, 0)])
+        whole = jnp.broadcast_to(sums[:, 255:256] + lost[:, 255:256], (PIX, 128))
+        if pair:
+            carry = jnp.where(slots[first] == slots[first - 1], carry, 0.0)
+        later = jnp.where(same, carry, 0.0)
+        weight = (jnp.exp(sums + jnp.concatenate([carry, later], axis=1)) * alpha).astype(bf16)
+        carry = whole + later
+        pair_w[pair] = weight
+        colour = dot(shades[pair].astype(bf16), weight, ((1,), (1,)))
+        colour = colour[0:8, :] + colour[8:16, :]
+        cols[slots[first]] += jnp.where(upper, colour, 0.0)
+        cols[slots[second]] += jnp.where(upper, 0.0, colour)
+    copies = (
+        pltpu.make_async_copy(pair_w, pair_o, sems.at[0]),
+        pltpu.make_async_copy(beta, beta_o, sems.at[1]),
+    )
+    for copy in copies:
+        copy.start()
     row_of = iota((TILE, PIX), 1) // TILE == iota((TILE, PIX), 0)
     lane = iota((TILE, 128), 1)
     pieces = []
@@ -259,14 +274,16 @@
     row = iota((8, 128), 0)
     tags = jnp.zeros((8, 128), jnp.int32)
     for s in range(TILES):
-        tags = jnp.where(row == s, jnp.bitwise_and(ints[REN + s], 3), tags)
+        tags = jnp.where(row == s, jnp.bitwise_and(render[s], 3), tags)
     tags = tags.astype(f32).astype(bf16)
     for q in range(N_IMG * N_ZQ):
         payload[q, 0:64, :] = body
         payload[q, 64:72, :] = tags
-
-
-def error_kernel(ints, got, vert, placet, up, err_own, rendered, errs, images):
+    for copy in copies:
+        copy.wait()
+
+
+def error_kernel(got, vert, placet, up, err_own, rendered, errs, images):
     lane = iota((TILE, 128), 1)
     half = lane // 64
     halff = half.astype(f32)
@@ -285,21 +302,29 @@
             images[strip * 4 + home] = image
             goal = got[strip * 4 + home, 32:64, :].astype(f32)
             errs[strip * 32 : strip * 32 + 32, home * 128 : home * 128 + 128] = image - goal
-    img = ints[IMG]
+    img = lax.axis_index("img")
     blurred = dot(vert[img], errs[...], precision=highest)
     for home in range(N_ZQ):
         up[home] = blurred[:, home * 128 : home * 128 + 128]
         err_own[home] = errs[pl.ds(pl.multiple_of(img * 32, 32), 32), home * 128 : home * 128 + 128]
-    mine = images[img * 4 + ints[ZQ]].astype(bf16)
+    mine = images[img * 4 + lax.axis_index("zq")].astype(bf16)
     for c in range(CH):
         rendered[c] = dot(mine, placet[c]).astype(bf16)
 
 
-def backward_kernel(ints, up, got_mate, got_other, err_own, horiz, placet, spreadt, momt, trib, raws, pair_w,
-                    beta_i, own, cross, grad_out, msg_own, msg_cross,
-                    ext, back, grads, grow, gcol, vals, sums, blk, pack):
-    parity = jnp.bitwise_and(ints[YC], 1)
-    place_mid = ints[MID]
+def backward_kernel(counts, lists, tile_counts, render, up, got_mate, got_other, err_own, horiz, placet, spreadt,
+                    momt, trib, raws, pair_o, beta_o, own, cross, grad_out, msg_own, msg_cross,
+                    ext, back, grads, vals, sums, blk, pack, shades, shade_sums, pair_w, beta, sems):
+    copies = (
+        pltpu.make_async_copy(pair_o, pair_w, sems.at[0]),
+        pltpu.make_async_copy(beta_o, beta, sems.at[1]),
+    )
+    for copy in copies:
+        copy.start()
+    yc = lax.axis_index("yc")
+    zq = lax.axis_index("zq")
+    parity = jnp.bitwise_and(yc, 1)
+    place_mid = lax.axis_index("zr") * N_YC + yc
     lane32 = iota((SIDE, 128), 1)
     for home in range(N_ZQ):
         at_left = home - jnp.where(place_mid == 0, 1, 0)
@@ -330,15 +355,15 @@
             (1.0 - lam_weight) * err_own[home] + lam_weight * back[home * 32 : home * 32 + 32, :]
         )
         grads[home] = total.astype(bf16).astype(f32)
-    mine = grads[ints[ZQ]].astype(bf16)
+    mine = grads[zq].astype(bf16)
     for c in range(CH):
         grad_out[c] = dot(mine, placet[c]).astype(bf16)
 
     lane = iota((TILE, 128), 1)
     pieces = []
     for s in range(TILES):
-        home = jnp.bitwise_and(ints[ZQ] + s, 3)
-        local = jnp.bitwise_and(ints[REN + s], 3)
+        home = jnp.bitwise_and(zq + s, 3)
+        local = jnp.bitwise_and(render[s], 3)
         down = local // 2
         across = jnp.bitwise_and(local, 1)
         tile = grads[home, pl.ds(pl.multiple_of(down * 16, 16), 16), :]
@@ -346,43 +371,53 @@
             pieces.append(jnp.where(lane // 16 == across * 4 + c, tile, 0.0))
     laid = dot(jnp.concatenate(pieces, axis=0).astype(bf16), spreadt[...])
     row_of = iota((TILE, PIX), 1) // TILE == iota((TILE, PIX), 0)
+    lines = []
     for s in range(TILES):
-        lines = []
+        four = []
         for c in range(CH):
             at = s * 64 + c * 16
-            lines.append(jnp.sum(jnp.where(row_of, laid[at : at + 16, :], 0.0), axis=0, keepdims=True))
-        four = jnp.concatenate(lines, axis=0)
-        sixteen = jnp.concatenate([four, four, four, jnp.zeros_like(four)], axis=0)
-        grow[s] = sixteen.astype(bf16)
-        gcol[s] = jnp.transpose(sixteen).astype(bf16)
-
-    slots = list_slots(ints)
-    places = source_places(ints)
-    carry = jnp.zeros((PIX, 128), f32)
-    for e in reversed(range(SLOTS)):
-        both = pair_w[e]
-        weight = both[:, :128].astype(f32) + both[:, 128:].astype(f32)
+            four.append(jnp.sum(jnp.where(row_of, laid[at : at + 16, :], 0.0), axis=0, keepdims=True))
+        lines = lines + four + four
+    grad_rows = jnp.concatenate(lines, axis=0)
+    grad_cols = jnp.transpose(grad_rows).astype(bf16)
+    grad_rows = grad_rows.astype(bf16)
+
+    slots = list_slots(tile_counts)
+    places = source_places(counts, lists, yc)
+    shades[...] = jnp.zeros_like(shades)
+    for e in range(SLOTS):
         shade = raws[e, 6:10, :]
         high = shade.astype(bf16).astype(f32)
-        rest = shade - high
-        mid = rest.astype(bf16).astype(f32)
-        shades = jnp.concatenate([high, mid, rest - mid, jnp.zeros_like(high)], axis=0).astype(bf16)
-        shade_dot = dot(gcol[slots[e]], shades)
-        product = weight * shade_dot
-        after = dot(jnp.concatenate(halves(product), axis=1), trib[...])
-        if e < SLOTS - 1:
-            carry = jnp.where(slots[e] == slots[e + 1], carry, 0.0)
-        unit = product - (after[:, :128] + carry) * beta_i[e]
-        carry = carry + after[:, 128:]
-        moment = dot(momt[...], jnp.concatenate(halves(unit), axis=1))
-        moment = moment[:, :128] + moment[:, 128:]
-        shade_grad = dot(grow[slots[e]], both)
-        shade_grad = shade_grad[:, :128] + shade_grad[:, 128:]
+        at = pl.ds(pl.multiple_of(slots[e] * 8, 8), 8)
+        shades[e // 2, at, 128 * (e % 2) : 128 * (e % 2) + 128] = jnp.concatenate([high, shade - high], axis=0)
         for k in range(6):
             vals[k, e : e + 1, :] = raws[e, k : k + 1, :]
-            sums[k, e : e + 1, :] = moment[k : k + 1, :]
+    for copy in copies:
+        copy.wait()
+    carry = jnp.zeros((PIX, 128), f32)
+    for pair in reversed(range(PAIRS)):
+        first, second = 2 * pair, 2 * pair + 1
+        same = slots[first] == slots[second]
+        product = pair_w[pair].astype(f32) * dot(grad_cols, shades[pair].astype(bf16))
+        after = dot(product.astype(bf16), trib[jnp.where(same, 1, 0)])
+        whole = jnp.broadcast_to(after[:, 0:1] + product[:, 0:1], (PIX, 128))
+        if pair < PAIRS - 1:
+            carry = jnp.where(slots[second] == slots[second + 1], carry, 0.0)
+        earlier = jnp.where(same, carry, 0.0)
+        unit = product - (after + jnp.concatenate([earlier, carry], axis=1)) * beta[pair].astype(f32)
+        carry = whole + earlier
+        high, low = halves(unit)
+        moment = dot(momt[...], high) + dot(momt[...], low)
+        shade_grad = dot(grad_rows, pair_w[pair])
+        for s in range(TILES):
+            shade_sums[pair, s] = shade_grad[8 * s : 8 * s + 8, :]
+        for k in range(6):
+            sums[k, first : first + 1, :] = moment[k : k + 1, :128]
+            sums[k, second : second + 1, :] = moment[k : k + 1, 128:]
+    for e in range(SLOTS):
+        shade_grad = shade_sums[e // 2, slots[e]]
         for c in range(CH):
-            sums[6 + c, e : e + 1, :] = shade_grad[c : c + 1, :]
+            sums[6 + c, e : e + 1, :] = shade_grad[c : c + 1, 128 * (e % 2) : 128 * (e % 2) + 128]
     mx = vals[0] - 8.0
     my = vals[1] - 8.0
     ca = vals[2]
@@ -415,7 +450,7 @@
         for v in range(VALS):
             blk[places[e], v : v + 1, :] = out[v][e : e + 1, :]
     lane1 = iota((2, 128), 1)
-    group = jnp.where(lane1 // 32 == jnp.bitwise_and(ints[YC], 3), 1.0, 0.0)
+    group = jnp.where(lane1 // 32 == jnp.bitwise_and(yc, 3), 1.0, 0.0)
     for m in range(12):
         for c in range(CAP):
             pack[m, 10 * c : 10 * c + 10, :] = blk[m * CAP + c, 0:10, :]
@@ -434,27 +469,30 @@
         ids = jnp.zeros((1, 128), f32)
         for m in range(4):
             ids = ids + got[quad * 4 + m, 16:32, :].astype(f32)[14:15, :]
-        goals.append(jnp.where(line < 30, ids.astype(jnp.int32) * 16 + value, -1))
+        goals.append(jnp.where(line < 30, ids.astype(jnp.int32) + value * BLK_DEV, -1))
     flat = got[...].reshape(32 * MSG, 128)
-    rows = 384
-    for part in range(BLK_DEV * 16 // rows):
+    rows = 2 * BLK_DEV
+    for part in range(VALS // 2):
         here = iota((rows, 128), 0) + part * rows
         hits = [jnp.where(here == goal, 1.0, 0.0).astype(bf16) for goal in goals]
         total = dot(jnp.concatenate(hits, axis=1), flat)
-        out[part * 24 : part * 24 + 24] = total.reshape(24, 16, 128)[:, :VALS, :]
+        out[2 * part] = total[:BLK_DEV]
+        out[2 * part + 1] = total[BLK_DEV:]
 
 
 VM = pl.BlockSpec(memory_space=pltpu.VMEM)
 SM = pl.BlockSpec(memory_space=pltpu.SMEM)
-
-
-def call(kernel, outs, scratch, n_in, name, flops=0):
+ANY = pl.BlockSpec(memory_space=pl.ANY)
+
+
+def call(kernel, ins, outs, scratch, name, limit=16):
     return pl.pallas_call(
         kernel,
-        out_shape=tuple(jax.ShapeDtypeStruct(shape, dtype) for shape, dtype in outs),
-        in_specs=[SM] + [VM] * (n_in - 1) if name != "collect" else [VM] * n_in,
-        out_specs=tuple(VM for _ in outs),
-        scratch_shapes=[pltpu.VMEM(shape, dtype) for shape, dtype in scratch],
+        out_shape=tuple(jax.ShapeDtypeStruct(shape, dtype) for shape, dtype, _ in outs),
+        in_specs=ins,
+        out_specs=tuple(space for _, _, space in outs),
+        scratch_shapes=scratch,
+        compiler_params=pltpu.CompilerParams(vmem_limit_bytes=limit << 20 if limit else None),
         name=name,
     )
 
@@ -462,19 +500,11 @@
 def on_device(gaussians, target, request, near_counts, render_tile, tile_lists, tile_counts):
     table = constants()
     yc = lax.axis_index("yc")
-    img = lax.axis_index("img")
-    zq = lax.axis_index("zq")
-    mid = lax.axis_index("zr") * N_YC + yc
-    ints = jnp.concatenate(
-        [
-            request.reshape(24),
-            near_counts.reshape(8),
-            render_tile.reshape(4),
-            tile_lists.reshape(16),
-            tile_counts.reshape(4),
-            jnp.stack([yc, img, zq, mid, yc, yc, yc, yc]).astype(jnp.int32),
-        ]
-    )
+    counts = near_counts.reshape(NEAR)
+    render = render_tile.reshape(TILES)
+    lists = tile_lists.reshape(SLOTS)
+    lengths = tile_counts.reshape(TILES)
+    wanted = request.transpose(0, 3, 1, 2).reshape(CAP, 1, NEAR)
     n_gs = N_ZQ * N_ZR * N_YC
     up_route = []
     for r in range(n_gs):
@@ -484,33 +514,50 @@
         elif j > 4:
             up_route.append((r, (r - N_YC) % n_gs))
     back_route = [(b, a) for a, b in up_route]
-
-    (sent,) = call(pack_kernel, [((N_YC, MSG, 128), f32)], [], 2, "pack")(ints, gaussians)
+    group = N_IMG * N_ZQ
+    vm = pltpu.VMEM
+
+    (sent,) = call(pack_kernel, [SM, VM], [((N_YC, MSG, 128), f32, VM)], [], "pack", None)(
+        wanted, gaussians.transpose(1, 0, 2)
+    )
     own = lax.all_to_all(sent, "yc", 0, 0, tiled=True)
     crossing = jnp.where(yc < 4, own[4:8], own[0:4])
     cross = lax.ppermute(crossing, GS, up_route)
 
     payload, raws, pair_w, beta = call(
         forward_kernel,
+        [SM] * 4 + [VM] * 7,
         [
-            ((N_IMG * N_ZQ, 72, 128), bf16),
-            ((SLOTS, 16, 128), f32),
-            ((SLOTS, PIX, 256), bf16),
-            ((SLOTS, PIX, 128), f32),
+            ((group, 72, 128), bf16, VM),
+            ((SLOTS, 16, 128), f32, VM),
+            ((PAIRS, PIX, 256), bf16, ANY),
+            ((PAIRS, PIX, 256), bf16, ANY),
         ],
-        [((36, 16, 128), f32), ((6, 16, 128), f32), ((SLOTS, 32, 128), f32), ((TILES, 8, PIX), f32)],
-        8,
+        [
+            vm((36, 16, 128), f32),
+            vm((6, 16, 128), f32),
+            vm((PAIRS, 32, 256), f32),
+            vm((PAIRS, 16, 256), f32),
+            vm((TILES, 8, PIX), f32),
+            vm((PAIRS, PIX, 256), bf16),
+            vm((PAIRS, PIX, 256), bf16),
+            pltpu.SemaphoreType.DMA((2,)),
+        ],
         "forward",
-    )(ints, own, cross, target, table["mom"], table["tri"], table["spread"], table["place"])
+        None,
+    )(
+        counts, lists, lengths, render, own, cross, target, table["mom"], table["tri"], table["spread"],
+        table["place"],
+    )
     got = lax.all_to_all(payload, ("img", "zq"), 0, 0, tiled=True)
 
     up, err_own, rendered = call(
         error_kernel,
-        [((N_ZQ, SIDE, 128), f32), ((N_ZQ, SIDE, 128), f32), ((CH, SIDE, SIDE), bf16)],
-        [((N_IMG * SIDE, 512), f32), ((16, SIDE, 128), f32)],
-        4,
+        [VM] * 3,
+        [((N_ZQ, SIDE, 128), f32, VM), ((N_ZQ, SIDE, 128), f32, VM), ((CH, SIDE, SIDE), bf16, VM)],
+        [vm((N_IMG * SIDE, 512), f32), vm((16, SIDE, 128), f32)],
         "error",
-    )(ints, got, table["vert"], table["placet"])
+    )(got, table["vert"], table["placet"])
 
     other = [((2 * c - 1) % n_gs, 2 * c) for c in range(n_gs // 2)]
     other = other + [(b, a) for a, b in other]
@@ -519,23 +566,27 @@
 
     pixel_grad, msg_own, msg_cross = call(
         backward_kernel,
-        [((CH, SIDE, SIDE), bf16), ((N_YC, MSG, 128), bf16), ((4, MSG, 128), bf16)],
+        [SM] * 4 + [VM] * 10 + [ANY] * 2 + [VM] * 2,
+        [((CH, SIDE, SIDE), bf16, VM), ((N_YC, MSG, 128), bf16, VM), ((4, MSG, 128), bf16, VM)],
         [
-            ((128, 256), f32),
-            ((128, 128), f32),
-            ((N_ZQ, SIDE, 128), f32),
-            ((TILES, 16, PIX), bf16),
-            ((TILES, PIX, 16), bf16),
-            ((6, 16, 128), f32),
-            ((10, 16, 128), f32),
-            ((36, 16, 128), f32),
-            ((12, MSG, 128), f32),
+            vm((128, 256), f32),
+            vm((128, 128), f32),
+            vm((N_ZQ, SIDE, 128), f32),
+            vm((6, 16, 128), f32),
+            vm((10, 16, 128), f32),
+            vm((36, 16, 128), f32),
+            vm((12, MSG, 128), f32),
+            vm((PAIRS, 32, 256), f32),
+            vm((PAIRS, TILES, 8, 256), f32),
+            vm((PAIRS, PIX, 256), bf16),
+            vm((PAIRS, PIX, 256), bf16),
+            pltpu.SemaphoreType.DMA((2,)),
         ],
-        15,
         "backward",
+        None,
     )(
-        ints, up, got_mate, got_other, err_own, table["horiz"], table["placet"], table["spreadt"], table["momt"],
-        table["trib"], raws, pair_w, beta, own, cross,
+        counts, lists, lengths, render, up, got_mate, got_other, err_own, table["horiz"], table["placet"],
+        table["spreadt"], table["momt"], table["trib"], raws, pair_w, beta, own, cross,
     )
     returned = lax.ppermute(msg_cross, GS, back_route)
     apart = jnp.arange(N_YC) + NEAR // 2 - yc
@@ -543,8 +594,8 @@
     merged = jnp.where(straight, msg_own, jnp.concatenate([returned, returned], axis=0))
     spread_out = jnp.broadcast_to(merged[None], (N_IMG, N_YC, MSG, 128)).reshape(N_IMG * N_YC, MSG, 128)
     all_msgs = lax.all_to_all(spread_out, ("img", "yc"), 0, 0, tiled=True)
-    (summed,) = call(collect_kernel, [((BLK_DEV, VALS, 128), f32)], [], 1, "collect")(all_msgs)
-    return (rendered, pixel_grad, summed)
+    (summed,) = call(collect_kernel, [VM], [((VALS, BLK_DEV, 128), f32, VM)], [], "collect")(all_msgs)
+    return (rendered, pixel_grad, summed.transpose(1, 0, 2))
 
 
 def solution(mesh):

time: 123 us -> 108 us (0.88)
  Pallas kernels: 25.9 us -> 17.6 us
  local copies, waits for them, and re-layouts: 7.74 us -> 1.93 us
    pallas_call x5, Pallas kernels: 25.9 us -> 17.6 us  [the longest x1 6.66 us: on_device(): call(backward_kernel, [SM] * 4 + [VM] * 10 + [ANY] * 2 + [VM] * 2, [((CH,...]
    unnamed x11 -> x16, local copies, waits for them, and re-layouts: 6.3 us -> 1.89 us
    concatenate x1 -> x0, local copies, waits for them, and re-layouts: 1.33 us -> none  [on_device(): jnp.concatenate([request.reshape(24), near_counts.reshape(8), render_tile...]
  transfers between devices with their start and end apart: 5 -> 5, of which waited for: 5 -> 4; matrix products, arithmetic and copies ran while one was open for 0% -> 0% of each run, Pallas kernels for 0% -> 0%
where the time goes in v2:
time: 108 us; the launch traced here: 107 us
  blocking collectives  47.8 us (44%)
  starting transfers between devices  22.2 us (21%)
  Pallas kernels  17.6 us (16%)
  waiting for transfers between devices  16.2 us (15%)
  local copies, waits for them, and re-layouts  1.93 us (2%)
    all_to_all x1, blocking collectives, on_device(): got = lax.all_to_all(payload, ('img', 'zq'), 0, 0, tiled=True)  31 us
    all_to_all x1, blocking collectives, on_device(): all_msgs = lax.all_to_all(spread_out, ('img', 'yc'), 0, 0, tiled=True)  16.8 us
    all_to_all x1, starting transfers between devices, on_device(): own = lax.all_to_all(sent, 'yc', 0, 0, tiled=True)  10.1 us
    ppermute x1, waiting for transfers between devices, on_device(): cross = lax.ppermute(crossing, GS, up_route)  6.66 us
    pallas_call x1, Pallas kernels, on_device(): call(backward_kernel, [SM] * 4 + [VM] * 10 + [ANY] * 2 + [VM] * 2, [((CH,...  6.66 us
    pallas_call x1, Pallas kernels, on_device(): call(forward_kernel, [SM] * 4 + [VM] * 7, [((group, 72, 128), bf16, VM),...  6.59 us
    ppermute x1, starting transfers between devices, on_device(): got_other = lax.ppermute(up, GS, other)  6.2 us
    all_to_all x1, waiting for transfers between devices, on_device(): own = lax.all_to_all(sent, 'yc', 0, 0, tiled=True)  5.27 us
  transfers between devices with their start and end apart: 5, of which 4 were waited for; matrix products, arithmetic and copies ran while one was open for 0% of the time, Pallas kernels for 0%

profile of v2, /device:TPU:1, one launch (start us, length us, event | category | flops | bytes accessed | tf_op | source)
XLA Modules:
  0.0 107.4 jit_solution(10345292770865956932)
XLA Ops:
  0.6 1.8 %pack.1 = f32[8,32,128]{2,1,0:T(8,128)} custom-call(s32[3,1,8]{2,1,0:T(1,128)} %bitcast.21, f32[10,96,128]{2,1,0:T(8,128)} %bitcast.11), custom_call_target="tpu_custom_call" | custom-call | tf_op jit(solution)/shard_map/pack/pallas_call | solution.py:520
  2.5 10.1 %all-to-all-start = ((f32[8,32,128]{2,1,0:T(8,128)}), f32[8,32,128]{2,1,0:T(8,128)S(1)}, u32[]{:S(2)}, u32[]{:S(2)}) async-start(f32[8,32,128]{2,1,0:T(8,128)} %pack.1), calls=%async_computation | async-start | bytes 262144 | tf_op jit(solution)/shard_map/all_to_all | solution.py:523
  12.6 5.3 %all-to-all-done.own = f32[8,32,128]{2,1,0:T(8,128)S(1)} async-done(((f32[8,32,128]{2,1,0:T(8,128)}), f32[8,32,128]{2,1,0:T(8,128)S(1)}, u32[]{:S(2)}, u32[]{:S(2)}) %all-to-all-start) | async-done | bytes 131104 | tf_op jit(solution)/shard_map/all_to_all | solution.py:523
  17.8 0.0 copy-start.4
  17.9 1.9 %collective-permute-start = (f32[4,32,128]{2,1,0:T(8,128)S(1)}, f32[4,32,128]{2,1,0:T(8,128)S(1)}, u32[]{:S(2)}, u32[]{:S(2)}) collective-permute-start(f32[4,32,128]{2,1,0:T(8,128)S(1)} %slice_select_fusion), channel_id=1, source_target_pairs={{0,8},{1,9},{2,10},{3,11},{5,125},{6,126},{7,127},{8,16},{9,17},{1... | collective-permute-start | bytes 196616 | tf_op jit(solution)/shard_map/ppermute | solution.py:525
  19.8 6.7 %collective-permute-done.cross = f32[4,32,128]{2,1,0:T(8,128)S(1)} collective-permute-done((f32[4,32,128]{2,1,0:T(8,128)S(1)}, f32[4,32,128]{2,1,0:T(8,128)S(1)}, u32[]{:S(2)}, u32[]{:S(2)}) %collective-permute-start) | collective-permute-done | bytes 65568 | tf_op jit(solution)/shard_map/ppermute | solution.py:525
  26.5 0.0 copy-start.5
  26.5 0.0 copy-done.4
  26.5 0.6 copy-done.5
  27.1 6.6 %forward.1 = (bf16[16,72,128]{2,1,0:T(8,128)(2,1)}, f32[16,16,128]{2,1,0:T(8,128)}, bf16[8,256,256]{2,1,0:T(8,128)(2,1)}, bf16[8,256,256]{2,1,0:T(8,128)(2,1)}) custom-call(s32[8]{0:T(128)} %bitcast.13, s32[16]{0:T(128)} %bitcast.15, s32[4]{0:T(128)} %bitcast.17, s32[4]{0:T(128)} %bitcast.19, f32[8,32,128]{2,1,0:T(8,128)} %copy-done.4, ...), custom_call_target="tpu_custom_call" | custom-call | tf_op jit(solution)/shard_map/forward/pallas_call | solution.py:527
  33.7 0.0 copy-start
  33.7 0.0 copy-start.1
  33.7 31.0 %all_to_all.15.got = bf16[16,72,128]{2,1,0:T(8,128)(2,1)S(1)} all-to-all(bf16[16,72,128]{2,1,0:T(8,128)(2,1)} %get-tuple-element.13), channel_id=1, replica_groups=mesh['img'=4,'zq'=4,'zr'=4,'yc'=8] {'img','zq'}, dimensions={0} | all-to-all | bytes 589824 | tf_op jit(solution)/shard_map/all_to_all | solution.py:552
  64.7 0.0 copy-done
  64.7 0.0 copy-done.1
  64.7 1.1 %error.1 = (f32[4,32,128]{2,1,0:T(8,128)S(1)}, f32[4,32,128]{2,1,0:T(8,128)S(1)}, bf16[4,32,32]{2,1,0:T(8,128)(2,1)}) custom-call(bf16[16,72,128]{2,1,0:T(8,128)(2,1)S(1)} %all_to_all.15.got, f32[4,32,128]{2,1,0:T(8,128)S(1)} %copy-done.1, bf16[4,128,32]{2,1,0:T(8,128)(2,1)S(1)} %copy-done), custom_call_target="tpu_custom_call" | custom-call | tf_op jit(solution)/shard_map/error/pallas_call | solution.py:554
  65.8 0.0 copy-start.3
  65.8 0.6 copy-done.3
  66.4 0.0 copy-start.2
  66.4 6.2 %collective-permute-start.2 = (f32[4,32,128]{2,1,0:T(8,128)S(1)}, f32[4,32,128]{2,1,0:T(8,128)S(1)}, u32[]{:S(2)}, u32[]{:S(2)}) collective-permute-start(f32[4,32,128]{2,1,0:T(8,128)S(1)} %get-tuple-element.15.up), channel_id=1, source_target_pairs={{127,0},{1,2},{3,4},{5,6},{7,8},{9,10},{11,12},{13,14},{15,16},{17... | collective-permute-start | bytes 196616 | tf_op jit(solution)/shard_map/ppermute | solution.py:564
  72.6 2.1 %collective-permute-start.1 = (f32[4,32,128]{2,1,0:T(8,128)S(1)}, f32[4,32,128]{2,1,0:T(8,128)S(1)}, u32[]{:S(2)}, u32[]{:S(2)}) collective-permute-start(f32[4,32,128]{2,1,0:T(8,128)S(1)} %get-tuple-element.15.up), channel_id=1, source_target_pairs={{0,1},{1,0},{2,3},{3,2},{4,5},{5,4},{6,7},{7,6},{8,9},{9,8},{10,11... | collective-permute-start | bytes 196616 | tf_op jit(solution)/shard_map/ppermute | solution.py:565
  74.7 0.0 collective-permute-done.2.got_other
  74.7 0.0 copy-start.6
  74.7 1.0 collective-permute-done.1.got_mate
  75.8 0.0 copy-start.7
  75.8 0.0 copy-done.2
  75.8 0.0 copy-done.6
  75.8 0.6 copy-done.7
  76.4 6.7 %backward.1 = (bf16[4,32,32]{2,1,0:T(8,128)(2,1)}, bf16[8,32,128]{2,1,0:T(8,128)(2,1)}, bf16[4,32,128]{2,1,0:T(8,128)(2,1)}) custom-call(s32[8]{0:T(128)} %bitcast.14, s32[16]{0:T(128)} %bitcast.16, s32[4]{0:T(128)} %bitcast.18, s32[4]{0:T(128)} %bitcast.20, f32[4,32,128]{2,1,0:T(8,128)} %copy-done.2, f32[4,32,128]{2,1,0:T(8,128)} %copy-done.7, ...), custom_call_target="tpu_custom_call" | custom-call | tf_op jit(solution)/shard_map/backward/pallas_call | solution.py:567
  83.0 1.9 %collective-permute-start.3 = (bf16[4,32,128]{2,1,0:T(8,128)(2,1)}, bf16[4,32,128]{2,1,0:T(8,128)(2,1)S(1)}, u32[]{:S(2)}, u32[]{:S(2)}) collective-permute-start(bf16[4,32,128]{2,1,0:T(8,128)(2,1)} %get-tuple-element.22), channel_id=1, source_target_pairs={{8,0},{9,1},{10,2},{11,3},{125,5},{126,6},{127,7},{16,8},{17,9},{1... | collective-permute-start | bytes 98312 | tf_op jit(solution)/shard_map/ppermute | solution.py:591
  85.0 3.2 %collective-permute-done.3 = bf16[4,32,128]{2,1,0:T(8,128)(2,1)S(1)} collective-permute-done((bf16[4,32,128]{2,1,0:T(8,128)(2,1)}, bf16[4,32,128]{2,1,0:T(8,128)(2,1)S(1)}, u32[]{:S(2)}, u32[]{:S(2)}) %collective-permute-start.3) | collective-permute-done | bytes 32800 | tf_op jit(solution)/shard_map/ppermute | solution.py:591
  88.2 0.9 maximum_select_fusion
  89.1 16.8 %all_to_all.16.got = bf16[32,32,128]{2,1,0:T(8,128)(2,1)S(1)} all-to-all(bf16[32,32,128]{2,1,0:T(8,128)(2,1)S(1)} %bitcast.10), channel_id=1, replica_groups=mesh['img'=4,'zq'=4,'zr'=4,'yc'=8] {'img','yc'}, dimensions={0} | all-to-all | bytes 524288 | tf_op jit(solution)/shard_map/all_to_all | solution.py:596
  106.0 1.4 %collect.1 = f32[10,96,128]{2,1,0:T(8,128)} custom-call(bf16[32,32,128]{2,1,0:T(8,128)(2,1)S(1)} %all_to_all.16.got), custom_call_target="tpu_custom_call" | custom-call | tf_op jit(solution)/shard_map/collect/pallas_call | solution.py:597
  (3 shorter events, 0.1 us)
Async XLA Ops:
  2.5 15.4 %all-to-all-start = ((f32[8,32,128]{2,1,0:T(8,128)}), f32[8,32,128]{2,1,0:T(8,128)S(1)}, u32[]{:S(2)}, u32[]{:S(2)}) async-start(f32[8,32,128]{2,1,0:T(8,128)} %pack.1), calls=%async_computation | async-start | bytes 262144 | tf_op jit(solution)/shard_map/all_to_all | solution.py:523
  17.8 8.6 %copy-start.4 = (f32[8,32,128]{2,1,0:T(8,128)}, f32[8,32,128]{2,1,0:T(8,128)S(1)}, u32[]{:S(2)}) copy-start(f32[8,32,128]{2,1,0:T(8,128)S(1)} %all-to-all-done.own) | copy-start | bytes 393220
  17.9 8.6 %collective-permute-start = (f32[4,32,128]{2,1,0:T(8,128)S(1)}, f32[4,32,128]{2,1,0:T(8,128)S(1)}, u32[]{:S(2)}, u32[]{:S(2)}) collective-permute-start(f32[4,32,128]{2,1,0:T(8,128)S(1)} %slice_select_fusion), channel_id=1, source_target_pairs={{0,8},{1,9},{2,10},{3,11},{5,125},{6,126},{7,127},{8,16},{9,17},{1... | collective-permute-start | bytes 196616 | tf_op jit(solution)/shard_map/ppermute | solution.py:525
  26.5 0.6 copy-start.5
  33.7 31.0 %copy-start = (bf16[4,128,32]{2,1,0:T(8,128)(2,1)S(1)}, bf16[4,128,32]{2,1,0:T(8,128)(2,1)}, u32[]{:S(2)}) copy-start(bf16[4,128,32]{2,1,0:T(8,128)(2,1)} %constant.38.clone.placet) | copy-start | bytes 98308
  33.7 31.0 %copy-start.1 = (f32[4,32,128]{2,1,0:T(8,128)S(1)}, f32[4,32,128]{2,1,0:T(8,128)}, u32[]{:S(2)}) copy-start(f32[4,32,128]{2,1,0:T(8,128)} %constant.39.clone.vert) | copy-start | bytes 196612
  65.8 0.6 copy-start.3
  66.4 9.4 %copy-start.2 = (f32[4,32,128]{2,1,0:T(8,128)}, f32[4,32,128]{2,1,0:T(8,128)S(1)}, u32[]{:S(2)}) copy-start(f32[4,32,128]{2,1,0:T(8,128)S(1)} %get-tuple-element.15.up) | copy-start | bytes 196612
  66.4 8.3 %collective-permute-start.2 = (f32[4,32,128]{2,1,0:T(8,128)S(1)}, f32[4,32,128]{2,1,0:T(8,128)S(1)}, u32[]{:S(2)}, u32[]{:S(2)}) collective-permute-start(f32[4,32,128]{2,1,0:T(8,128)S(1)} %get-tuple-element.15.up), channel_id=1, source_target_pairs={{127,0},{1,2},{3,4},{5,6},{7,8},{9,10},{11,12},{13,14},{15,16},{17... | collective-permute-start | bytes 196616 | tf_op jit(solution)/shard_map/ppermute | solution.py:564
  72.6 3.1 %collective-permute-start.1 = (f32[4,32,128]{2,1,0:T(8,128)S(1)}, f32[4,32,128]{2,1,0:T(8,128)S(1)}, u32[]{:S(2)}, u32[]{:S(2)}) collective-permute-start(f32[4,32,128]{2,1,0:T(8,128)S(1)} %get-tuple-element.15.up), channel_id=1, source_target_pairs={{0,1},{1,0},{2,3},{3,2},{4,5},{5,4},{6,7},{7,6},{8,9},{9,8},{10,11... | collective-permute-start | bytes 196616 | tf_op jit(solution)/shard_map/ppermute | solution.py:565
  74.7 1.1 copy-start.6
  75.8 0.6 copy-start.7
  83.0 5.1 %collective-permute-start.3 = (bf16[4,32,128]{2,1,0:T(8,128)(2,1)}, bf16[4,32,128]{2,1,0:T(8,128)(2,1)S(1)}, u32[]{:S(2)}, u32[]{:S(2)}) collective-permute-start(bf16[4,32,128]{2,1,0:T(8,128)(2,1)} %get-tuple-element.22), channel_id=1, source_target_pairs={{8,0},{9,1},{10,2},{11,3},{125,5},{126,6},{127,7},{16,8},{17,9},{1... | collective-permute-start | bytes 98312 | tf_op jit(solution)/shard_map/ppermute | solution.py:591

commit v3 on v2

--- a/solution.py
+++ b/solution.py
@@ -18,6 +18,7 @@
 NEAR = 8
 CAP = 3
 RADIUS = 5
+KMAX = 6
 TILES = 4
 PIX = 256
 N_IMG = 4
@@ -38,6 +39,8 @@
 bf16 = jnp.bfloat16
 highest = lax.Precision.HIGHEST
 GS = ("zq", "zr", "yc")
+
+CNT, LST, TCN, REN = 0, 8, 24, 28
 
 
 def constants():
@@ -53,7 +56,7 @@
     momt[:6] = moments.T
     long = (np.arange(256)[:, None] < np.arange(256)[None, :]).astype(float)
     alone = long * (np.arange(256)[:, None] // 128 == np.arange(256)[None, :] // 128)
-    tri = np.stack([alone, long])
+    tri = -np.stack([alone, long])
     trib = np.stack([alone.T, long.T])
     spread = (pix[:, None] % 16 == lane[None, :] % 16).astype(float)
     place = np.zeros((CH, SIDE, 128))
@@ -123,44 +126,41 @@
     return lax.broadcasted_iota(jnp.int32, shape, dim)
 
 
-def source_places(counts, lists, yc):
-    ends = []
-    total = 0
+def source_places(ints, table, yc):
+    start = jnp.int32(0)
     for o in range(NEAR):
-        total = total + counts[o]
-        ends.append(total)
-    places = []
-    for e in range(SLOTS):
-        s = lists[e]
-        group = 0
-        start = 0
-        for o in range(NEAR):
-            past = s >= ends[o]
-            group = group + jnp.where(past, 1, 0)
-            start = start + jnp.where(past, counts[o], 0)
-        apart = yc + group - NEAR // 2
+        apart = yc + o - NEAR // 2
         near = jnp.bitwise_and(apart, 7)
-        chunk = jnp.where(apart == near, near, 8 + jnp.bitwise_and(near, 3))
-        places.append(chunk * CAP + s - start)
-    return places
-
-
-def list_slots(tile_counts):
-    ends = []
-    total = 0
-    for t in range(TILES - 1):
-        total = total + tile_counts[t]
-        ends.append(total)
-    slots = []
-    for e in range(SLOTS):
-        slot = 0
-        for t in range(TILES - 1):
-            slot = slot + jnp.where(ends[t] <= e, 1, 0)
-        slots.append(slot)
-    return slots
-
-
-def pack_kernel(request, gauss, out):
+        base = CAP * jnp.where(apart == near, near, 8 + jnp.bitwise_and(near, 3))
+        for c in range(CAP):
+            table[start + c] = base + c
+        start = start + ints[CNT + o]
+    return [table[ints[LST + e]] for e in range(SLOTS)]
+
+
+def list_slots(ints, table):
+    start = jnp.int32(0)
+    for t in range(TILES):
+        for c in range(KMAX):
+            table[start + c] = jnp.int32(t)
+        start = start + ints[TCN + t]
+    return [table[e] for e in range(SLOTS)]
+
+
+def fetch(pairs, sems):
+    copies = [pltpu.make_async_copy(src, dst, sems.at[n]) for n, (src, dst) in enumerate(pairs)]
+    for copy in copies:
+        copy.start()
+    return copies
+
+
+def wait(copies):
+    for copy in copies:
+        copy.wait()
+
+
+def pack_kernel(request_in, gauss_in, out, request, gauss, sems):
+    wait(fetch([(request_in, request), (gauss_in, gauss)], sems))
     yc = lax.axis_index("yc")
     lane = iota((1, 128), 1) % 32
     for chunk in range(N_YC):
@@ -175,14 +175,24 @@
         out[chunk, 30:32, :] = jnp.broadcast_to(row.astype(f32), (2, 128))
 
 
-def forward_kernel(counts, lists, tile_counts, render, own, cross, target, mom, tri, spread, place,
-                   payload, raws, pair_o, beta_o, blk, vals, coefs, shades, cols, pair_w, beta, sems):
+def forward_kernel(ints_in, target_in, mom_in, tri_in, spread_in, place_in, own, cross, payload, raws, pair_o,
+                   beta_o, ints, group_table, slot_table, target, mom, tri, spread, place, blk, vals, coefs, shades, cols, pair_w, beta, in_sems, sems):
+    loads = fetch(
+        [
+            (ints_in, ints),
+            (mom_in, mom), (tri_in, tri), (spread_in, spread), (place_in, place), (target_in, target),
+        ],
+        in_sems,
+    )
     for m in range(12):
         for c in range(CAP):
             src = own[m, 10 * c : 10 * c + 10, :] if m < 8 else cross[m - 8, 10 * c : 10 * c + 10, :]
             blk[m * CAP + c, 0:10, :] = src
-    places = source_places(counts, lists, lax.axis_index("yc"))
-    slots = list_slots(tile_counts)
+    coefs[...] = jnp.zeros_like(coefs)
+    cols[...] = jnp.zeros_like(cols)
+    wait(loads[:1])
+    places = source_places(ints, group_table, lax.axis_index("yc"))
+    slots = list_slots(ints, slot_table)
     shades[...] = jnp.zeros_like(shades)
     for e in range(SLOTS):
         raw = blk[places[e]]
@@ -212,7 +222,6 @@
         -log2e * cb,
         (-0.5 * log2e) * cc,
     ]
-    coefs[...] = jnp.zeros_like(coefs)
     for k in range(6):
         high = table[k].astype(bf16).astype(f32)
         rest = table[k] - high
@@ -222,21 +231,21 @@
             coefs[e // 2, k : k + 1, lanes] = high[e : e + 1, :]
             coefs[e // 2, 8 + k : 9 + k, lanes] = mid[e : e + 1, :]
             coefs[e // 2, 16 + k : 17 + k, lanes] = (rest - mid)[e : e + 1, :]
-    cols[...] = jnp.zeros_like(cols)
+    wait(loads[1:])
     upper = iota((8, PIX), 0) < 4
     carry = jnp.zeros((PIX, 128), f32)
     for pair in range(PAIRS):
         first, second = 2 * pair, 2 * pair + 1
         same = slots[first] == slots[second]
         alpha = jnp.exp2(dot(mom[...], coefs[pair].astype(bf16)))
-        lost = alpha * (-1.0 + alpha * (-1.0 / 2 + alpha * (-1.0 / 3 + alpha * (-1.0 / 4))))
-        beta[pair] = (alpha * jnp.exp(-lost)).astype(bf16)
+        lost = alpha * (log2e + alpha * (log2e / 2 + alpha * (log2e / 3 + alpha * (log2e / 4))))
+        beta[pair] = (alpha * jnp.exp2(lost)).astype(bf16)
         sums = dot(lost.astype(bf16), tri[jnp.where(same, 1, 0)])
-        whole = jnp.broadcast_to(sums[:, 255:256] + lost[:, 255:256], (PIX, 128))
+        whole = jnp.broadcast_to(sums[:, 255:256] - lost[:, 255:256], (PIX, 128))
         if pair:
             carry = jnp.where(slots[first] == slots[first - 1], carry, 0.0)
         later = jnp.where(same, carry, 0.0)
-        weight = (jnp.exp(sums + jnp.concatenate([carry, later], axis=1)) * alpha).astype(bf16)
+        weight = (jnp.exp2(sums + jnp.concatenate([carry, later], axis=1)) * alpha).astype(bf16)
         carry = whole + later
         pair_w[pair] = weight
         colour = dot(shades[pair].astype(bf16), weight, ((1,), (1,)))
@@ -274,7 +283,7 @@
     row = iota((8, 128), 0)
     tags = jnp.zeros((8, 128), jnp.int32)
     for s in range(TILES):
-        tags = jnp.where(row == s, jnp.bitwise_and(render[s], 3), tags)
+        tags = jnp.where(row == s, jnp.bitwise_and(ints[REN + s], 3), tags)
     tags = tags.astype(f32).astype(bf16)
     for q in range(N_IMG * N_ZQ):
         payload[q, 0:64, :] = body
@@ -283,7 +292,7 @@
         copy.wait()
 
 
-def error_kernel(got, vert, placet, up, err_own, rendered, errs, images):
+def error_kernel(got, vert, placet, up, edge, err_own, rendered, errs, images):
     lane = iota((TILE, 128), 1)
     half = lane // 64
     halff = half.astype(f32)
@@ -306,21 +315,26 @@
     blurred = dot(vert[img], errs[...], precision=highest)
     for home in range(N_ZQ):
         up[home] = blurred[:, home * 128 : home * 128 + 128]
+        edge[home] = blurred[:, home * 128 : home * 128 + 128].astype(bf16)
         err_own[home] = errs[pl.ds(pl.multiple_of(img * 32, 32), 32), home * 128 : home * 128 + 128]
     mine = images[img * 4 + lax.axis_index("zq")].astype(bf16)
     for c in range(CH):
         rendered[c] = dot(mine, placet[c]).astype(bf16)
 
 
-def backward_kernel(counts, lists, tile_counts, render, up, got_mate, got_other, err_own, horiz, placet, spreadt,
-                    momt, trib, raws, pair_o, beta_o, own, cross, grad_out, msg_own, msg_cross,
-                    ext, back, grads, vals, sums, blk, pack, shades, shade_sums, pair_w, beta, sems):
-    copies = (
-        pltpu.make_async_copy(pair_o, pair_w, sems.at[0]),
-        pltpu.make_async_copy(beta_o, beta, sems.at[1]),
-    )
-    for copy in copies:
-        copy.start()
+def backward_kernel(ints_in, horiz_in, placet_in, spreadt_in, momt_in, trib_in,
+                    pair_o, beta_o, up, got_mate, got_other, err_own, raws, own, cross,
+                    grad_out, msg_own, msg_cross,
+                    ints, group_table, slot_table, horiz, placet, spreadt, momt, trib, pair_w, beta,
+                    ext, back, grads, vals, sums, blk, pack, shades, shade_sums, sems):
+    loads = fetch(
+        [
+            (ints_in, ints),
+            (horiz_in, horiz), (placet_in, placet), (spreadt_in, spreadt), (momt_in, momt), (trib_in, trib),
+            (pair_o, pair_w), (beta_o, beta),
+        ],
+        sems,
+    )
     yc = lax.axis_index("yc")
     zq = lax.axis_index("zq")
     parity = jnp.bitwise_and(yc, 1)
@@ -335,11 +349,12 @@
         at_right = jnp.minimum(at_right, N_ZQ - 1)
         left = jnp.where(parity == 0, got_other[at_left], got_mate[at_left])
         right = jnp.where(parity == 0, got_mate[at_right], got_other[at_right])
-        left = jnp.where(in_left, left, 0.0)
-        right = jnp.where(in_right, right, 0.0)
+        left = jnp.where(in_left, left.astype(f32), 0.0)
+        right = jnp.where(in_right, right.astype(f32), 0.0)
         rows = slice(home * 32, home * 32 + 32)
         ext[rows, 0:128] = up[home]
         ext[rows, 128:256] = jnp.where(lane32 < 64, right, left)
+    wait(loads[:4])
     back[...] = dot(ext[...], horiz[0], precision=highest)
 
     @pl.when(place_mid == 0)
@@ -363,7 +378,7 @@
     pieces = []
     for s in range(TILES):
         home = jnp.bitwise_and(zq + s, 3)
-        local = jnp.bitwise_and(render[s], 3)
+        local = jnp.bitwise_and(ints[REN + s], 3)
         down = local // 2
         across = jnp.bitwise_and(local, 1)
         tile = grads[home, pl.ds(pl.multiple_of(down * 16, 16), 16), :]
@@ -382,8 +397,8 @@
     grad_cols = jnp.transpose(grad_rows).astype(bf16)
     grad_rows = grad_rows.astype(bf16)
 
-    slots = list_slots(tile_counts)
-    places = source_places(counts, lists, yc)
+    slots = list_slots(ints, slot_table)
+    places = source_places(ints, group_table, yc)
     shades[...] = jnp.zeros_like(shades)
     for e in range(SLOTS):
         shade = raws[e, 6:10, :]
@@ -392,8 +407,7 @@
         shades[e // 2, at, 128 * (e % 2) : 128 * (e % 2) + 128] = jnp.concatenate([high, shade - high], axis=0)
         for k in range(6):
             vals[k, e : e + 1, :] = raws[e, k : k + 1, :]
-    for copy in copies:
-        copy.wait()
+    wait(loads[4:])
     carry = jnp.zeros((PIX, 128), f32)
     for pair in reversed(range(PAIRS)):
         first, second = 2 * pair, 2 * pair + 1
@@ -482,7 +496,7 @@
 
 VM = pl.BlockSpec(memory_space=pltpu.VMEM)
 SM = pl.BlockSpec(memory_space=pltpu.SMEM)
-ANY = pl.BlockSpec(memory_space=pl.ANY)
+HB = pl.BlockSpec(memory_space=pltpu.HBM)
 
 
 def call(kernel, ins, outs, scratch, name, limit=16):
@@ -500,10 +514,9 @@
 def on_device(gaussians, target, request, near_counts, render_tile, tile_lists, tile_counts):
     table = constants()
     yc = lax.axis_index("yc")
-    counts = near_counts.reshape(NEAR)
-    render = render_tile.reshape(TILES)
-    lists = tile_lists.reshape(SLOTS)
-    lengths = tile_counts.reshape(TILES)
+    ints = jnp.concatenate(
+        [near_counts.reshape(NEAR), tile_lists.reshape(SLOTS), tile_counts.reshape(TILES), render_tile.reshape(TILES)]
+    )
     wanted = request.transpose(0, 3, 1, 2).reshape(CAP, 1, NEAR)
     n_gs = N_ZQ * N_ZR * N_YC
     up_route = []
@@ -517,23 +530,37 @@
     group = N_IMG * N_ZQ
     vm = pltpu.VMEM
 
-    (sent,) = call(pack_kernel, [SM, VM], [((N_YC, MSG, 128), f32, VM)], [], "pack", None)(
-        wanted, gaussians.transpose(1, 0, 2)
-    )
+    small = [pltpu.SMEM((32,), jnp.int32) for _ in range(3)]
+    dma = pltpu.SemaphoreType.DMA
+
+    (sent,) = call(
+        pack_kernel,
+        [HB, HB],
+        [((N_YC, MSG, 128), f32, VM)],
+        [pltpu.SMEM((CAP, 1, NEAR), jnp.int32), vm((VALS, BLK_DEV, 128), f32), dma((2,))],
+        "pack",
+        None,
+    )(wanted, gaussians.transpose(1, 0, 2))
     own = lax.all_to_all(sent, "yc", 0, 0, tiled=True)
     crossing = jnp.where(yc < 4, own[4:8], own[0:4])
     cross = lax.ppermute(crossing, GS, up_route)
 
     payload, raws, pair_w, beta = call(
         forward_kernel,
-        [SM] * 4 + [VM] * 7,
+        [HB] * 6 + [VM] * 2,
         [
             ((group, 72, 128), bf16, VM),
             ((SLOTS, 16, 128), f32, VM),
-            ((PAIRS, PIX, 256), bf16, ANY),
-            ((PAIRS, PIX, 256), bf16, ANY),
+            ((PAIRS, PIX, 256), bf16, HB),
+            ((PAIRS, PIX, 256), bf16, HB),
         ],
-        [
+        small
+        + [
+            vm((CH, SIDE, SIDE), bf16),
+            vm((PIX, 32), bf16),
+            vm((2, 256, 256), bf16),
+            vm((PIX, 128), bf16),
+            vm((CH, SIDE, 128), bf16),
             vm((36, 16, 128), f32),
             vm((6, 16, 128), f32),
             vm((PAIRS, 32, 256), f32),
@@ -541,34 +568,47 @@
             vm((TILES, 8, PIX), f32),
             vm((PAIRS, PIX, 256), bf16),
             vm((PAIRS, PIX, 256), bf16),
-            pltpu.SemaphoreType.DMA((2,)),
+            dma((6,)),
+            dma((2,)),
         ],
         "forward",
-        None,
     )(
-        counts, lists, lengths, render, own, cross, target, table["mom"], table["tri"], table["spread"],
-        table["place"],
+        ints, target, table["mom"], table["tri"], table["spread"], table["place"],
+        own, cross,
     )
     got = lax.all_to_all(payload, ("img", "zq"), 0, 0, tiled=True)
 
-    up, err_own, rendered = call(
+    up, edge, err_own, rendered = call(
         error_kernel,
         [VM] * 3,
-        [((N_ZQ, SIDE, 128), f32, VM), ((N_ZQ, SIDE, 128), f32, VM), ((CH, SIDE, SIDE), bf16, VM)],
+        [
+            ((N_ZQ, SIDE, 128), f32, VM),
+            ((N_ZQ, SIDE, 128), bf16, VM),
+            ((N_ZQ, SIDE, 128), f32, VM),
+            ((CH, SIDE, SIDE), bf16, VM),
+        ],
         [vm((N_IMG * SIDE, 512), f32), vm((16, SIDE, 128), f32)],
         "error",
     )(got, table["vert"], table["placet"])
 
     other = [((2 * c - 1) % n_gs, 2 * c) for c in range(n_gs // 2)]
     other = other + [(b, a) for a, b in other]
-    got_other = lax.ppermute(up, GS, other)
-    got_mate = lax.ppermute(up, GS, [(r, r ^ 1) for r in range(n_gs)])
+    got_other = lax.ppermute(edge, GS, other)
+    got_mate = lax.ppermute(edge, GS, [(r, r ^ 1) for r in range(n_gs)])
 
     pixel_grad, msg_own, msg_cross = call(
         backward_kernel,
-        [SM] * 4 + [VM] * 10 + [ANY] * 2 + [VM] * 2,
+        [HB] * 8 + [VM] * 7,
         [((CH, SIDE, SIDE), bf16, VM), ((N_YC, MSG, 128), bf16, VM), ((4, MSG, 128), bf16, VM)],
-        [
+        small
+        + [
+            vm((3, 256, 128), f32),
+            vm((CH, 128, SIDE), bf16),
+            vm((128, PIX), bf16),
+            vm((16, PIX), bf16),
+            vm((2, 256, 256), bf16),
+            vm((PAIRS, PIX, 256), bf16),
+            vm((PAIRS, PIX, 256), bf16),
             vm((128, 256), f32),
             vm((128, 128), f32),
             vm((N_ZQ, SIDE, 128), f32),
@@ -578,15 +618,12 @@
             vm((12, MSG, 128), f32),
             vm((PAIRS, 32, 256), f32),
             vm((PAIRS, TILES, 8, 256), f32),
-            vm((PAIRS, PIX, 256), bf16),
-            vm((PAIRS, PIX, 256), bf16),
-            pltpu.SemaphoreType.DMA((2,)),
+            dma((8,)),
         ],
         "backward",
-        None,
     )(
-        counts, lists, lengths, render, up, got_mate, got_other, err_own, table["horiz"], table["placet"],
-        table["spreadt"], table["momt"], table["trib"], raws, pair_w, beta, own, cross,
+        ints, table["horiz"], table["placet"], table["spreadt"], table["momt"],
+        table["trib"], pair_w, beta, up, got_mate, got_other, err_own, raws, own, cross,
     )
     returned = lax.ppermute(msg_cross, GS, back_route)
     apart = jnp.arange(N_YC) + NEAR // 2 - yc

time: 108 us -> 101 us (0.935)
  Pallas kernels: 17.6 us -> 13.3 us
  local copies, waits for them, and re-layouts: 1.93 us -> 0.75 us
    pallas_call x3, Pallas kernels: 15.1 us -> 10.8 us  [the longest x1 4.83 us: on_device(): call(backward_kernel, [HB] * 8 + [VM] * 7, [((CH, SIDE, SIDE), bf16, VM),...]
    unnamed x16 -> x30, local copies, waits for them, and re-layouts: 1.89 us -> 0.71 us
where the time goes in v3:
time: 101 us; the launch traced here: 100 us
  blocking collectives  47.6 us (47%)
  starting transfers between devices  22.6 us (22%)
  waiting for transfers between devices  15.2 us (15%)
  Pallas kernels  13.3 us (13%)
    all_to_all x1, blocking collectives, on_device(): got = lax.all_to_all(payload, ('img', 'zq'), 0, 0, tiled=True)  30.7 us
    all_to_all x1, blocking collectives, on_device(): all_msgs = lax.all_to_all(spread_out, ('img', 'yc'), 0, 0, tiled=True)  16.8 us
    all_to_all x1, starting transfers between devices, on_device(): own = lax.all_to_all(sent, 'yc', 0, 0, tiled=True)  10.3 us
    ppermute x1, starting transfers between devices, on_device(): got_other = lax.ppermute(edge, GS, other)  6.34 us
    ppermute x1, waiting for transfers between devices, on_device(): cross = lax.ppermute(crossing, GS, up_route)  5.9 us
    all_to_all x1, waiting for transfers between devices, on_device(): own = lax.all_to_all(sent, 'yc', 0, 0, tiled=True)  5.26 us
    pallas_call x1, Pallas kernels, on_device(): call(backward_kernel, [HB] * 8 + [VM] * 7, [((CH, SIDE, SIDE), bf16, VM),...  4.83 us
    pallas_call x1, Pallas kernels, on_device(): call(forward_kernel, [HB] * 6 + [VM] * 2, [((group, 72, 128), bf16, VM),...  4.09 us
  transfers between devices with their start and end apart: 5, of which 4 were waited for; matrix products, arithmetic and copies ran while one was open for 0% of the time, Pallas kernels for 0%

profile of v3, /device:TPU:1, one launch (start us, length us, event | category | flops | bytes accessed | tf_op | source)
XLA Modules:
  0.0 100.4 jit_solution(15399015192227323207)
XLA Ops:
  0.6 1.8 %pack.1 = f32[8,32,128]{2,1,0:T(8,128)} custom-call(s32[3,1,8]{2,1,0:T(1,128)} %bitcast.13, f32[10,96,128]{2,1,0:T(8,128)} %bitcast.11), custom_call_target="tpu_custom_call" | custom-call | tf_op jit(solution)/shard_map/pack/pallas_call | solution.py:536
  2.5 0.0 copy-start.3
  2.5 10.3 %all-to-all-start = ((f32[8,32,128]{2,1,0:T(8,128)}), f32[8,32,128]{2,1,0:T(8,128)S(1)}, u32[]{:S(2)}, u32[]{:S(2)}) async-start(f32[8,32,128]{2,1,0:T(8,128)} %pack.1), calls=%async_computation | async-start | bytes 262144 | tf_op jit(solution)/shard_map/all_to_all | solution.py:544
  12.7 0.0 copy-start.6
  12.7 0.0 copy-start.7
  12.7 5.3 %all-to-all-done.own = f32[8,32,128]{2,1,0:T(8,128)S(1)} async-done(((f32[8,32,128]{2,1,0:T(8,128)}), f32[8,32,128]{2,1,0:T(8,128)S(1)}, u32[]{:S(2)}, u32[]{:S(2)}) %all-to-all-start) | async-done | bytes 131104 | tf_op jit(solution)/shard_map/all_to_all | solution.py:544
  18.0 0.0 copy-start.14
  18.0 0.0 copy-start.8
  18.0 0.0 copy-start.9
  18.0 2.1 %collective-permute-start = (f32[4,32,128]{2,1,0:T(8,128)S(1)}, f32[4,32,128]{2,1,0:T(8,128)S(1)}, u32[]{:S(2)}, u32[]{:S(2)}) collective-permute-start(f32[4,32,128]{2,1,0:T(8,128)S(1)} %slice_select_fusion), channel_id=1, source_target_pairs={{0,8},{1,9},{2,10},{3,11},{5,125},{6,126},{7,127},{8,16},{9,17},{1... | collective-permute-start | bytes 196616 | tf_op jit(solution)/shard_map/ppermute | solution.py:546
  20.1 0.0 copy-start.11
  20.1 0.0 copy-start.12
  20.1 0.0 copy-start.13
  20.1 0.0 copy-done.14
  20.1 0.6 copy-done.11
  20.7 0.0 copy-done.12
  20.8 0.0 copy-done.13
  20.8 0.1 pad_add_fusion.ints_in
  20.9 5.9 %collective-permute-done.cross = f32[4,32,128]{2,1,0:T(8,128)S(1)} collective-permute-done((f32[4,32,128]{2,1,0:T(8,128)S(1)}, f32[4,32,128]{2,1,0:T(8,128)S(1)}, u32[]{:S(2)}, u32[]{:S(2)}) %collective-permute-start) | collective-permute-done | bytes 65568 | tf_op jit(solution)/shard_map/ppermute | solution.py:546
  26.8 0.0 copy-done.3
  26.8 0.0 copy-done.6
  26.8 0.0 copy-done.7
  26.8 0.0 copy-done.8
  26.8 0.0 copy-done.9
  26.8 4.1 %forward.1 = (bf16[16,72,128]{2,1,0:T(8,128)(2,1)S(1)}, f32[16,16,128]{2,1,0:T(8,128)S(1)}, bf16[8,256,256]{2,1,0:T(8,128)(2,1)S(1)}, bf16[8,256,256]{2,1,0:T(8,128)(2,1)S(1)}) custom-call(s32[32]{0:T(128)S(1)} %pad_add_fusion.ints_in, bf16[4,32,32]{2,1,0:T(8,128)(2,1)S(1)} %copy-done.8, bf16[256,32]{1,0:T(8,128)(2,1)S(1)} %copy-done.7, ...), custom_call_target="tpu_custom_call" | custom-call | tf_op jit(solution)/shard_map/forward/pallas_call | solution.py:548
  30.9 0.0 copy-start
  30.9 0.0 copy-start.5
  30.9 0.0 copy-start.2
  30.9 30.7 %all_to_all.15.got = bf16[16,72,128]{2,1,0:T(8,128)(2,1)S(1)} all-to-all(bf16[16,72,128]{2,1,0:T(8,128)(2,1)S(1)} %get-tuple-element.14), channel_id=1, replica_groups=mesh['img'=4,'zq'=4,'zr'=4,'yc'=8] {'img','zq'}, dimensions={0} | all-to-all | bytes 589824 | tf_op jit(solution)/shard_map/all_to_all | solution.py:579
  61.7 0.0 copy-done
  61.7 0.0 copy-done.5
  61.7 0.0 copy-start.1
  61.7 0.0 copy-start.4
  61.7 1.1 %error.1 = (f32[4,32,128]{2,1,0:T(8,128)S(1)}, bf16[4,32,128]{2,1,0:T(8,128)(2,1)S(1)}, f32[4,32,128]{2,1,0:T(8,128)S(1)}, bf16[4,32,32]{2,1,0:T(8,128)(2,1)}) custom-call(bf16[16,72,128]{2,1,0:T(8,128)(2,1)S(1)} %all_to_all.15.got, f32[4,32,128]{2,1,0:T(8,128)S(1)} %copy-done.5, bf16[4,128,32]{2,1,0:T(8,128)(2,1)S(1)} %copy-done), custom_call_target="tpu_custom_call" | custom-call | tf_op jit(solution)/shard_map/error/pallas_call | solution.py:581
  62.8 0.0 copy-start.10
  62.8 6.3 %collective-permute-start.2 = (bf16[4,32,128]{2,1,0:T(8,128)(2,1)S(1)}, bf16[4,32,128]{2,1,0:T(8,128)(2,1)S(1)}, u32[]{:S(2)}, u32[]{:S(2)}) collective-permute-start(bf16[4,32,128]{2,1,0:T(8,128)(2,1)S(1)} %get-tuple-element.19), channel_id=1, source_target_pairs={{127,0},{1,2},{3,4},{5,6},{7,8},{9,10},{11,12},{13,14},{15,16},{17... | collective-permute-start | bytes 98312 | tf_op jit(solution)/shard_map/ppermute | solution.py:596
  69.1 2.1 %collective-permute-start.1 = (bf16[4,32,128]{2,1,0:T(8,128)(2,1)S(1)}, bf16[4,32,128]{2,1,0:T(8,128)(2,1)S(1)}, u32[]{:S(2)}, u32[]{:S(2)}) collective-permute-start(bf16[4,32,128]{2,1,0:T(8,128)(2,1)S(1)} %get-tuple-element.19), channel_id=1, source_target_pairs={{0,1},{1,0},{2,3},{3,2},{4,5},{5,4},{6,7},{7,6},{8,9},{9,8},{10,11... | collective-permute-start | bytes 98312 | tf_op jit(solution)/shard_map/ppermute | solution.py:597
  71.2 0.0 collective-permute-done.2.got_other
  71.2 1.0 %collective-permute-done.1.got_mate = bf16[4,32,128]{2,1,0:T(8,128)(2,1)S(1)} collective-permute-done((bf16[4,32,128]{2,1,0:T(8,128)(2,1)S(1)}, bf16[4,32,128]{2,1,0:T(8,128)(2,1)S(1)}, u32[]{:S(2)}, u32[]{:S(2)}) %collective-permute-start.1) | collective-permute-done | bytes 32800 | tf_op jit(solution)/shard_map/ppermute | solution.py:597
  72.2 0.0 copy-done.2
  72.2 0.0 copy-done.1
  72.2 0.0 copy-done.4
  72.2 0.0 copy-done.10
  72.2 4.8 %backward.1 = (bf16[4,32,32]{2,1,0:T(8,128)(2,1)}, bf16[8,32,128]{2,1,0:T(8,128)(2,1)S(1)}, bf16[4,32,128]{2,1,0:T(8,128)(2,1)S(1)}) custom-call(s32[32]{0:T(128)S(1)} %pad_add_fusion.ints_in, f32[3,256,128]{2,1,0:T(8,128)S(1)} %copy-done.1, bf16[4,128,32]{2,1,0:T(8,128)(2,1)S(1)} %copy-done, bf16[128,256]{1,0:T(8,128)(2,1)S(1)} %copy-done.4, ...), custom_call_target="tpu_custom_call" | custom-call | tf_op jit(solution)/shard_map/backward/pallas_call | solution.py:599
  77.1 1.9 %collective-permute-start.3 = (bf16[4,32,128]{2,1,0:T(8,128)(2,1)S(1)}, bf16[4,32,128]{2,1,0:T(8,128)(2,1)S(1)}, u32[]{:S(2)}, u32[]{:S(2)}) collective-permute-start(bf16[4,32,128]{2,1,0:T(8,128)(2,1)S(1)} %get-tuple-element.24), channel_id=1, source_target_pairs={{8,0},{9,1},{10,2},{11,3},{125,5},{126,6},{127,7},{16,8},{17,9},{1... | collective-permute-start | bytes 98312 | tf_op jit(solution)/shard_map/ppermute | solution.py:628
  79.0 3.0 %collective-permute-done.3 = bf16[4,32,128]{2,1,0:T(8,128)(2,1)S(1)} collective-permute-done((bf16[4,32,128]{2,1,0:T(8,128)(2,1)S(1)}, bf16[4,32,128]{2,1,0:T(8,128)(2,1)S(1)}, u32[]{:S(2)}, u32[]{:S(2)}) %collective-permute-start.3) | collective-permute-done | bytes 32800 | tf_op jit(solution)/shard_map/ppermute | solution.py:628
  82.0 0.1 maximum_select_fusion
  82.2 16.8 %all_to_all.16.got = bf16[32,32,128]{2,1,0:T(8,128)(2,1)S(1)} all-to-all(bf16[32,32,128]{2,1,0:T(8,128)(2,1)S(1)} %bitcast.10), channel_id=1, replica_groups=mesh['img'=4,'zq'=4,'zr'=4,'yc'=8] {'img','yc'}, dimensions={0} | all-to-all | bytes 524288 | tf_op jit(solution)/shard_map/all_to_all | solution.py:633
  99.0 1.4 %collect.1 = f32[10,96,128]{2,1,0:T(8,128)} custom-call(bf16[32,32,128]{2,1,0:T(8,128)(2,1)S(1)} %all_to_all.16.got), custom_call_target="tpu_custom_call" | custom-call | tf_op jit(solution)/shard_map/collect/pallas_call | solution.py:634
  (3 shorter events, 0.1 us)
Async XLA Ops:
  2.5 24.3 %copy-start.3 = (bf16[2,256,256]{2,1,0:T(8,128)(2,1)S(1)}, bf16[2,256,256]{2,1,0:T(8,128)(2,1)}, u32[]{:S(2)}) copy-start(bf16[2,256,256]{2,1,0:T(8,128)(2,1)} %constant.33.clone.tri_in) | copy-start | bytes 786436
  2.5 15.5 %all-to-all-start = ((f32[8,32,128]{2,1,0:T(8,128)}), f32[8,32,128]{2,1,0:T(8,128)S(1)}, u32[]{:S(2)}, u32[]{:S(2)}) async-start(f32[8,32,128]{2,1,0:T(8,128)} %pack.1), calls=%async_computation | async-start | bytes 262144 | tf_op jit(solution)/shard_map/all_to_all | solution.py:544
  12.7 14.0 %copy-start.6 = (bf16[256,128]{1,0:T(8,128)(2,1)S(1)}, bf16[256,128]{1,0:T(8,128)(2,1)}, u32[]{:S(2)}) copy-start(bf16[256,128]{1,0:T(8,128)(2,1)} %constant.35.clone.spread_in) | copy-start | bytes 196612
  12.7 14.0 %copy-start.7 = (bf16[256,32]{1,0:T(8,128)(2,1)S(1)}, bf16[256,32]{1,0:T(8,128)(2,1)}, u32[]{:S(2)}) copy-start(bf16[256,32]{1,0:T(8,128)(2,1)} %constant.13.clone.mom_in) | copy-start | bytes 49156
  18.0 2.1 %copy-start.14 = (s32[1,1,8]{2,1,0:T(1,128)S(1)}, s32[1,1,8]{2,1,0:T(1,128)}, u32[]{:S(2)}) copy-start(s32[1,1,8]{2,1,0:T(1,128)} %param.20) | copy-start | bytes 100
  18.0 8.8 %copy-start.8 = (bf16[4,32,32]{2,1,0:T(8,128)(2,1)S(1)}, bf16[4,32,32]{2,1,0:T(8,128)(2,1)}, u32[]{:S(2)}) copy-start(bf16[4,32,32]{2,1,0:T(8,128)(2,1)} %target_in.1) | copy-start | bytes 24580
  18.0 8.8 %copy-start.9 = (bf16[4,32,128]{2,1,0:T(8,128)(2,1)S(1)}, bf16[4,32,128]{2,1,0:T(8,128)(2,1)}, u32[]{:S(2)}) copy-start(bf16[4,32,128]{2,1,0:T(8,128)(2,1)} %constant.37.clone.place_in) | copy-start | bytes 98308
  18.0 8.7 %collective-permute-start = (f32[4,32,128]{2,1,0:T(8,128)S(1)}, f32[4,32,128]{2,1,0:T(8,128)S(1)}, u32[]{:S(2)}, u32[]{:S(2)}) collective-permute-start(f32[4,32,128]{2,1,0:T(8,128)S(1)} %slice_select_fusion), channel_id=1, source_target_pairs={{0,8},{1,9},{2,10},{3,11},{5,125},{6,126},{7,127},{8,16},{9,17},{1... | collective-permute-start | bytes 196616 | tf_op jit(solution)/shard_map/ppermute | solution.py:546
  20.1 0.7 copy-start.11
  20.1 0.7 copy-start.12
  20.1 0.7 copy-start.13
  30.9 30.8 %copy-start = (bf16[4,128,32]{2,1,0:T(8,128)(2,1)S(1)}, bf16[4,128,32]{2,1,0:T(8,128)(2,1)}, u32[]{:S(2)}) copy-start(bf16[4,128,32]{2,1,0:T(8,128)(2,1)} %constant.38.clone.placet.placet_in) | copy-start | bytes 98308
  30.9 30.8 %copy-start.5 = (f32[4,32,128]{2,1,0:T(8,128)S(1)}, f32[4,32,128]{2,1,0:T(8,128)}, u32[]{:S(2)}) copy-start(f32[4,32,128]{2,1,0:T(8,128)} %constant.39.clone.vert) | copy-start | bytes 196612
  30.9 41.3 %copy-start.2 = (bf16[2,256,256]{2,1,0:T(8,128)(2,1)S(1)}, bf16[2,256,256]{2,1,0:T(8,128)(2,1)}, u32[]{:S(2)}) copy-start(bf16[2,256,256]{2,1,0:T(8,128)(2,1)} %constant.34.clone.trib_in) | copy-start | bytes 786436
  61.7 10.6 %copy-start.1 = (f32[3,256,128]{2,1,0:T(8,128)S(1)}, f32[3,256,128]{2,1,0:T(8,128)}, u32[]{:S(2)}) copy-start(f32[3,256,128]{2,1,0:T(8,128)} %constant.40.clone.horiz_in) | copy-start | bytes 1179652
  61.7 10.6 %copy-start.4 = (bf16[128,256]{1,0:T(8,128)(2,1)S(1)}, bf16[128,256]{1,0:T(8,128)(2,1)}, u32[]{:S(2)}) copy-start(bf16[128,256]{1,0:T(8,128)(2,1)} %constant.36.clone.spreadt_in) | copy-start | bytes 196612
  62.8 9.5 %copy-start.10 = (bf16[16,256]{1,0:T(8,128)(2,1)S(1)}, bf16[16,256]{1,0:T(8,128)(2,1)}, u32[]{:S(2)}) copy-start(bf16[16,256]{1,0:T(8,128)(2,1)} %constant.32.clone.momt_in) | copy-start | bytes 24580
  62.8 8.4 %collective-permute-start.2 = (bf16[4,32,128]{2,1,0:T(8,128)(2,1)S(1)}, bf16[4,32,128]{2,1,0:T(8,128)(2,1)S(1)}, u32[]{:S(2)}, u32[]{:S(2)}) collective-permute-start(bf16[4,32,128]{2,1,0:T(8,128)(2,1)S(1)} %get-tuple-element.19), channel_id=1, source_target_pairs={{127,0},{1,2},{3,4},{5,6},{7,8},{9,10},{11,12},{13,14},{15,16},{17... | collective-permute-start | bytes 98312 | tf_op jit(solution)/shard_map/ppermute | solution.py:596
  69.1 3.1 %collective-permute-start.1 = (bf16[4,32,128]{2,1,0:T(8,128)(2,1)S(1)}, bf16[4,32,128]{2,1,0:T(8,128)(2,1)S(1)}, u32[]{:S(2)}, u32[]{:S(2)}) collective-permute-start(bf16[4,32,128]{2,1,0:T(8,128)(2,1)S(1)} %get-tuple-element.19), channel_id=1, source_target_pairs={{0,1},{1,0},{2,3},{3,2},{4,5},{5,4},{6,7},{7,6},{8,9},{9,8},{10,11... | collective-permute-start | bytes 98312 | tf_op jit(solution)/shard_map/ppermute | solution.py:597
  77.1 4.9 %collective-permute-start.3 = (bf16[4,32,128]{2,1,0:T(8,128)(2,1)S(1)}, bf16[4,32,128]{2,1,0:T(8,128)(2,1)S(1)}, u32[]{:S(2)}, u32[]{:S(2)}) collective-permute-start(bf16[4,32,128]{2,1,0:T(8,128)(2,1)S(1)} %get-tuple-element.24), channel_id=1, source_target_pairs={{8,0},{9,1},{10,2},{11,3},{125,5},{126,6},{127,7},{16,8},{17,9},{1... | collective-permute-start | bytes 98312 | tf_op jit(solution)/shard_map/ppermute | solution.py:628

commit v4 on v3

--- a/solution.py
+++ b/solution.py
@@ -37,7 +37,6 @@
 
 f32 = jnp.float32
 bf16 = jnp.bfloat16
-highest = lax.Precision.HIGHEST
 GS = ("zq", "zr", "yc")
 
 CNT, LST, TCN, REN = 0, 8, 24, 28
@@ -107,13 +106,19 @@
         spreadt=jnp.asarray(spread.T, bf16),
         place=jnp.asarray(place, bf16),
         placet=jnp.asarray(place.transpose(0, 2, 1), bf16),
-        vert=jnp.asarray(vert, f32),
-        horiz=jnp.asarray(horiz, f32),
-    )
-
-
-def dot(a, b, dims=((1,), (0,)), precision=None):
-    return lax.dot_general(a, b, (dims, ((), ())), precision=precision, preferred_element_type=f32)
+        vert=stacked(vert, 2),
+        horiz=stacked(horiz, 1),
+    )
+
+
+def stacked(table, axis):
+    high = table.astype(bf16)
+    low = (table - high.astype(np.float64)).astype(bf16)
+    return jnp.asarray(np.concatenate([high, high, low], axis=axis))
+
+
+def dot(a, b, dims=((1,), (0,))):
+    return lax.dot_general(a, b, (dims, ((), ())), preferred_element_type=f32)
 
 
 def halves(value):
@@ -234,14 +239,23 @@
     wait(loads[1:])
     upper = iota((8, PIX), 0) < 4
     carry = jnp.zeros((PIX, 128), f32)
-    for pair in range(PAIRS):
+
+    def front(pair):
         first, second = 2 * pair, 2 * pair + 1
         same = slots[first] == slots[second]
         alpha = jnp.exp2(dot(mom[...], coefs[pair].astype(bf16)))
         lost = alpha * (log2e + alpha * (log2e / 2 + alpha * (log2e / 3 + alpha * (log2e / 4))))
         beta[pair] = (alpha * jnp.exp2(lost)).astype(bf16)
         sums = dot(lost.astype(bf16), tri[jnp.where(same, 1, 0)])
-        whole = jnp.broadcast_to(sums[:, 255:256] - lost[:, 255:256], (PIX, 128))
+        whole = sums[:, 255:256] - lost[:, 255:256]
+        return first, second, same, alpha, sums, whole
+
+    ahead = front(0)
+    for pair in range(PAIRS):
+        first, second, same, alpha, sums, whole = ahead
+        if pair + 1 < PAIRS:
+            ahead = front(pair + 1)
+        whole = jnp.broadcast_to(whole, (PIX, 128))
         if pair:
             carry = jnp.where(slots[first] == slots[first - 1], carry, 0.0)
         later = jnp.where(same, carry, 0.0)
@@ -312,7 +326,8 @@
             goal = got[strip * 4 + home, 32:64, :].astype(f32)
             errs[strip * 32 : strip * 32 + 32, home * 128 : home * 128 + 128] = image - goal
     img = lax.axis_index("img")
-    blurred = dot(vert[img], errs[...], precision=highest)
+    high, low = halves(errs[...])
+    blurred = dot(vert[img], jnp.concatenate([high, low, high], axis=0))
     for home in range(N_ZQ):
         up[home] = blurred[:, home * 128 : home * 128 + 128]
         edge[home] = blurred[:, home * 128 : home * 128 + 128].astype(bf16)
@@ -355,15 +370,17 @@
         ext[rows, 0:128] = up[home]
         ext[rows, 128:256] = jnp.where(lane32 < 64, right, left)
     wait(loads[:4])
-    back[...] = dot(ext[...], horiz[0], precision=highest)
+    high, low = halves(ext[...])
+    split = jnp.concatenate([high, low, high], axis=1)
+    back[...] = dot(split, horiz[0])
 
     @pl.when(place_mid == 0)
     def _():
-        back[0:32, :] = dot(ext[0:32, :], horiz[1], precision=highest)
+        back[0:32, :] = dot(split[0:32, :], horiz[1])
 
     @pl.when(place_mid == 31)
     def _():
-        back[96:128, :] = dot(ext[96:128, :], horiz[2], precision=highest)
+        back[96:128, :] = dot(split[96:128, :], horiz[2])
 
     for home in range(N_ZQ):
         total = loss_weight * (
@@ -409,12 +426,20 @@
             vals[k, e : e + 1, :] = raws[e, k : k + 1, :]
     wait(loads[4:])
     carry = jnp.zeros((PIX, 128), f32)
-    for pair in reversed(range(PAIRS)):
+
+    def front(pair):
         first, second = 2 * pair, 2 * pair + 1
         same = slots[first] == slots[second]
         product = pair_w[pair].astype(f32) * dot(grad_cols, shades[pair].astype(bf16))
         after = dot(product.astype(bf16), trib[jnp.where(same, 1, 0)])
-        whole = jnp.broadcast_to(after[:, 0:1] + product[:, 0:1], (PIX, 128))
+        return first, second, same, product, after, after[:, 0:1] + product[:, 0:1]
+
+    ahead = front(PAIRS - 1)
+    for pair in reversed(range(PAIRS)):
+        first, second, same, product, after, whole = ahead
+        if pair:
+            ahead = front(pair - 1)
+        whole = jnp.broadcast_to(whole, (PIX, 128))
         if pair < PAIRS - 1:
             carry = jnp.where(slots[second] == slots[second + 1], carry, 0.0)
         earlier = jnp.where(same, carry, 0.0)
@@ -514,9 +539,6 @@
 def on_device(gaussians, target, request, near_counts, render_tile, tile_lists, tile_counts):
     table = constants()
     yc = lax.axis_index("yc")
-    ints = jnp.concatenate(
-        [near_counts.reshape(NEAR), tile_lists.reshape(SLOTS), tile_counts.reshape(TILES), render_tile.reshape(TILES)]
-    )
     wanted = request.transpose(0, 3, 1, 2).reshape(CAP, 1, NEAR)
     n_gs = N_ZQ * N_ZR * N_YC
     up_route = []
@@ -542,6 +564,12 @@
         None,
     )(wanted, gaussians.transpose(1, 0, 2))
     own = lax.all_to_all(sent, "yc", 0, 0, tiled=True)
+    own, near_counts, tile_lists, tile_counts, render_tile = lax.optimization_barrier(
+        (own, near_counts, tile_lists, tile_counts, render_tile)
+    )
+    ints = jnp.concatenate(
+        [near_counts.reshape(NEAR), tile_lists.reshape(SLOTS), tile_counts.reshape(TILES), render_tile.reshape(TILES)]
+    )
     crossing = jnp.where(yc < 4, own[4:8], own[0:4])
     cross = lax.ppermute(crossing, GS, up_route)
 
@@ -602,7 +630,7 @@
         [((CH, SIDE, SIDE), bf16, VM), ((N_YC, MSG, 128), bf16, VM), ((4, MSG, 128), bf16, VM)],
         small
         + [
-            vm((3, 256, 128), f32),
+            vm((3, 768, 128), bf16),
             vm((CH, 128, SIDE), bf16),
             vm((128, PIX), bf16),
             vm((16, PIX), bf16),

time: 101 us -> 98.6 us (0.976)
  Pallas kernels: 13.3 us -> 10.9 us
    pallas_call x1, Pallas kernels: 4.83 us -> 3.6 us  [on_device(): call(backward_kernel, [HB] * 8 + [VM] * 7, [((CH, SIDE, SIDE), bf16, VM),...]
    pallas_call x1, Pallas kernels: 4.09 us -> 3.04 us  [on_device(): call(forward_kernel, [HB] * 6 + [VM] * 2, [((group, 72, 128), bf16, VM),...]
where the time goes in v4:
time: 98.6 us; the launch traced here: 98.1 us
  blocking collectives  47.6 us (48%)
  starting transfers between devices  22.6 us (23%)
  waiting for transfers between devices  15.2 us (15%)
  Pallas kernels  10.9 us (11%)
    all_to_all x1, blocking collectives, on_device(): got = lax.all_to_all(payload, ('img', 'zq'), 0, 0, tiled=True)  30.7 us
    all_to_all x1, blocking collectives, on_device(): all_msgs = lax.all_to_all(spread_out, ('img', 'yc'), 0, 0, tiled=True)  16.8 us
    all_to_all x1, starting transfers between devices, on_device(): own = lax.all_to_all(sent, 'yc', 0, 0, tiled=True)  10.3 us
    ppermute x1, starting transfers between devices, on_device(): got_other = lax.ppermute(edge, GS, other)  6.35 us
    ppermute x1, waiting for transfers between devices, on_device(): cross = lax.ppermute(crossing, GS, up_route)  5.9 us
    all_to_all x1, waiting for transfers between devices, on_device(): own = lax.all_to_all(sent, 'yc', 0, 0, tiled=True)  5.26 us
    pallas_call x1, Pallas kernels, on_device(): call(backward_kernel, [HB] * 8 + [VM] * 7, [((CH, SIDE, SIDE), bf16, VM),...  3.6 us
    pallas_call x1, Pallas kernels, on_device(): call(forward_kernel, [HB] * 6 + [VM] * 2, [((group, 72, 128), bf16, VM),...  3.04 us
  transfers between devices with their start and end apart: 5, of which 4 were waited for; matrix products, arithmetic and copies ran while one was open for 0% of the time, Pallas kernels for 0%

profile of v4, /device:TPU:1, one launch (start us, length us, event | category | flops | bytes accessed | tf_op | source)
XLA Modules:
  0.0 98.1 jit_solution(3670006986582847849)
XLA Ops:
  0.6 1.8 %pack.1 = f32[8,32,128]{2,1,0:T(8,128)} custom-call(s32[3,1,8]{2,1,0:T(1,128)} %bitcast.13, f32[10,96,128]{2,1,0:T(8,128)} %bitcast.11), custom_call_target="tpu_custom_call" | custom-call | tf_op jit(solution)/shard_map/pack/pallas_call | solution.py:558
  2.5 0.0 copy-start.2
  2.5 10.3 %all-to-all-start = ((f32[8,32,128]{2,1,0:T(8,128)}), f32[8,32,128]{2,1,0:T(8,128)S(1)}, u32[]{:S(2)}, u32[]{:S(2)}) async-start(f32[8,32,128]{2,1,0:T(8,128)} %pack.1), calls=%async_computation | async-start | bytes 262144 | tf_op jit(solution)/shard_map/all_to_all | solution.py:566
  12.7 0.0 copy-start.6
  12.7 0.0 copy-start.7
  12.7 5.3 %all-to-all-done.own = f32[8,32,128]{2,1,0:T(8,128)S(1)} async-done(((f32[8,32,128]{2,1,0:T(8,128)}), f32[8,32,128]{2,1,0:T(8,128)S(1)}, u32[]{:S(2)}, u32[]{:S(2)}) %all-to-all-start) | async-done | bytes 131104 | tf_op jit(solution)/shard_map/all_to_all | solution.py:566
  18.0 0.0 copy-start.14
  18.0 0.0 copy-start.8
  18.0 0.0 copy-start.9
  18.0 2.1 %collective-permute-start = (f32[4,32,128]{2,1,0:T(8,128)S(1)}, f32[4,32,128]{2,1,0:T(8,128)S(1)}, u32[]{:S(2)}, u32[]{:S(2)}) collective-permute-start(f32[4,32,128]{2,1,0:T(8,128)S(1)} %slice_select_fusion), channel_id=1, source_target_pairs={{0,8},{1,9},{2,10},{3,11},{5,125},{6,126},{7,127},{8,16},{9,17},{1... | collective-permute-start | bytes 196616 | tf_op jit(solution)/shard_map/ppermute | solution.py:574
  20.1 0.0 copy-start.11
  20.1 0.0 copy-start.12
  20.1 0.0 copy-start.13
  20.1 0.0 copy-done.14
  20.1 0.6 copy-done.11
  20.7 0.0 copy-done.12
  20.8 0.0 copy-done.13
  20.8 0.1 pad_add_fusion.ints_in
  20.9 5.9 %collective-permute-done.cross = f32[4,32,128]{2,1,0:T(8,128)S(1)} collective-permute-done((f32[4,32,128]{2,1,0:T(8,128)S(1)}, f32[4,32,128]{2,1,0:T(8,128)S(1)}, u32[]{:S(2)}, u32[]{:S(2)}) %collective-permute-start) | collective-permute-done | bytes 65568 | tf_op jit(solution)/shard_map/ppermute | solution.py:574
  26.8 0.0 copy-done.2
  26.8 0.0 copy-done.6
  26.8 0.0 copy-done.7
  26.8 0.0 copy-done.8
  26.8 0.0 copy-done.9
  26.8 0.0 copy-start.1
  26.8 0.0 copy-start.4
  26.8 3.0 %forward.1 = (bf16[16,72,128]{2,1,0:T(8,128)(2,1)S(1)}, f32[16,16,128]{2,1,0:T(8,128)S(1)}, bf16[8,256,256]{2,1,0:T(8,128)(2,1)S(1)}, bf16[8,256,256]{2,1,0:T(8,128)(2,1)S(1)}) custom-call(s32[32]{0:T(128)S(1)} %pad_add_fusion.ints_in, bf16[4,32,32]{2,1,0:T(8,128)(2,1)S(1)} %copy-done.8, bf16[256,32]{1,0:T(8,128)(2,1)S(1)} %copy-done.7, ...), custom_call_target="tpu_custom_call" | custom-call | tf_op jit(solution)/shard_map/forward/pallas_call | solution.py:576
  29.9 0.0 copy-start
  29.9 30.7 %all_to_all.15.got = bf16[16,72,128]{2,1,0:T(8,128)(2,1)S(1)} all-to-all(bf16[16,72,128]{2,1,0:T(8,128)(2,1)S(1)} %get-tuple-element.24), channel_id=1, replica_groups=mesh['img'=4,'zq'=4,'zr'=4,'yc'=8] {'img','zq'}, dimensions={0} | all-to-all | bytes 589824 | tf_op jit(solution)/shard_map/all_to_all | solution.py:607
  60.6 0.0 copy-done.1
  60.6 0.0 copy-done.4
  60.6 0.0 copy-start.3
  60.6 0.0 copy-start.5
  60.6 1.0 %error.1 = (f32[4,32,128]{2,1,0:T(8,128)S(1)}, bf16[4,32,128]{2,1,0:T(8,128)(2,1)S(1)}, f32[4,32,128]{2,1,0:T(8,128)S(1)}, bf16[4,32,32]{2,1,0:T(8,128)(2,1)}) custom-call(bf16[16,72,128]{2,1,0:T(8,128)(2,1)S(1)} %all_to_all.15.got, bf16[4,32,384]{2,1,0:T(8,128)(2,1)S(1)} %copy-done.4, bf16[4,128,32]{2,1,0:T(8,128)(2,1)S(1)} %copy-done.1), custom_call_target="tpu_custom_call" | custom-call | tf_op jit(solution)/shard_map/error/pallas_call | solution.py:609
  61.6 0.0 copy-start.10
  61.6 6.3 %collective-permute-start.2 = (bf16[4,32,128]{2,1,0:T(8,128)(2,1)S(1)}, bf16[4,32,128]{2,1,0:T(8,128)(2,1)S(1)}, u32[]{:S(2)}, u32[]{:S(2)}) collective-permute-start(bf16[4,32,128]{2,1,0:T(8,128)(2,1)S(1)} %get-tuple-element.29), channel_id=1, source_target_pairs={{127,0},{1,2},{3,4},{5,6},{7,8},{9,10},{11,12},{13,14},{15,16},{17... | collective-permute-start | bytes 98312 | tf_op jit(solution)/shard_map/ppermute | solution.py:624
  68.0 2.1 %collective-permute-start.1 = (bf16[4,32,128]{2,1,0:T(8,128)(2,1)S(1)}, bf16[4,32,128]{2,1,0:T(8,128)(2,1)S(1)}, u32[]{:S(2)}, u32[]{:S(2)}) collective-permute-start(bf16[4,32,128]{2,1,0:T(8,128)(2,1)S(1)} %get-tuple-element.29), channel_id=1, source_target_pairs={{0,1},{1,0},{2,3},{3,2},{4,5},{5,4},{6,7},{7,6},{8,9},{9,8},{10,11... | collective-permute-start | bytes 98312 | tf_op jit(solution)/shard_map/ppermute | solution.py:625
  70.1 0.0 collective-permute-done.2.got_other
  70.1 1.0 %collective-permute-done.1.got_mate = bf16[4,32,128]{2,1,0:T(8,128)(2,1)S(1)} collective-permute-done((bf16[4,32,128]{2,1,0:T(8,128)(2,1)S(1)}, bf16[4,32,128]{2,1,0:T(8,128)(2,1)S(1)}, u32[]{:S(2)}, u32[]{:S(2)}) %collective-permute-start.1) | collective-permute-done | bytes 32800 | tf_op jit(solution)/shard_map/ppermute | solution.py:625
  71.1 0.0 copy-done
  71.1 0.0 copy-done.3
  71.1 0.0 copy-done.5
  71.1 0.0 copy-done.10
  71.1 3.6 %backward.1 = (bf16[4,32,32]{2,1,0:T(8,128)(2,1)}, bf16[8,32,128]{2,1,0:T(8,128)(2,1)S(1)}, bf16[4,32,128]{2,1,0:T(8,128)(2,1)S(1)}) custom-call(s32[32]{0:T(128)S(1)} %pad_add_fusion.ints_in, bf16[3,768,128]{2,1,0:T(8,128)(2,1)S(1)} %copy-done, bf16[4,128,32]{2,1,0:T(8,128)(2,1)S(1)} %copy-done.1, bf16[128,256]{1,0:T(8,128)(2,1)S(1)} %copy-done.5, ...), custom_call_target="tpu_custom_call" | custom-call | tf_op jit(solution)/shard_map/backward/pallas_call | solution.py:627
  74.7 1.9 %collective-permute-start.3 = (bf16[4,32,128]{2,1,0:T(8,128)(2,1)S(1)}, bf16[4,32,128]{2,1,0:T(8,128)(2,1)S(1)}, u32[]{:S(2)}, u32[]{:S(2)}) collective-permute-start(bf16[4,32,128]{2,1,0:T(8,128)(2,1)S(1)} %get-tuple-element.34), channel_id=1, source_target_pairs={{8,0},{9,1},{10,2},{11,3},{125,5},{126,6},{127,7},{16,8},{17,9},{1... | collective-permute-start | bytes 98312 | tf_op jit(solution)/shard_map/ppermute | solution.py:656
  76.7 3.0 %collective-permute-done.3 = bf16[4,32,128]{2,1,0:T(8,128)(2,1)S(1)} collective-permute-done((bf16[4,32,128]{2,1,0:T(8,128)(2,1)S(1)}, bf16[4,32,128]{2,1,0:T(8,128)(2,1)S(1)}, u32[]{:S(2)}, u32[]{:S(2)}) %collective-permute-start.3) | collective-permute-done | bytes 32800 | tf_op jit(solution)/shard_map/ppermute | solution.py:656
  79.7 0.1 maximum_select_fusion
  79.8 16.8 %all_to_all.16.got = bf16[32,32,128]{2,1,0:T(8,128)(2,1)S(1)} all-to-all(bf16[32,32,128]{2,1,0:T(8,128)(2,1)S(1)} %bitcast.10), channel_id=1, replica_groups=mesh['img'=4,'zq'=4,'zr'=4,'yc'=8] {'img','yc'}, dimensions={0} | all-to-all | bytes 524288 | tf_op jit(solution)/shard_map/all_to_all | solution.py:661
  96.6 1.4 %collect.1 = f32[10,96,128]{2,1,0:T(8,128)} custom-call(bf16[32,32,128]{2,1,0:T(8,128)(2,1)S(1)} %all_to_all.16.got), custom_call_target="tpu_custom_call" | custom-call | tf_op jit(solution)/shard_map/collect/pallas_call | solution.py:662
  (3 shorter events, 0.1 us)
Async XLA Ops:
  2.5 24.3 %copy-start.2 = (bf16[2,256,256]{2,1,0:T(8,128)(2,1)S(1)}, bf16[2,256,256]{2,1,0:T(8,128)(2,1)}, u32[]{:S(2)}) copy-start(bf16[2,256,256]{2,1,0:T(8,128)(2,1)} %constant.33.clone.tri_in) | copy-start | bytes 786436
  2.5 15.5 %all-to-all-start = ((f32[8,32,128]{2,1,0:T(8,128)}), f32[8,32,128]{2,1,0:T(8,128)S(1)}, u32[]{:S(2)}, u32[]{:S(2)}) async-start(f32[8,32,128]{2,1,0:T(8,128)} %pack.1), calls=%async_computation | async-start | bytes 262144 | tf_op jit(solution)/shard_map/all_to_all | solution.py:566
  12.7 14.0 %copy-start.6 = (bf16[256,128]{1,0:T(8,128)(2,1)S(1)}, bf16[256,128]{1,0:T(8,128)(2,1)}, u32[]{:S(2)}) copy-start(bf16[256,128]{1,0:T(8,128)(2,1)} %constant.35.clone.spread_in) | copy-start | bytes 196612
  12.7 14.0 %copy-start.7 = (bf16[256,32]{1,0:T(8,128)(2,1)S(1)}, bf16[256,32]{1,0:T(8,128)(2,1)}, u32[]{:S(2)}) copy-start(bf16[256,32]{1,0:T(8,128)(2,1)} %constant.13.clone.mom_in) | copy-start | bytes 49156
  18.0 2.1 %copy-start.14 = (s32[1,1,8]{2,1,0:T(1,128)S(1)}, s32[1,1,8]{2,1,0:T(1,128)}, u32[]{:S(2)}) copy-start(s32[1,1,8]{2,1,0:T(1,128)} %param.20) | copy-start | bytes 100
  18.0 8.8 %copy-start.8 = (bf16[4,32,32]{2,1,0:T(8,128)(2,1)S(1)}, bf16[4,32,32]{2,1,0:T(8,128)(2,1)}, u32[]{:S(2)}) copy-start(bf16[4,32,32]{2,1,0:T(8,128)(2,1)} %target_in.1) | copy-start | bytes 24580
  18.0 8.8 %copy-start.9 = (bf16[4,32,128]{2,1,0:T(8,128)(2,1)S(1)}, bf16[4,32,128]{2,1,0:T(8,128)(2,1)}, u32[]{:S(2)}) copy-start(bf16[4,32,128]{2,1,0:T(8,128)(2,1)} %constant.37.clone.place_in) | copy-start | bytes 98308
  18.0 8.7 %collective-permute-start = (f32[4,32,128]{2,1,0:T(8,128)S(1)}, f32[4,32,128]{2,1,0:T(8,128)S(1)}, u32[]{:S(2)}, u32[]{:S(2)}) collective-permute-start(f32[4,32,128]{2,1,0:T(8,128)S(1)} %slice_select_fusion), channel_id=1, source_target_pairs={{0,8},{1,9},{2,10},{3,11},{5,125},{6,126},{7,127},{8,16},{9,17},{1... | collective-permute-start | bytes 196616 | tf_op jit(solution)/shard_map/ppermute | solution.py:574
  20.1 0.7 copy-start.11
  20.1 0.7 copy-start.12
  20.1 0.7 copy-start.13
  26.8 33.8 %copy-start.1 = (bf16[4,128,32]{2,1,0:T(8,128)(2,1)S(1)}, bf16[4,128,32]{2,1,0:T(8,128)(2,1)}, u32[]{:S(2)}) copy-start(bf16[4,128,32]{2,1,0:T(8,128)(2,1)} %constant.38.clone.placet.placet_in) | copy-start | bytes 98308
  26.8 33.8 %copy-start.4 = (bf16[4,32,384]{2,1,0:T(8,128)(2,1)S(1)}, bf16[4,32,384]{2,1,0:T(8,128)(2,1)}, u32[]{:S(2)}) copy-start(bf16[4,32,384]{2,1,0:T(8,128)(2,1)} %constant.39.clone.vert) | copy-start | bytes 294916
  29.9 41.2 %copy-start = (bf16[3,768,128]{2,1,0:T(8,128)(2,1)S(1)}, bf16[3,768,128]{2,1,0:T(8,128)(2,1)}, u32[]{:S(2)}) copy-start(bf16[3,768,128]{2,1,0:T(8,128)(2,1)} %constant.40.clone.horiz_in) | copy-start | bytes 1769476
  60.6 10.5 %copy-start.3 = (bf16[2,256,256]{2,1,0:T(8,128)(2,1)S(1)}, bf16[2,256,256]{2,1,0:T(8,128)(2,1)}, u32[]{:S(2)}) copy-start(bf16[2,256,256]{2,1,0:T(8,128)(2,1)} %constant.34.clone.trib_in) | copy-start | bytes 786436
  60.6 10.5 %copy-start.5 = (bf16[128,256]{1,0:T(8,128)(2,1)S(1)}, bf16[128,256]{1,0:T(8,128)(2,1)}, u32[]{:S(2)}) copy-start(bf16[128,256]{1,0:T(8,128)(2,1)} %constant.36.clone.spreadt_in) | copy-start | bytes 196612
  61.6 9.5 %copy-start.10 = (bf16[16,256]{1,0:T(8,128)(2,1)S(1)}, bf16[16,256]{1,0:T(8,128)(2,1)}, u32[]{:S(2)}) copy-start(bf16[16,256]{1,0:T(8,128)(2,1)} %constant.32.clone.momt_in) | copy-start | bytes 24580
  61.6 8.4 %collective-permute-start.2 = (bf16[4,32,128]{2,1,0:T(8,128)(2,1)S(1)}, bf16[4,32,128]{2,1,0:T(8,128)(2,1)S(1)}, u32[]{:S(2)}, u32[]{:S(2)}) collective-permute-start(bf16[4,32,128]{2,1,0:T(8,128)(2,1)S(1)} %get-tuple-element.29), channel_id=1, source_target_pairs={{127,0},{1,2},{3,4},{5,6},{7,8},{9,10},{11,12},{13,14},{15,16},{17... | collective-permute-start | bytes 98312 | tf_op jit(solution)/shard_map/ppermute | solution.py:624
  68.0 3.1 %collective-permute-start.1 = (bf16[4,32,128]{2,1,0:T(8,128)(2,1)S(1)}, bf16[4,32,128]{2,1,0:T(8,128)(2,1)S(1)}, u32[]{:S(2)}, u32[]{:S(2)}) collective-permute-start(bf16[4,32,128]{2,1,0:T(8,128)(2,1)S(1)} %get-tuple-element.29), channel_id=1, source_target_pairs={{0,1},{1,0},{2,3},{3,2},{4,5},{5,4},{6,7},{7,6},{8,9},{9,8},{10,11... | collective-permute-start | bytes 98312 | tf_op jit(solution)/shard_map/ppermute | solution.py:625
  74.7 4.9 %collective-permute-start.3 = (bf16[4,32,128]{2,1,0:T(8,128)(2,1)S(1)}, bf16[4,32,128]{2,1,0:T(8,128)(2,1)S(1)}, u32[]{:S(2)}, u32[]{:S(2)}) collective-permute-start(bf16[4,32,128]{2,1,0:T(8,128)(2,1)S(1)} %get-tuple-element.34), channel_id=1, source_target_pairs={{8,0},{9,1},{10,2},{11,3},{125,5},{126,6},{127,7},{16,8},{17,9},{1... | collective-permute-start | bytes 98312 | tf_op jit(solution)/shard_map/ppermute | solution.py:656

commit v5 on v4

--- a/solution.py
+++ b/solution.py
@@ -180,8 +180,8 @@
         out[chunk, 30:32, :] = jnp.broadcast_to(row.astype(f32), (2, 128))
 
 
-def forward_kernel(ints_in, target_in, mom_in, tri_in, spread_in, place_in, own, cross, payload, raws, pair_o,
-                   beta_o, ints, group_table, slot_table, target, mom, tri, spread, place, blk, vals, coefs, shades, cols, pair_w, beta, in_sems, sems):
+def forward_kernel(ints_in, target_in, mom_in, tri_in, spread_in, place_in, own, cross, payload, raws, pair_w,
+                   beta, ints, group_table, slot_table, target, mom, tri, spread, place, blk, vals, coefs, shades, cols, in_sems):
     loads = fetch(
         [
             (ints_in, ints),
@@ -246,7 +246,9 @@
         alpha = jnp.exp2(dot(mom[...], coefs[pair].astype(bf16)))
         lost = alpha * (log2e + alpha * (log2e / 2 + alpha * (log2e / 3 + alpha * (log2e / 4))))
         beta[pair] = (alpha * jnp.exp2(lost)).astype(bf16)
-        sums = dot(lost.astype(bf16), tri[jnp.where(same, 1, 0)])
+        high, low = halves(lost)
+        earlier = tri[jnp.where(same, 1, 0)]
+        sums = dot(high, earlier) + dot(low, earlier)
         whole = sums[:, 255:256] - lost[:, 255:256]
         return first, second, same, alpha, sums, whole
 
@@ -259,19 +261,14 @@
         if pair:
             carry = jnp.where(slots[first] == slots[first - 1], carry, 0.0)
         later = jnp.where(same, carry, 0.0)
-        weight = (jnp.exp2(sums + jnp.concatenate([carry, later], axis=1)) * alpha).astype(bf16)
+        high, low = halves(jnp.exp2(sums + jnp.concatenate([carry, later], axis=1)) * alpha)
+        pair_w[pair] = high
         carry = whole + later
-        pair_w[pair] = weight
-        colour = dot(shades[pair].astype(bf16), weight, ((1,), (1,)))
+        shade = shades[pair].astype(bf16)
+        colour = dot(shade, high, ((1,), (1,))) + dot(shade, low, ((1,), (1,)))
         colour = colour[0:8, :] + colour[8:16, :]
         cols[slots[first]] += jnp.where(upper, colour, 0.0)
         cols[slots[second]] += jnp.where(upper, 0.0, colour)
-    copies = (
-        pltpu.make_async_copy(pair_w, pair_o, sems.at[0]),
-        pltpu.make_async_copy(beta, beta_o, sems.at[1]),
-    )
-    for copy in copies:
-        copy.start()
     row_of = iota((TILE, PIX), 1) // TILE == iota((TILE, PIX), 0)
     lane = iota((TILE, 128), 1)
     pieces = []
@@ -302,8 +299,6 @@
     for q in range(N_IMG * N_ZQ):
         payload[q, 0:64, :] = body
         payload[q, 64:72, :] = tags
-    for copy in copies:
-        copy.wait()
 
 
 def error_kernel(got, vert, placet, up, edge, err_own, rendered, errs, images):
@@ -338,15 +333,14 @@
 
 
 def backward_kernel(ints_in, horiz_in, placet_in, spreadt_in, momt_in, trib_in,
-                    pair_o, beta_o, up, got_mate, got_other, err_own, raws, own, cross,
+                    up, got_mate, got_other, err_own, raws, pair_w, beta, own, cross,
                     grad_out, msg_own, msg_cross,
-                    ints, group_table, slot_table, horiz, placet, spreadt, momt, trib, pair_w, beta,
+                    ints, group_table, slot_table, horiz, placet, spreadt, momt, trib,
                     ext, back, grads, vals, sums, blk, pack, shades, shade_sums, sems):
     loads = fetch(
         [
             (ints_in, ints),
             (horiz_in, horiz), (placet_in, placet), (spreadt_in, spreadt), (momt_in, momt), (trib_in, trib),
-            (pair_o, pair_w), (beta_o, beta),
         ],
         sems,
     )
@@ -579,8 +573,8 @@
         [
             ((group, 72, 128), bf16, VM),
             ((SLOTS, 16, 128), f32, VM),
-            ((PAIRS, PIX, 256), bf16, HB),
-            ((PAIRS, PIX, 256), bf16, HB),
+            ((PAIRS, PIX, 256), bf16, VM),
+            ((PAIRS, PIX, 256), bf16, VM),
         ],
         small
         + [
@@ -594,10 +588,7 @@
             vm((PAIRS, 32, 256), f32),
             vm((PAIRS, 16, 256), f32),
             vm((TILES, 8, PIX), f32),
-            vm((PAIRS, PIX, 256), bf16),
-            vm((PAIRS, PIX, 256), bf16),
             dma((6,)),
-            dma((2,)),
         ],
         "forward",
     )(
@@ -626,7 +617,7 @@
 
     pixel_grad, msg_own, msg_cross = call(
         backward_kernel,
-        [HB] * 8 + [VM] * 7,
+        [HB] * 6 + [VM] * 9,
         [((CH, SIDE, SIDE), bf16, VM), ((N_YC, MSG, 128), bf16, VM), ((4, MSG, 128), bf16, VM)],
         small
         + [
@@ -635,8 +626,6 @@
             vm((128, PIX), bf16),
             vm((16, PIX), bf16),
             vm((2, 256, 256), bf16),
-            vm((PAIRS, PIX, 256), bf16),
-            vm((PAIRS, PIX, 256), bf16),
             vm((128, 256), f32),
             vm((128, 128), f32),
             vm((N_ZQ, SIDE, 128), f32),
@@ -646,12 +635,12 @@
             vm((12, MSG, 128), f32),
             vm((PAIRS, 32, 256), f32),
             vm((PAIRS, TILES, 8, 256), f32),
-            dma((8,)),
+            dma((6,)),
         ],
         "backward",
     )(
         ints, table["horiz"], table["placet"], table["spreadt"], table["momt"],
-        table["trib"], pair_w, beta, up, got_mate, got_other, err_own, raws, own, cross,
+        table["trib"], up, got_mate, got_other, err_own, raws, pair_w, beta, own, cross,
     )
     returned = lax.ppermute(msg_cross, GS, back_route)
     apart = jnp.arange(N_YC) + NEAR // 2 - yc

time: 98.6 us -> 98.9 us (level)
  no operation moved by 1% of the time
where the time goes in v5:
time: 98.9 us; the launch traced here: 98.4 us
  blocking collectives  47.6 us (48%)
  starting transfers between devices  22.6 us (23%)
  waiting for transfers between devices  15.2 us (15%)
  Pallas kernels  11.3 us (11%)
    all_to_all x1, blocking collectives, on_device(): got = lax.all_to_all(payload, ('img', 'zq'), 0, 0, tiled=True)  30.8 us
    all_to_all x1, blocking collectives, on_device(): all_msgs = lax.all_to_all(spread_out, ('img', 'yc'), 0, 0, tiled=True)  16.8 us
    all_to_all x1, starting transfers between devices, on_device(): own = lax.all_to_all(sent, 'yc', 0, 0, tiled=True)  10.3 us
    ppermute x1, starting transfers between devices, on_device(): got_other = lax.ppermute(edge, GS, other)  6.34 us
    ppermute x1, waiting for transfers between devices, on_device(): cross = lax.ppermute(crossing, GS, up_route)  5.9 us
    all_to_all x1, waiting for transfers between devices, on_device(): own = lax.all_to_all(sent, 'yc', 0, 0, tiled=True)  5.26 us
    pallas_call x1, Pallas kernels, on_device(): call(backward_kernel, [HB] * 6 + [VM] * 9, [((CH, SIDE, SIDE), bf16, VM),...  3.55 us
    pallas_call x1, Pallas kernels, on_device(): call(forward_kernel, [HB] * 6 + [VM] * 2, [((group, 72, 128), bf16, VM),...  3.45 us
  transfers between devices with their start and end apart: 5, of which 4 were waited for; matrix products, arithmetic and copies ran while one was open for 0% of the time, Pallas kernels for 0%

profile of v5, /device:TPU:1, one launch (start us, length us, event | category | flops | bytes accessed | tf_op | source)
XLA Modules:
  0.0 98.4 jit_solution(12267743998101691378)
XLA Ops:
  0.6 1.8 %pack.1 = f32[8,32,128]{2,1,0:T(8,128)} custom-call(s32[3,1,8]{2,1,0:T(1,128)} %bitcast.13, f32[10,96,128]{2,1,0:T(8,128)} %bitcast.11), custom_call_target="tpu_custom_call" | custom-call | tf_op jit(solution)/shard_map/pack/pallas_call | solution.py:552
  2.5 0.0 copy-start.2
  2.5 10.3 %all-to-all-start = ((f32[8,32,128]{2,1,0:T(8,128)}), f32[8,32,128]{2,1,0:T(8,128)S(1)}, u32[]{:S(2)}, u32[]{:S(2)}) async-start(f32[8,32,128]{2,1,0:T(8,128)} %pack.1), calls=%async_computation | async-start | bytes 262144 | tf_op jit(solution)/shard_map/all_to_all | solution.py:560
  12.7 0.0 copy-start.6
  12.7 0.0 copy-start.7
  12.7 5.3 %all-to-all-done.own = f32[8,32,128]{2,1,0:T(8,128)S(1)} async-done(((f32[8,32,128]{2,1,0:T(8,128)}), f32[8,32,128]{2,1,0:T(8,128)S(1)}, u32[]{:S(2)}, u32[]{:S(2)}) %all-to-all-start) | async-done | bytes 131104 | tf_op jit(solution)/shard_map/all_to_all | solution.py:560
  18.0 0.0 copy-start.14
  18.0 0.0 copy-start.8
  18.0 0.0 copy-start.9
  18.0 2.1 %collective-permute-start = (f32[4,32,128]{2,1,0:T(8,128)S(1)}, f32[4,32,128]{2,1,0:T(8,128)S(1)}, u32[]{:S(2)}, u32[]{:S(2)}) collective-permute-start(f32[4,32,128]{2,1,0:T(8,128)S(1)} %slice_select_fusion), channel_id=1, source_target_pairs={{0,8},{1,9},{2,10},{3,11},{5,125},{6,126},{7,127},{8,16},{9,17},{1... | collective-permute-start | bytes 196616 | tf_op jit(solution)/shard_map/ppermute | solution.py:568
  20.1 0.0 copy-start.11
  20.1 0.0 copy-start.12
  20.1 0.0 copy-start.13
  20.1 0.0 copy-done.14
  20.1 0.6 copy-done.11
  20.7 0.0 copy-done.12
  20.8 0.0 copy-done.13
  20.8 0.1 pad_add_fusion.ints_in
  20.9 5.9 %collective-permute-done.cross = f32[4,32,128]{2,1,0:T(8,128)S(1)} collective-permute-done((f32[4,32,128]{2,1,0:T(8,128)S(1)}, f32[4,32,128]{2,1,0:T(8,128)S(1)}, u32[]{:S(2)}, u32[]{:S(2)}) %collective-permute-start) | collective-permute-done | bytes 65568 | tf_op jit(solution)/shard_map/ppermute | solution.py:568
  26.8 0.0 copy-done.2
  26.8 0.0 copy-done.6
  26.8 0.0 copy-done.7
  26.8 0.0 copy-done.8
  26.8 0.0 copy-done.9
  26.8 0.0 copy-start.1
  26.8 0.0 copy-start.4
  26.8 3.5 %forward.1 = (bf16[16,72,128]{2,1,0:T(8,128)(2,1)S(1)}, f32[16,16,128]{2,1,0:T(8,128)S(1)}, bf16[8,256,256]{2,1,0:T(8,128)(2,1)S(1)}, bf16[8,256,256]{2,1,0:T(8,128)(2,1)S(1)}) custom-call(s32[32]{0:T(128)S(1)} %pad_add_fusion.ints_in, bf16[4,32,32]{2,1,0:T(8,128)(2,1)S(1)} %copy-done.8, bf16[256,32]{1,0:T(8,128)(2,1)S(1)} %copy-done.7, ...), custom_call_target="tpu_custom_call" | custom-call | tf_op jit(solution)/shard_map/forward/pallas_call | solution.py:570
  30.3 0.0 copy-start
  30.3 30.8 %all_to_all.15.got = bf16[16,72,128]{2,1,0:T(8,128)(2,1)S(1)} all-to-all(bf16[16,72,128]{2,1,0:T(8,128)(2,1)S(1)} %get-tuple-element.24), channel_id=1, replica_groups=mesh['img'=4,'zq'=4,'zr'=4,'yc'=8] {'img','zq'}, dimensions={0} | all-to-all | bytes 589824 | tf_op jit(solution)/shard_map/all_to_all | solution.py:598
  61.0 0.0 copy-done.1
  61.0 0.0 copy-done.4
  61.0 0.0 copy-start.3
  61.0 0.0 copy-start.5
  61.0 1.0 %error.1 = (f32[4,32,128]{2,1,0:T(8,128)S(1)}, bf16[4,32,128]{2,1,0:T(8,128)(2,1)S(1)}, f32[4,32,128]{2,1,0:T(8,128)S(1)}, bf16[4,32,32]{2,1,0:T(8,128)(2,1)}) custom-call(bf16[16,72,128]{2,1,0:T(8,128)(2,1)S(1)} %all_to_all.15.got, bf16[4,32,384]{2,1,0:T(8,128)(2,1)S(1)} %copy-done.4, bf16[4,128,32]{2,1,0:T(8,128)(2,1)S(1)} %copy-done.1), custom_call_target="tpu_custom_call" | custom-call | tf_op jit(solution)/shard_map/error/pallas_call | solution.py:600
  62.1 0.0 copy-start.10
  62.1 6.3 %collective-permute-start.2 = (bf16[4,32,128]{2,1,0:T(8,128)(2,1)S(1)}, bf16[4,32,128]{2,1,0:T(8,128)(2,1)S(1)}, u32[]{:S(2)}, u32[]{:S(2)}) collective-permute-start(bf16[4,32,128]{2,1,0:T(8,128)(2,1)S(1)} %get-tuple-element.27), channel_id=1, source_target_pairs={{127,0},{1,2},{3,4},{5,6},{7,8},{9,10},{11,12},{13,14},{15,16},{17... | collective-permute-start | bytes 98312 | tf_op jit(solution)/shard_map/ppermute | solution.py:615
  68.4 2.1 %collective-permute-start.1 = (bf16[4,32,128]{2,1,0:T(8,128)(2,1)S(1)}, bf16[4,32,128]{2,1,0:T(8,128)(2,1)S(1)}, u32[]{:S(2)}, u32[]{:S(2)}) collective-permute-start(bf16[4,32,128]{2,1,0:T(8,128)(2,1)S(1)} %get-tuple-element.27), channel_id=1, source_target_pairs={{0,1},{1,0},{2,3},{3,2},{4,5},{5,4},{6,7},{7,6},{8,9},{9,8},{10,11... | collective-permute-start | bytes 98312 | tf_op jit(solution)/shard_map/ppermute | solution.py:616
  70.5 0.0 collective-permute-done.2.got_other
  70.5 1.0 %collective-permute-done.1.got_mate = bf16[4,32,128]{2,1,0:T(8,128)(2,1)S(1)} collective-permute-done((bf16[4,32,128]{2,1,0:T(8,128)(2,1)S(1)}, bf16[4,32,128]{2,1,0:T(8,128)(2,1)S(1)}, u32[]{:S(2)}, u32[]{:S(2)}) %collective-permute-start.1) | collective-permute-done | bytes 32800 | tf_op jit(solution)/shard_map/ppermute | solution.py:616
  71.5 0.0 copy-done
  71.5 0.0 copy-done.3
  71.5 0.0 copy-done.5
  71.5 0.0 copy-done.10
  71.5 3.5 %backward.1 = (bf16[4,32,32]{2,1,0:T(8,128)(2,1)}, bf16[8,32,128]{2,1,0:T(8,128)(2,1)S(1)}, bf16[4,32,128]{2,1,0:T(8,128)(2,1)S(1)}) custom-call(s32[32]{0:T(128)S(1)} %pad_add_fusion.ints_in, bf16[3,768,128]{2,1,0:T(8,128)(2,1)S(1)} %copy-done, bf16[4,128,32]{2,1,0:T(8,128)(2,1)S(1)} %copy-done.1, bf16[128,256]{1,0:T(8,128)(2,1)S(1)} %copy-done.5, ...), custom_call_target="tpu_custom_call" | custom-call | tf_op jit(solution)/shard_map/backward/pallas_call | solution.py:618
  75.1 1.9 %collective-permute-start.3 = (bf16[4,32,128]{2,1,0:T(8,128)(2,1)S(1)}, bf16[4,32,128]{2,1,0:T(8,128)(2,1)S(1)}, u32[]{:S(2)}, u32[]{:S(2)}) collective-permute-start(bf16[4,32,128]{2,1,0:T(8,128)(2,1)S(1)} %get-tuple-element.34), channel_id=1, source_target_pairs={{8,0},{9,1},{10,2},{11,3},{125,5},{126,6},{127,7},{16,8},{17,9},{1... | collective-permute-start | bytes 98312 | tf_op jit(solution)/shard_map/ppermute | solution.py:645
  77.0 3.0 %collective-permute-done.3 = bf16[4,32,128]{2,1,0:T(8,128)(2,1)S(1)} collective-permute-done((bf16[4,32,128]{2,1,0:T(8,128)(2,1)S(1)}, bf16[4,32,128]{2,1,0:T(8,128)(2,1)S(1)}, u32[]{:S(2)}, u32[]{:S(2)}) %collective-permute-start.3) | collective-permute-done | bytes 32800 | tf_op jit(solution)/shard_map/ppermute | solution.py:645
  80.0 0.1 maximum_select_fusion
  80.1 16.8 %all_to_all.16.got = bf16[32,32,128]{2,1,0:T(8,128)(2,1)S(1)} all-to-all(bf16[32,32,128]{2,1,0:T(8,128)(2,1)S(1)} %bitcast.10), channel_id=1, replica_groups=mesh['img'=4,'zq'=4,'zr'=4,'yc'=8] {'img','yc'}, dimensions={0} | all-to-all | bytes 524288 | tf_op jit(solution)/shard_map/all_to_all | solution.py:650
  97.0 1.4 %collect.1 = f32[10,96,128]{2,1,0:T(8,128)} custom-call(bf16[32,32,128]{2,1,0:T(8,128)(2,1)S(1)} %all_to_all.16.got), custom_call_target="tpu_custom_call" | custom-call | tf_op jit(solution)/shard_map/collect/pallas_call | solution.py:651
  (3 shorter events, 0.1 us)
Async XLA Ops:
  2.5 24.3 %copy-start.2 = (bf16[2,256,256]{2,1,0:T(8,128)(2,1)S(1)}, bf16[2,256,256]{2,1,0:T(8,128)(2,1)}, u32[]{:S(2)}) copy-start(bf16[2,256,256]{2,1,0:T(8,128)(2,1)} %constant.33.clone.tri_in) | copy-start | bytes 786436
  2.5 15.5 %all-to-all-start = ((f32[8,32,128]{2,1,0:T(8,128)}), f32[8,32,128]{2,1,0:T(8,128)S(1)}, u32[]{:S(2)}, u32[]{:S(2)}) async-start(f32[8,32,128]{2,1,0:T(8,128)} %pack.1), calls=%async_computation | async-start | bytes 262144 | tf_op jit(solution)/shard_map/all_to_all | solution.py:560
  12.7 14.0 %copy-start.6 = (bf16[256,128]{1,0:T(8,128)(2,1)S(1)}, bf16[256,128]{1,0:T(8,128)(2,1)}, u32[]{:S(2)}) copy-start(bf16[256,128]{1,0:T(8,128)(2,1)} %constant.35.clone.spread_in) | copy-start | bytes 196612
  12.7 14.0 %copy-start.7 = (bf16[256,32]{1,0:T(8,128)(2,1)S(1)}, bf16[256,32]{1,0:T(8,128)(2,1)}, u32[]{:S(2)}) copy-start(bf16[256,32]{1,0:T(8,128)(2,1)} %constant.13.clone.mom_in) | copy-start | bytes 49156
  18.0 2.1 %copy-start.14 = (s32[1,1,8]{2,1,0:T(1,128)S(1)}, s32[1,1,8]{2,1,0:T(1,128)}, u32[]{:S(2)}) copy-start(s32[1,1,8]{2,1,0:T(1,128)} %param.20) | copy-start | bytes 100
  18.0 8.8 %copy-start.8 = (bf16[4,32,32]{2,1,0:T(8,128)(2,1)S(1)}, bf16[4,32,32]{2,1,0:T(8,128)(2,1)}, u32[]{:S(2)}) copy-start(bf16[4,32,32]{2,1,0:T(8,128)(2,1)} %target_in.1) | copy-start | bytes 24580
  18.0 8.8 %copy-start.9 = (bf16[4,32,128]{2,1,0:T(8,128)(2,1)S(1)}, bf16[4,32,128]{2,1,0:T(8,128)(2,1)}, u32[]{:S(2)}) copy-start(bf16[4,32,128]{2,1,0:T(8,128)(2,1)} %constant.37.clone.place_in) | copy-start | bytes 98308
  18.0 8.7 %collective-permute-start = (f32[4,32,128]{2,1,0:T(8,128)S(1)}, f32[4,32,128]{2,1,0:T(8,128)S(1)}, u32[]{:S(2)}, u32[]{:S(2)}) collective-permute-start(f32[4,32,128]{2,1,0:T(8,128)S(1)} %slice_select_fusion), channel_id=1, source_target_pairs={{0,8},{1,9},{2,10},{3,11},{5,125},{6,126},{7,127},{8,16},{9,17},{1... | collective-permute-start | bytes 196616 | tf_op jit(solution)/shard_map/ppermute | solution.py:568
  20.1 0.7 copy-start.11
  20.1 0.7 copy-start.12
  20.1 0.7 copy-start.13
  26.8 34.3 %copy-start.1 = (bf16[4,128,32]{2,1,0:T(8,128)(2,1)S(1)}, bf16[4,128,32]{2,1,0:T(8,128)(2,1)}, u32[]{:S(2)}) copy-start(bf16[4,128,32]{2,1,0:T(8,128)(2,1)} %constant.38.clone.placet.placet_in) | copy-start | bytes 98308
  26.8 34.2 %copy-start.4 = (bf16[4,32,384]{2,1,0:T(8,128)(2,1)S(1)}, bf16[4,32,384]{2,1,0:T(8,128)(2,1)}, u32[]{:S(2)}) copy-start(bf16[4,32,384]{2,1,0:T(8,128)(2,1)} %constant.39.clone.vert) | copy-start | bytes 294916
  30.3 41.2 %copy-start = (bf16[3,768,128]{2,1,0:T(8,128)(2,1)S(1)}, bf16[3,768,128]{2,1,0:T(8,128)(2,1)}, u32[]{:S(2)}) copy-start(bf16[3,768,128]{2,1,0:T(8,128)(2,1)} %constant.40.clone.horiz_in) | copy-start | bytes 1769476
  61.0 10.5 %copy-start.3 = (bf16[2,256,256]{2,1,0:T(8,128)(2,1)S(1)}, bf16[2,256,256]{2,1,0:T(8,128)(2,1)}, u32[]{:S(2)}) copy-start(bf16[2,256,256]{2,1,0:T(8,128)(2,1)} %constant.34.clone.trib_in) | copy-start | bytes 786436
  61.0 10.5 %copy-start.5 = (bf16[128,256]{1,0:T(8,128)(2,1)S(1)}, bf16[128,256]{1,0:T(8,128)(2,1)}, u32[]{:S(2)}) copy-start(bf16[128,256]{1,0:T(8,128)(2,1)} %constant.36.clone.spreadt_in) | copy-start | bytes 196612
  62.1 9.5 %copy-start.10 = (bf16[16,256]{1,0:T(8,128)(2,1)S(1)}, bf16[16,256]{1,0:T(8,128)(2,1)}, u32[]{:S(2)}) copy-start(bf16[16,256]{1,0:T(8,128)(2,1)} %constant.32.clone.momt_in) | copy-start | bytes 24580
  62.1 8.4 %collective-permute-start.2 = (bf16[4,32,128]{2,1,0:T(8,128)(2,1)S(1)}, bf16[4,32,128]{2,1,0:T(8,128)(2,1)S(1)}, u32[]{:S(2)}, u32[]{:S(2)}) collective-permute-start(bf16[4,32,128]{2,1,0:T(8,128)(2,1)S(1)} %get-tuple-element.27), channel_id=1, source_target_pairs={{127,0},{1,2},{3,4},{5,6},{7,8},{9,10},{11,12},{13,14},{15,16},{17... | collective-permute-start | bytes 98312 | tf_op jit(solution)/shard_map/ppermute | solution.py:615
  68.4 3.1 %collective-permute-start.1 = (bf16[4,32,128]{2,1,0:T(8,128)(2,1)S(1)}, bf16[4,32,128]{2,1,0:T(8,128)(2,1)S(1)}, u32[]{:S(2)}, u32[]{:S(2)}) collective-permute-start(bf16[4,32,128]{2,1,0:T(8,128)(2,1)S(1)} %get-tuple-element.27), channel_id=1, source_target_pairs={{0,1},{1,0},{2,3},{3,2},{4,5},{5,4},{6,7},{7,6},{8,9},{9,8},{10,11... | collective-permute-start | bytes 98312 | tf_op jit(solution)/shard_map/ppermute | solution.py:616
  75.1 4.9 %collective-permute-start.3 = (bf16[4,32,128]{2,1,0:T(8,128)(2,1)S(1)}, bf16[4,32,128]{2,1,0:T(8,128)(2,1)S(1)}, u32[]{:S(2)}, u32[]{:S(2)}) collective-permute-start(bf16[4,32,128]{2,1,0:T(8,128)(2,1)S(1)} %get-tuple-element.34), channel_id=1, source_target_pairs={{8,0},{9,1},{10,2},{11,3},{125,5},{126,6},{127,7},{16,8},{17,9},{1... | collective-permute-start | bytes 98312 | tf_op jit(solution)/shard_map/ppermute | solution.py:645
